TPU v7x, 512 devices: a whole 4x8x8 slice. The times are simulated.
512 devices in a mesh: seq: 128 (over x_hi, z, y), ch: 4 (over x_lo, core).
Axes of the slice: x: 4 (x_hi: 2, x_lo: 2; x = x_hi * 2 + x_lo), y: 8, z: 8, core: 2. Of those that a mesh axis runs over, the one named last changes fastest.
Arguments:
- values: bfloat16 [1048576, 512], P('seq', 'ch'), may hold values from -6 to 6
- factor_low: bfloat16 [64, 64], replicated, may hold values from -0.75 to 0.75
- twist_low: float32 [128, 64], replicated, may hold values from 0.25 to 1.75
- factor_mid: bfloat16 [128, 128], replicated, may hold values from -0.5 to 0.5
- twist_top: float32 [128, 128], replicated, may hold values from 0.25 to 1.75
- factor_top: bfloat16 [128, 128], replicated, may hold values from -0.5 to 0.5
- kernel_top: float32 [128, 512], P(None, 'ch'), may hold values from 0.3 to 3
- kernel_low: bfloat16 [8192, 512], P('seq', 'ch'), may hold values from -6 to 6
- inverse_top: bfloat16 [128, 128], replicated, may hold values from -0.5 to 0.5
- untwist_top: float32 [128, 128], replicated, may hold values from 0.25 to 1.75
- inverse_mid: bfloat16 [128, 128], replicated, may hold values from -0.5 to 0.5
- untwist_low: float32 [128, 64], replicated, may hold values from 0.25 to 1.75
- inverse_low: bfloat16 [64, 64], replicated, may hold values from -0.75 to 0.75
- out_weight: bfloat16 [512, 512], P('ch'), may hold values from -0.25 to 0.25
Outputs:
- layer_out: bfloat16 [1048576, 512], P(('seq', 'ch'))
All inputs are finite; a program needn't handle non-finite values.
Results may differ from a plain program's by a relative error of at most 0.023.
Values may be sent and summed in bfloat16 or wider, within the bound.
No kernel may reach another device: no remote copies, remote signals or barrier semaphores. Data moves between devices by JAX's collectives and lax.ppermute only.
A program may use at most 64 MiB of HBM per device.

v0:
```python
import jax
import jax.numpy as jnp
from jax import lax
from jax.sharding import PartitionSpec as P


def add_rows(whole, piece):
    return jnp.dot(whole, piece, preferred_element_type=jnp.float32)


def local(
    values,
    factor_low,
    twist_low,
    factor_mid,
    twist_top,
    factor_top,
    kernel_top,
    kernel_low,
    inverse_top,
    untwist_top,
    inverse_mid,
    untwist_low,
    inverse_low,
    out_weight,
):
    seq_count = lax.axis_size("seq")
    seq_place = lax.axis_index("seq")
    top_all = factor_top.shape[0]
    mid_all = factor_mid.shape[0]
    low_all = factor_low.shape[0]
    width = values.shape[1]
    top_part = top_all // seq_count
    mid_part = mid_all // seq_count
    field = values.reshape(top_part, mid_all, low_all, width)
    first = jnp.einsum("kc,abcd->abkd", factor_low, field, preferred_element_type=jnp.float32)
    first = (twist_low[None, :, :, None] * first).astype(jnp.bfloat16)
    second = jnp.einsum("jb,abkd->ajkd", factor_mid, first, preferred_element_type=jnp.float32)
    top_scale = lax.dynamic_slice_in_dim(twist_top, seq_place * top_part, top_part, 0)
    second = (top_scale[:, :, None, None] * second).astype(jnp.bfloat16)
    columns = lax.all_to_all(second, "seq", split_axis=1, concat_axis=0, tiled=True)
    spectrum = jnp.dot(factor_top, columns.reshape(top_all, -1), preferred_element_type=jnp.float32)
    spectrum = spectrum.astype(jnp.bfloat16).reshape(top_all, mid_part, low_all, width)
    profile = kernel_low.reshape(mid_part, low_all, width)
    product = (
        spectrum.astype(jnp.float32)
        * kernel_top[:, None, None, :]
        * profile[None].astype(jnp.float32)
    )
    filtered = product.astype(jnp.bfloat16)
    back = jnp.dot(inverse_top, filtered.reshape(top_all, -1), preferred_element_type=jnp.float32)
    back = back.reshape(top_all, mid_part, low_all, width)
    mid_scale = lax.dynamic_slice_in_dim(untwist_top, seq_place * mid_part, mid_part, 1)
    back = (mid_scale[:, :, None, None] * back).astype(jnp.bfloat16)
    restored = lax.all_to_all(back, "seq", split_axis=0, concat_axis=1, tiled=True)
    third = jnp.einsum("bj,ajkd->abkd", inverse_mid, restored, preferred_element_type=jnp.float32)
    third = (untwist_low[None, :, :, None] * third).astype(jnp.bfloat16)
    mixed = jnp.einsum("ck,abkd->abcd", inverse_low, third, preferred_element_type=jnp.float32)
    gated = (mixed * jax.nn.silu(field.astype(jnp.float32))).astype(jnp.bfloat16).reshape(-1, width)
    whole = lax.all_to_all(gated, "ch", split_axis=0, concat_axis=1, tiled=True)
    total = add_rows(whole, lax.all_gather(out_weight, "ch", axis=0, tiled=True))
    return total.astype(jnp.bfloat16)


def solution(mesh):
    return jax.shard_map(
        local,
        mesh=mesh,
        in_specs=(
            P("seq", "ch"),
            P(),
            P(),
            P(),
            P(),
            P(),
            P(None, "ch"),
            P("seq", "ch"),
            P(),
            P(),
            P(),
            P(),
            P(),
            P("ch", None),
        ),
        out_specs=P(("seq", "ch"), None),
        check_vma=False,
    )
```

profile of v0, /device:TPU:1, one launch (start us, length us, event | category | flops | bytes accessed | tf_op | source)
XLA Modules:
  0.0 215.9 jit_solution(3054751934637489545)
XLA Ops:
  0.0 0.0 copy-start
  0.0 0.9 copy.24
  0.9 0.0 copy-done
  0.9 0.0 copy-start.4
  0.9 2.5 %fusion.17 = bf16[128,64,128]{2,1,0:T(8,128)(2,1)S(1)} fusion(bf16[128,64,128]{2,1,0:T(8,128)(2,1)} %bitcast.94, f32[128,64]{1,0:T(8,128)S(1)} %copy.24, bf16[64,64]{1,0:T(8,128)(2,1)} %param.15), kind=kOutput, calls=%fused_computation.25 | convolution fusion | flops 136314880 | bytes 4235264 | tf_op jit(solution)/shard_map/kc,abcd->abkd/dot_general | solution.py:36
  3.5 0.0 copy-done.4
  3.5 2.5 %fusion.18 = bf16[1,128,64,128]{1,3,2,0:T(8,128)(2,1)S(1)} fusion(bf16[128,64,128]{2,1,0:T(8,128)(2,1)S(1)} %fusion.17, f32[128]{0:T(128)S(1)} %dynamic-slice_bitcast_fusion, bf16[128,128]{1,0:T(8,128)(2,1)S(1)} %copy-done.4), kind=kOutput, calls=%fused_computation.26 | convolution fusion | flops 270532608 | bytes 4227584 | tf_op jit(solution)/shard_map/jb,abkd->ajkd/dot_general | solution.py:38
  6.0 2.8 %copy.26 = bf16[1,128,64,128]{3,2,0,1:T(8,128)(2,1)} copy(bf16[1,128,64,128]{1,3,2,0:T(8,128)(2,1)S(1)} %fusion.18) | data formatting | bytes 4194304 | tf_op jit(solution)/shard_map/convert_element_type | solution.py:40
  8.7 0.0 copy-start.2
  8.7 0.0 copy-start.3
  8.7 0.0 copy-start.9
  8.7 20.9 %all-to-all-start = ((bf16[1,128,64,128]{3,2,0,1:T(8,128)(2,1)}), bf16[1,128,64,128]{3,2,0,1:T(8,128)(2,1)S(1)}, u32[]{:S(2)}, u32[]{:S(2)}) async-start(bf16[1,128,64,128]{3,2,0,1:T(8,128)(2,1)} %copy.26), calls=%async_computation | async-start | bytes 4194304 | tf_op jit(solution)/shard_map/all_to_all | solution.py:41
  29.7 0.0 copy-done.2
  29.7 0.1 copy.27
  29.8 0.0 copy-done.3
  29.8 0.2 dynamic-slice_reduce_fusion
  30.0 0.0 copy-done.9
  30.0 53.0 %all-to-all-done = bf16[1,128,64,128]{3,2,0,1:T(8,128)(2,1)S(1)} async-done(((bf16[1,128,64,128]{3,2,0,1:T(8,128)(2,1)}), bf16[1,128,64,128]{3,2,0,1:T(8,128)(2,1)S(1)}, u32[]{:S(2)}, u32[]{:S(2)}) %all-to-all-start) | async-done | bytes 2097184 | tf_op jit(solution)/shard_map/all_to_all | solution.py:41
  83.0 0.0 copy-start.5
  83.0 0.0 copy-start.6
  83.0 2.5 %mul.97 = f32[128,64,128]{0,2,1:T(8,128)} broadcast(f32[128,128]{0,1:T(8,128)S(1)} %copy.27), dimensions={0,2} | broadcast | bytes 4259840 | tf_op jit(solution)/shard_map/mul | solution.py:46
  85.5 0.0 copy-done.5
  85.5 0.0 copy-done.6
  85.5 8.7 %fusion.25 = f32[8192,128]{1,0:T(8,128)} fusion(bf16[128,128]{1,0:T(8,128)(2,1)S(1)} %copy-done.5, f32[128,8192]{0,1:T(8,128)} %bitcast.91, bf16[128,128]{1,0:T(8,128)(2,1)S(1)} %copy-done.6, bf16[16,8,64,128]{3,2,1,0:T(8,128)(2,1)S(1)} %bitcast.93, f32[8192]{0:T(1024)S(1)} %bitcast_convert_fusion), kind=kOutput, calls=%fused_computation.28 | convolution fusion | flops 542113792 | bytes 10584064 | tf_op jit(solution)/shard_map/dot_general | solution.py:51
  94.2 5.4 %copy.28 = f32[128,1,64,128]{3,2,1,0:T(8,128)} copy(f32[128,1,64,128]{0,3,2,1:T(8,128)} %bitcast.92) | data formatting | bytes 8388608 | tf_op jit(solution)/shard_map/reshape | solution.py:52
  99.6 2.6 %multiply_convert_fusion = bf16[128,1,64,128]{3,2,1,0:T(8,128)(2,1)S(1)} fusion(f32[128,1,64,128]{3,2,1,0:T(8,128)} %copy.28, f32[128]{0:T(128)S(1)} %dynamic-slice_reduce_fusion), kind=kLoop, calls=%fused_computation.18 | loop fusion | flops 2097152 | bytes 6291968 | tf_op jit(solution)/shard_map/convert_element_type | solution.py:54
  102.2 60.8 %all_to_all.37 = bf16[128,1,64,128]{3,2,1,0:T(8,128)(2,1)S(1)} all-to-all(bf16[128,1,64,128]{3,2,1,0:T(8,128)(2,1)S(1)} %multiply_convert_fusion), channel_id=1, replica_groups=mesh['seq'=128,'ch'=4] {'seq'}, dimensions={0} | all-to-all | bytes 4194304 | tf_op jit(solution)/shard_map/all_to_all | solution.py:55
  163.0 0.0 copy-start.7
  163.0 0.0 copy-start.8
  163.0 2.9 %copy.29 = bf16[128,1,64,128]{0,3,2,1:T(8,128)(2,1)} copy(bf16[128,1,64,128]{3,2,1,0:T(8,128)(2,1)S(1)} %all_to_all.37) | data formatting | bytes 4194304 | tf_op jit(solution)/shard_map/all_to_all | solution.py:55
  165.9 0.0 copy-done.7
  165.9 0.0 copy-done.8
  165.9 2.3 %fusion.21 = bf16[128,64,128]{0,2,1:T(8,128)(2,1)S(1)} fusion(bf16[128,1,64,128]{0,3,2,1:T(8,128)(2,1)} %copy.29, f32[128,64]{0,1:T(8,128)S(1)} %copy-done.7, bf16[128,128]{1,0:T(8,128)(2,1)S(1)} %copy-done.8), kind=kOutput, calls=%fused_computation.27 | convolution fusion | flops 270532608 | bytes 4259840 | tf_op jit(solution)/shard_map/bj,ajkd->abkd/dot_general | solution.py:56
  168.2 0.0 copy-start.10
  168.2 2.8 %copy.30 = bf16[128,64,128]{2,1,0:T(8,128)(2,1)} copy(bf16[128,64,128]{0,2,1:T(8,128)(2,1)S(1)} %fusion.21) | data formatting | bytes 4194304 | tf_op jit(solution)/shard_map/reshape.23
  171.0 0.0 copy-done.10
  171.0 3.8 %fusion.12 = bf16[1,128,64,128]{3,2,1,0:T(8,128)(2,1)S(1)} fusion(bf16[1,128,64,128]{3,2,1,0:T(8,128)(2,1)} %bitcast.95, bf16[128,64,128]{2,1,0:T(8,128)(2,1)} %copy.30, bf16[64,64]{1,0:T(8,128)(2,1)S(1)} %copy-done.10), kind=kOutput, calls=%fused_computation.19 | convolution fusion | flops 141557760 | bytes 6299648 | tf_op jit(solution)/shard_map/ck,abkd->abcd/dot_general | solution.py:58
  174.7 2.6 %copy.31 = bf16[4,2048,128]{1,2,0:T(8,128)(2,1)} copy(bf16[4,2048,128]{2,1,0:T(8,128)(2,1)S(1)} %bitcast.97) | data formatting | bytes 4194304 | tf_op jit(solution)/shard_map/all_to_all | solution.py:60
  177.3 0.0 copy-start.1
  177.3 6.7 %all-to-all-start.2 = ((bf16[4,2048,128]{1,2,0:T(8,128)(2,1)}), bf16[4,2048,128]{1,2,0:T(8,128)(2,1)S(1)}, u32[]{:S(2)}, u32[]{:S(2)}) async-start(bf16[4,2048,128]{1,2,0:T(8,128)(2,1)} %copy.31), calls=%async_computation.2 | async-start | bytes 4194304 | tf_op jit(solution)/shard_map/all_to_all | solution.py:60
  184.0 0.0 copy-done.1
  184.0 29.2 %all_gather.3 = bf16[512,512]{1,0:T(8,128)(2,1)S(1)} all-gather(bf16[128,512]{1,0:T(8,128)(2,1)S(1)} %copy-done.1), channel_id=1, replica_groups=mesh['seq'=128,'ch'=4] {'ch'}, dimensions={0}, use_global_device_ids=true | all-gather | bytes 655360 | tf_op jit(solution)/shard_map/all_gather | solution.py:61
  213.2 0.0 all-to-all-done.2
  213.2 2.6 %convolution_convert_fusion.1 = bf16[2048,512]{1,0:T(8,128)(2,1)} fusion(bf16[2048,512]{0,1:T(8,128)(2,1)S(1)} %bitcast.96, bf16[512,512]{1,0:T(8,128)(2,1)S(1)} %all_gather.3), kind=kOutput, calls=%fused_computation.20 | convolution fusion | flops 1074790400 | bytes 4718592 | tf_op jit(solution)/shard_map/dot_general | solution.py:8
  (2 shorter events, 0.0 us)
Async XLA Ops:
  0.0 0.9 copy-start
  0.9 2.6 %copy-start.4 = (bf16[128,128]{1,0:T(8,128)(2,1)S(1)}, bf16[128,128]{1,0:T(8,128)(2,1)}, u32[]{:S(2)}) copy-start(bf16[128,128]{1,0:T(8,128)(2,1)} %param.17) | copy-start | bytes 98308
  8.7 21.0 %copy-start.2 = (f32[128,128]{1,0:T(8,128)S(1)}, f32[128,128]{1,0:T(8,128)}, u32[]{:S(2)}) copy-start(f32[128,128]{1,0:T(8,128)} %param.20) | copy-start | bytes 196612
  8.7 21.1 %copy-start.3 = (f32[128,128]{1,0:T(8,128)S(1)}, f32[128,128]{1,0:T(8,128)}, u32[]{:S(2)}) copy-start(f32[128,128]{1,0:T(8,128)} %param.23) | copy-start | bytes 196612
  8.7 21.3 %copy-start.9 = (bf16[64,128]{1,0:T(8,128)(2,1)S(1)}, bf16[64,128]{1,0:T(8,128)(2,1)}, u32[]{:S(2)}) copy-start(bf16[64,128]{1,0:T(8,128)(2,1)} %param.21) | copy-start | bytes 49156
  8.7 74.2 %all-to-all-start = ((bf16[1,128,64,128]{3,2,0,1:T(8,128)(2,1)}), bf16[1,128,64,128]{3,2,0,1:T(8,128)(2,1)S(1)}, u32[]{:S(2)}, u32[]{:S(2)}) async-start(bf16[1,128,64,128]{3,2,0,1:T(8,128)(2,1)} %copy.26), calls=%async_computation | async-start | bytes 4194304 | tf_op jit(solution)/shard_map/all_to_all | solution.py:41
  83.0 2.5 %copy-start.5 = (bf16[128,128]{1,0:T(8,128)(2,1)S(1)}, bf16[128,128]{1,0:T(8,128)(2,1)}, u32[]{:S(2)}) copy-start(bf16[128,128]{1,0:T(8,128)(2,1)} %param.22) | copy-start | bytes 98308
  83.0 2.5 %copy-start.6 = (bf16[128,128]{1,0:T(8,128)(2,1)S(1)}, bf16[128,128]{1,0:T(8,128)(2,1)}, u32[]{:S(2)}) copy-start(bf16[128,128]{1,0:T(8,128)(2,1)} %param.19) | copy-start | bytes 98308
  163.0 2.9 %copy-start.7 = (f32[128,64]{0,1:T(8,128)S(1)}, f32[128,64]{0,1:T(8,128)}, u32[]{:S(2)}) copy-start(f32[128,64]{0,1:T(8,128)} %param.25) | copy-start | bytes 98308
  163.0 2.9 %copy-start.8 = (bf16[128,128]{1,0:T(8,128)(2,1)S(1)}, bf16[128,128]{1,0:T(8,128)(2,1)}, u32[]{:S(2)}) copy-start(bf16[128,128]{1,0:T(8,128)(2,1)} %param.24) | copy-start | bytes 98308
  168.2 2.8 %copy-start.10 = (bf16[64,64]{1,0:T(8,128)(2,1)S(1)}, bf16[64,64]{1,0:T(8,128)(2,1)}, u32[]{:S(2)}) copy-start(bf16[64,64]{1,0:T(8,128)(2,1)} %param.26) | copy-start | bytes 24580
  177.3 6.7 %copy-start.1 = (bf16[128,512]{1,0:T(8,128)(2,1)S(1)}, bf16[128,512]{1,0:T(8,128)(2,1)}, u32[]{:S(2)}) copy-start(bf16[128,512]{1,0:T(8,128)(2,1)} %param.27) | copy-start | bytes 393220
  177.3 35.9 %all-to-all-start.2 = ((bf16[4,2048,128]{1,2,0:T(8,128)(2,1)}), bf16[4,2048,128]{1,2,0:T(8,128)(2,1)S(1)}, u32[]{:S(2)}, u32[]{:S(2)}) async-start(bf16[4,2048,128]{1,2,0:T(8,128)(2,1)} %copy.31), calls=%async_computation.2 | async-start | bytes 4194304 | tf_op jit(solution)/shard_map/all_to_all | solution.py:60
where the time goes:
time: 216 us
  blocking collectives  90 us (42%)
  waiting for transfers between devices  53 us (25%)
  starting transfers between devices  27.6 us (13%)
  matrix products  22.4 us (10%)
  local copies, waits for them, and re-layouts  20.1 us (9%)
  other arithmetic  2.59 us (1%)
    all_to_all x1, blocking collectives, local(): lax.all_to_all(back, 'seq', split_axis=0, concat_axis=1, tiled=True)  60.8 us
    all_to_all x1, waiting for transfers between devices, local(): lax.all_to_all(second, 'seq', split_axis=1, concat_axis=0, tiled=True)  53 us
    all_gather x1, blocking collectives, local(): lax.all_gather(out_weight, 'ch', axis=0, tiled=True)  29.2 us
    all_to_all x1, starting transfers between devices, local(): lax.all_to_all(second, 'seq', split_axis=1, concat_axis=0, tiled=True)  20.9 us
    dot_general x1, matrix products, local(): jnp.dot(inverse_top, filtered.reshape(top_all, -1), preferred_element_typ...  8.72 us
    all_to_all x1, starting transfers between devices, local(): whole = lax.all_to_all(gated, 'ch', split_axis=0, concat_axis=1, tiled=True)  6.68 us
    reshape x1, local copies, waits for them, and re-layouts, local(): back = back.reshape(top_all, mid_part, low_all, width)  5.38 us
  transfers between devices with their start and end apart: 2, of which 1 were waited for; matrix products, arithmetic and copies ran while one was open for 0% of the time, Pallas kernels for 0%

commit v1 on v0

v1 whole, which is shorter than its diff:
```python
import functools

import jax
import jax.numpy as jnp
from jax import lax
from jax.experimental import pallas as pl
from jax.experimental.pallas import tpu as pltpu
from jax.sharding import PartitionSpec as P

F32 = jnp.float32
BF16 = jnp.bfloat16
STEP = 512


def iota(shape, axis):
    return lax.broadcasted_iota(jnp.int32, shape, axis)


def dot(left, right):
    return jnp.dot(left, right, preferred_element_type=F32)


def widen(source, target):
    rows = target.shape[0]

    def body(n, _):
        at = pl.multiple_of(n * STEP, STEP)
        target[pl.ds(at, STEP), :] = source[pl.ds(at, STEP), :].astype(F32)
        return 0

    lax.fori_loop(0, rows // STEP, body, 0)


def narrow(source, target):
    rows = target.shape[0]

    def body(n, _):
        at = pl.multiple_of(n * STEP, STEP)
        target[pl.ds(at, STEP), :] = source[pl.ds(at, STEP), :].astype(BF16)
        return 0

    lax.fori_loop(0, rows // STEP, body, 0)


def repeat_lanes(matrix, times):
    n = matrix.shape[1]
    shape = (n, n * times)
    pick = (lax.rem(iota(shape, 1), n) == iota(shape, 0)).astype(F32).astype(BF16)
    return dot(matrix, pick)


def column_of_row(row):
    n = row.shape[1]
    square = jnp.broadcast_to(row, (n, n))
    return jnp.sum(jnp.where(iota((n, n), 0) == iota((n, n), 1), square, 0.0), axis=1, keepdims=True)


def forward_kernel(low, values, factor_low, twist_low, factor_mid, twist_top, second, rows_f, rows_g, diag):
    mid = factor_mid.shape[0]
    times = 256 // low
    place = lax.axis_index("seq")
    tiled = repeat_lanes(factor_low[...], times)
    for t in range(times):
        block = jnp.where(iota(tiled.shape, 1) // low == t, tiled, 0.0)
        diag[t * low:(t + 1) * low, :] = block.astype(BF16)

    def lows(n, _):
        at = pl.multiple_of(n * 512, 512)
        top = values[pl.ds(at, 256), :]
        bottom = values[pl.ds(at + 256, 256), :]
        both = dot(diag[...], jnp.concatenate([top, bottom], axis=1))
        rows_f[pl.ds(at, 256), :] = both[:, :128]
        rows_f[pl.ds(at + 256, 256), :] = both[:, 128:]
        return 0

    lax.fori_loop(0, mid * low // 512, lows, 0)
    scaled = column_of_row(twist_top[pl.ds(place, 1), :]) * factor_mid[...].astype(F32)
    for k in range(low):
        matrix = (scaled * twist_low[k:k + 1, :]).astype(BF16)
        piece = rows_f[pl.ds(k, mid, stride=low), :].astype(BF16)
        rows_g[pl.ds(k, mid, stride=low), :] = dot(matrix, piece)
    narrow(rows_g, second)


def filter_kernel(low, columns, factor_top, kernel_top, kernel_low, inverse_top, untwist_top, back, rows_f, rows_g):
    top = factor_top.shape[0]
    place = lax.axis_index("seq")
    widen(columns, rows_f)
    picked = jnp.where(iota((top, top), 1) == place, untwist_top[...], 0.0)
    scale = jnp.broadcast_to(jnp.sum(picked, axis=1, keepdims=True), (top, 128))
    scale = jnp.concatenate([scale, scale], axis=1)
    profile = kernel_top[...]
    for k in range(0, low, 2):
        one = rows_f[pl.ds(k, top, stride=low), :].astype(BF16)
        two = rows_f[pl.ds(k + 1, top, stride=low), :].astype(BF16)
        spectrum = dot(factor_top[...], jnp.concatenate([one, two], axis=1)).astype(BF16).astype(F32)
        first = spectrum[:, :128] * profile * kernel_low[k:k + 1, :].astype(F32)
        other = spectrum[:, 128:] * profile * kernel_low[k + 1:k + 2, :].astype(F32)
        filtered = jnp.concatenate([first.astype(BF16), other.astype(BF16)], axis=1)
        result = scale * dot(inverse_top[...], filtered)
        rows_g[pl.ds(k, top, stride=low), :] = result[:, :128]
        rows_g[pl.ds(k + 1, top, stride=low), :] = result[:, 128:]
    narrow(rows_g, back)


def gate_block(low, third, values, inverse_low, untwist_low, start, groups, gated):
    times = 256 // low
    tiled = repeat_lanes(inverse_low[...], times)
    lane = iota(tiled.shape, 1) // low

    def body(n, _):
        at = pl.multiple_of(start + n * 256, 256)
        weights = tiled * untwist_low[pl.ds(at // 256, 1), :]
        diag = jnp.concatenate([jnp.where(lane == t, weights, 0.0).astype(BF16) for t in range(times)], axis=0)
        mixed = dot(diag, third[pl.ds(at, 256), :].astype(BF16))
        value = values[pl.ds(at, 256), :].astype(F32)
        silu = (0.5 * value) * (1.0 + jnp.tanh(0.5 * value))
        gated[pl.ds(pl.multiple_of(n * 256, 256), 256), :] = (mixed * silu).astype(BF16)
        return 0

    lax.fori_loop(0, groups, body, 0)


def third_kernel(low, turn, restored, values, inverse_mid, inverse_low, untwist_low, third, gated, rows_f, rows_g):
    mid = inverse_mid.shape[0]
    widen(restored, rows_f)
    for k in range(0, low, 2):
        one = rows_f[pl.ds(k, mid, stride=low), :].astype(BF16)
        two = rows_f[pl.ds(k + 1, mid, stride=low), :].astype(BF16)
        result = dot(inverse_mid[...], jnp.concatenate([one, two], axis=1))
        rows_g[pl.ds(k, mid, stride=low), :] = result[:, :128]
        rows_g[pl.ds(k + 1, mid, stride=low), :] = result[:, 128:]
    share = gated.shape[0]
    start = (lax.axis_index("ch") ^ turn) * share
    gate_block(low, rows_g, values, inverse_low, untwist_low, start, share // 256, gated)
    narrow(rows_g, third)


def gate_kernel(low, turns, third, values, inverse_low, untwist_low, *gated):
    for turn, target in zip(turns, gated):
        share = target.shape[0]
        start = (lax.axis_index("ch") ^ turn) * share
        gate_block(low, third, values, inverse_low, untwist_low, start, share // 256, target)


def project_kernel(*refs):
    count = (len(refs) - 1) // 2
    pieces, weights, out = refs[:count], refs[count:2 * count], refs[-1]

    def body(n, _):
        at = pl.multiple_of(n * 256, 256)
        total = dot(pieces[0][pl.ds(at, 256), :], weights[0][...])
        for piece, weight in zip(pieces[1:], weights[1:]):
            total += dot(piece[pl.ds(at, 256), :], weight[...])
        out[pl.ds(at, 256), :] = total.astype(out.dtype)
        return 0

    lax.fori_loop(0, out.shape[0] // 256, body, 0)


def call(kernel, name, out_shape, scratch, flops, *args):
    vmem = pl.BlockSpec(memory_space=pltpu.VMEM)
    outs = jax.tree.leaves(out_shape)
    moved = sum(a.size * a.dtype.itemsize for a in args) + sum(o.size * o.dtype.itemsize for o in outs)
    return pl.pallas_call(
        kernel,
        name=name,
        out_shape=out_shape,
        in_specs=[vmem] * len(args),
        out_specs=jax.tree.map(lambda _: vmem, out_shape),
        scratch_shapes=scratch,
        compiler_params=pltpu.CompilerParams(vmem_limit_bytes=40 << 20),
        cost_estimate=pl.CostEstimate(flops=flops, bytes_accessed=moved, transcendentals=0),
    )(*args)


def local(
    values,
    factor_low,
    twist_low,
    factor_mid,
    twist_top,
    factor_top,
    kernel_top,
    kernel_low,
    inverse_top,
    untwist_top,
    inverse_mid,
    untwist_low,
    inverse_low,
    out_weight,
):
    low = factor_low.shape[0]
    mid = factor_mid.shape[0]
    top = factor_top.shape[0]
    rows, width = values.shape
    ch_count = lax.axis_size("ch")
    share = rows // ch_count
    wide = pltpu.VMEM((rows, width), F32)
    shape = jax.ShapeDtypeStruct((rows, width), BF16)
    part = jax.ShapeDtypeStruct((share, width), BF16)
    unit = 2 * rows * width

    def swap(array, turn):
        return lax.ppermute(array, "ch", [(c, c ^ turn) for c in range(ch_count)])

    second = call(
        functools.partial(forward_kernel, low), "forward", shape,
        [wide, wide, pltpu.VMEM((256, 256), BF16)], unit * (low + mid),
        values, factor_low, twist_low.T, factor_mid, twist_top,
    )
    columns = lax.all_to_all(second.reshape(mid, low, width), "seq", 0, 0, tiled=True)
    weights = [out_weight] + [swap(out_weight, turn) for turn in range(1, ch_count)]
    back = call(
        functools.partial(filter_kernel, low), "filter", shape, [wide, wide], unit * 2 * top,
        columns.reshape(rows, width), factor_top, kernel_top, kernel_low, inverse_top, untwist_top,
    )
    restored = lax.all_to_all(back.reshape(top, low, width), "seq", 0, 0, tiled=True)
    scale = untwist_low.reshape(-1, 256)
    third, far = call(
        functools.partial(third_kernel, low, 2), "third", (shape, part), [wide, wide],
        unit * (mid + low // 4), restored.reshape(rows, width), values, inverse_mid, inverse_low, scale,
    )
    far = swap(far, 2)
    across, = call(
        functools.partial(gate_kernel, low, (3,)), "gate", (part,), [], unit * low // 4,
        third, values, inverse_low, scale,
    )
    across = swap(across, 3)
    near, own = call(
        functools.partial(gate_kernel, low, (1, 0)), "gate", (part, part), [], unit * low // 2,
        third, values, inverse_low, scale,
    )
    near = swap(near, 1)
    return call(
        project_kernel, "project", jax.ShapeDtypeStruct((share, out_weight.shape[1]), BF16), [],
        2 * share * out_weight.shape[1] ** 2,
        own, near, far, across, *weights,
    )


def solution(mesh):
    return jax.shard_map(
        local,
        mesh=mesh,
        in_specs=(
            P("seq", "ch"),
            P(),
            P(),
            P(),
            P(),
            P(),
            P(None, "ch"),
            P("seq", "ch"),
            P(),
            P(),
            P(),
            P(),
            P(),
            P("ch", None),
        ),
        out_specs=P(("seq", "ch"), None),
        check_vma=False,
    )
```

time: 216 us -> 211 us (0.977)
  Pallas kernels: 0 us -> 32 us
  matrix products: 22.4 us -> 0 us
  waiting for transfers between devices: 53 us -> 70.8 us
  blocking collectives: 90 us -> 74 us
  local copies, waits for them, and re-layouts: 20.1 us -> 6.2 us
  other arithmetic: 2.59 us -> 0 us
    pallas_call x0 -> x6, Pallas kernels: none -> 32 us  [call(): pl.pallas_call(kernel, name=name, out_shape=out_shape, in_specs=[vmem] *...]
    all_gather x1 -> x0, blocking collectives: 29.2 us -> none  [local(): lax.all_gather(out_weight, 'ch', axis=0, tiled=True)]
    dot_general x6 -> x0, matrix products: 22.4 us -> none  [the longest x1 8.72 us: local(): jnp.dot(inverse_top, filtered.reshape(top_all, -1), preferred_element_typ...]
    ppermute x0 -> x6, waiting for transfers between devices: none -> 18.9 us  [swap(): return lax.ppermute(array, 'ch', [(c, c ^ turn) for c in range(ch_count)])]
    all_to_all x2 -> x1, starting transfers between devices: 27.6 us -> 9.15 us  [local(): lax.all_to_all(back.reshape(top, low, width), 'seq', 0, 0, tiled=True)]
    ppermute x0 -> x6, starting transfers between devices: none -> 18.2 us  [swap(): return lax.ppermute(array, 'ch', [(c, c ^ turn) for c in range(ch_count)])]
    all_to_all x1, blocking collectives: 60.8 us -> 74 us  [local(): lax.all_to_all(second.reshape(mid, low, width), 'seq', 0, 0, tiled=True)]
    all_to_all x2 -> x0, local copies, waits for them, and re-layouts: 5.5 us -> none  [the longest x1 2.9 us: local(): lax.all_to_all(back, 'seq', split_axis=0, concat_axis=1, tiled=True)]
  transfers between devices with their start and end apart: 2 -> 7, of which waited for: 1 -> 3; matrix products, arithmetic and copies ran while one was open for 0% -> 0% of each run, Pallas kernels for 0% -> 0%
where the time goes in v1:
time: 211 us
  blocking collectives  74 us (35%)
  waiting for transfers between devices  70.8 us (34%)
  Pallas kernels  32 us (15%)
  starting transfers between devices  27.3 us (13%)
  local copies, waits for them, and re-layouts  6.2 us (3%)
    all_to_all x1, blocking collectives, local(): lax.all_to_all(second.reshape(mid, low, width), 'seq', 0, 0, tiled=True)  74 us
    all_to_all x1, waiting for transfers between devices, local(): lax.all_to_all(back.reshape(top, low, width), 'seq', 0, 0, tiled=True)  51.9 us
    pallas_call x6, Pallas kernels, call(): pl.pallas_call(kernel, name=name, out_shape=out_shape, in_specs=[vmem] *...  32 us
    ppermute x6, waiting for transfers between devices, swap(): return lax.ppermute(array, 'ch', [(c, c ^ turn) for c in range(ch_count)])  18.9 us
    ppermute x6, starting transfers between devices, swap(): return lax.ppermute(array, 'ch', [(c, c ^ turn) for c in range(ch_count)])  18.2 us
    all_to_all x1, starting transfers between devices, local(): lax.all_to_all(back.reshape(top, low, width), 'seq', 0, 0, tiled=True)  9.15 us
    unnamed x33, local copies, waits for them, and re-layouts  6.12 us
  transfers between devices with their start and end apart: 7, of which 3 were waited for; matrix products, arithmetic and copies ran while one was open for 0% of the time, Pallas kernels for 0%

profile of v1, /device:TPU:1, one launch (start us, length us, event | category | flops | bytes accessed | tf_op | source)
XLA Modules:
  0.0 210.6 jit_solution(11314260397332858247)
XLA Ops:
  0.0 0.0 copy-start
  0.0 1.6 copy-done
  1.6 0.0 copy-start.5
  1.6 0.8 copy-done.5
  2.4 0.0 copy-start.8
  2.4 0.8 copy-done.8
  3.2 0.0 copy-start.9
  3.2 0.8 copy-done.9
  3.9 0.0 copy-start.13
  4.0 0.7 copy-done.13
  4.7 8.6 %forward.1 = bf16[8192,128]{1,0:T(8,128)(2,1)S(1)} custom-call(bf16[8192,128]{1,0:T(8,128)(2,1)S(1)} %copy-done, bf16[64,64]{1,0:T(8,128)(2,1)S(1)} %copy-done.13, f32[64,128]{1,0:T(8,128)S(1)} %bitcast.8, bf16[128,128]{1,0:T(8,128)(2,1)S(1)} %copy-done.9, f32[128,128]{1,0:T(8,128)S(1)} %copy-done.5), custom_call_target="tpu_custom_call" | custom-call | flops 402653184 | bytes 4333568 | tf_op jit(solution)/shard_map/forward/pallas_call | solution.py:165
  13.3 0.0 copy-start.6
  13.3 0.0 copy-start.7
  13.3 0.0 copy-start.10
  13.3 0.0 copy-start.11
  13.3 0.0 copy-start.14
  13.3 74.0 %all_to_all.10 = bf16[128,64,128]{2,1,0:T(8,128)(2,1)S(1)} all-to-all(bf16[128,64,128]{2,1,0:T(8,128)(2,1)S(1)} %bitcast.7), channel_id=1, replica_groups=mesh['seq'=128,'ch'=4] {'seq'}, dimensions={0} | all-to-all | bytes 4194304 | tf_op jit(solution)/shard_map/all_to_all | solution.py:212
  87.4 0.0 copy-done.6
  87.4 0.0 copy-done.7
  87.4 0.0 copy-done.10
  87.4 0.0 copy-done.11
  87.4 0.0 copy-done.14
  87.4 5.8 %filter.1 = bf16[8192,128]{1,0:T(8,128)(2,1)S(1)} custom-call(bf16[8192,128]{1,0:T(8,128)(2,1)S(1)} %bitcast.6, bf16[128,128]{1,0:T(8,128)(2,1)S(1)} %copy-done.10, f32[128,128]{1,0:T(8,128)S(1)} %copy-done.6, bf16[64,128]{1,0:T(8,128)(2,1)S(1)} %copy-done.14, bf16[128,128]{1,0:T(8,128)(2,1)S(1)} %copy-done.11, f32[128,128]{1,0:T(8,128)S(1)} %copy-done.7), custom_call_target="tpu_custom_call" | custom-call | flops 536870912 | bytes 4407296 | tf_op jit(solution)/shard_map/filter/pallas_call | solution.py:165
  93.2 0.0 copy-start.2
  93.2 1.3 copy-done.2
  94.5 0.0 copy-start.15
  94.5 0.0 copy-start.1
  94.5 0.0 copy-start.3
  94.5 0.0 copy-start.12
  94.5 9.1 %all-to-all-start.1 = ((bf16[128,64,128]{2,1,0:T(8,128)(2,1)}), bf16[128,64,128]{2,1,0:T(8,128)(2,1)}, u32[]{:S(2)}, u32[]{:S(2)}) async-start(bf16[128,64,128]{2,1,0:T(8,128)(2,1)} %bitcast.5), calls=%async_computation.1 | async-start | bytes 4194304 | tf_op jit(solution)/shard_map/all_to_all | solution.py:218
  103.7 0.0 copy-done.15
  103.7 0.1 copy.16
  103.8 0.1 reshape.19.untwist_low
  103.9 51.9 %all-to-all-done.1 = bf16[128,64,128]{2,1,0:T(8,128)(2,1)} async-done(((bf16[128,64,128]{2,1,0:T(8,128)(2,1)}), bf16[128,64,128]{2,1,0:T(8,128)(2,1)}, u32[]{:S(2)}, u32[]{:S(2)}) %all-to-all-start.1) | async-done | bytes 2097184 | tf_op jit(solution)/shard_map/all_to_all | solution.py:218
  155.7 0.0 copy-done.1
  155.7 0.0 copy-done.3
  155.7 0.0 copy-done.12
  155.7 8.4 %third.1 = (bf16[8192,128]{1,0:T(8,128)(2,1)S(1)}, bf16[2048,128]{1,0:T(8,128)(2,1)S(1)}) custom-call(bf16[8192,128]{1,0:T(8,128)(2,1)} %bitcast.4.restored, bf16[8192,128]{1,0:T(8,128)(2,1)S(1)} %copy-done.1, bf16[128,128]{1,0:T(8,128)(2,1)S(1)} %copy-done.12, bf16[64,64]{1,0:T(8,128)(2,1)S(1)} %copy-done.3, f32[32,256]{1,0:T(8,128)S(1)} %reshape.19.untwist_low), custom_call_target="tpu_custom_call" | custom-call | flops 301989888 | bytes 6889472 | tf_op jit(solution)/shard_map/third/pallas_call | solution.py:165
  164.1 3.1 %gate.2 = (bf16[2048,128]{1,0:T(8,128)(2,1)S(1)}, bf16[2048,128]{1,0:T(8,128)(2,1)S(1)}) custom-call(bf16[8192,128]{1,0:T(8,128)(2,1)S(1)} %get-tuple-element.9.third, bf16[8192,128]{1,0:T(8,128)(2,1)S(1)} %copy-done.1, bf16[64,64]{1,0:T(8,128)(2,1)S(1)} %copy-done.3, f32[32,256]{1,0:T(8,128)S(1)} %reshape.19.untwist_low), custom_call_target="tpu_custom_call" | custom-call | flops 67108864 | bytes 5283840 | tf_op jit(solution)/shard_map/gate/pallas_call | solution.py:165
  167.2 0.0 copy-start.4
  167.2 1.5 gate.3
  168.8 4.8 %collective-permute-start = (bf16[2048,128]{1,0:T(8,128)(2,1)S(1)}, bf16[2048,128]{1,0:T(8,128)(2,1)S(1)}, u32[]{:S(2)}, u32[]{:S(2)}) collective-permute-start(bf16[2048,128]{1,0:T(8,128)(2,1)S(1)} %get-tuple-element.11), channel_id=1, source_target_pairs={{0,1},{1,0},{2,3},{3,2},{4,5},{5,4},{6,7},{7,6},{8,9},{9,8},{10,11... | collective-permute-start | bytes 1572872 | tf_op jit(solution)/shard_map/ppermute | solution.py:205
  173.6 2.1 %collective-permute-start.2 = (bf16[2048,128]{1,0:T(8,128)(2,1)S(1)}, bf16[2048,128]{1,0:T(8,128)(2,1)S(1)}, u32[]{:S(2)}, u32[]{:S(2)}) collective-permute-start(bf16[2048,128]{1,0:T(8,128)(2,1)S(1)} %gate.3), channel_id=1, source_target_pairs={{0,3},{1,2},{2,1},{3,0},{4,7},{5,6},{6,5},{7,4},{8,11},{9,10},{10,... | collective-permute-start | bytes 1572872 | tf_op jit(solution)/shard_map/ppermute | solution.py:205
  175.8 3.0 %collective-permute-start.1 = (bf16[2048,128]{1,0:T(8,128)(2,1)S(1)}, bf16[2048,128]{1,0:T(8,128)(2,1)S(1)}, u32[]{:S(2)}, u32[]{:S(2)}) collective-permute-start(bf16[2048,128]{1,0:T(8,128)(2,1)S(1)} %get-tuple-element.12), channel_id=1, source_target_pairs={{0,2},{1,3},{2,0},{3,1},{4,6},{5,7},{6,4},{7,5},{8,10},{9,11},{10,... | collective-permute-start | bytes 1572872 | tf_op jit(solution)/shard_map/ppermute | solution.py:205
  178.8 0.0 copy-done.4
  178.8 2.7 %collective-permute-start.3 = (bf16[128,512]{1,0:T(8,128)(2,1)S(1)}, bf16[128,512]{1,0:T(8,128)(2,1)S(1)}, u32[]{:S(2)}, u32[]{:S(2)}) collective-permute-start(bf16[128,512]{1,0:T(8,128)(2,1)S(1)} %copy-done.4), channel_id=1, source_target_pairs={{0,1},{1,0},{2,3},{3,2},{4,5},{5,4},{6,7},{7,6},{8,9},{9,8},{10,11... | collective-permute-start | bytes 393224 | tf_op jit(solution)/shard_map/ppermute | solution.py:205
  181.5 2.2 %collective-permute-start.4 = (bf16[128,512]{1,0:T(8,128)(2,1)S(1)}, bf16[128,512]{1,0:T(8,128)(2,1)S(1)}, u32[]{:S(2)}, u32[]{:S(2)}) collective-permute-start(bf16[128,512]{1,0:T(8,128)(2,1)S(1)} %copy-done.4), channel_id=1, source_target_pairs={{0,2},{1,3},{2,0},{3,1},{4,6},{5,7},{6,4},{7,5},{8,10},{9,11},{10,... | collective-permute-start | bytes 393224 | tf_op jit(solution)/shard_map/ppermute | solution.py:205
  183.8 0.0 collective-permute-done.3.refs_5_
  183.8 3.2 %collective-permute-start.5 = (bf16[128,512]{1,0:T(8,128)(2,1)S(1)}, bf16[128,512]{1,0:T(8,128)(2,1)S(1)}, u32[]{:S(2)}, u32[]{:S(2)}) collective-permute-start(bf16[128,512]{1,0:T(8,128)(2,1)S(1)} %copy-done.4), channel_id=1, source_target_pairs={{0,3},{1,2},{2,1},{3,0},{4,7},{5,6},{6,5},{7,4},{8,11},{9,10},{10,... | collective-permute-start | bytes 393224 | tf_op jit(solution)/shard_map/ppermute | solution.py:205
  187.0 15.8 %collective-permute-done.4.refs_6_ = bf16[128,512]{1,0:T(8,128)(2,1)S(1)} collective-permute-done((bf16[128,512]{1,0:T(8,128)(2,1)S(1)}, bf16[128,512]{1,0:T(8,128)(2,1)S(1)}, u32[]{:S(2)}, u32[]{:S(2)}) %collective-permute-start.4) | collective-permute-done | bytes 131104 | tf_op jit(solution)/shard_map/ppermute | solution.py:205
  202.8 3.1 %collective-permute-done.5.refs_7_ = bf16[128,512]{1,0:T(8,128)(2,1)S(1)} collective-permute-done((bf16[128,512]{1,0:T(8,128)(2,1)S(1)}, bf16[128,512]{1,0:T(8,128)(2,1)S(1)}, u32[]{:S(2)}, u32[]{:S(2)}) %collective-permute-start.5) | collective-permute-done | bytes 131104 | tf_op jit(solution)/shard_map/ppermute | solution.py:205
  205.9 0.0 collective-permute-done.refs_1_
  205.9 0.0 collective-permute-done.2.refs_3_
  205.9 0.0 collective-permute-done.1.refs_2_
  205.9 4.6 %project.1 = bf16[2048,512]{1,0:T(8,128)(2,1)} custom-call(bf16[2048,128]{1,0:T(8,128)(2,1)S(1)} %get-tuple-element.10.refs_0_, bf16[2048,128]{1,0:T(8,128)(2,1)S(1)} %collective-permute-done.refs_1_, bf16[2048,128]{1,0:T(8,128)(2,1)S(1)} %collective-permute-done.1.refs_2_, bf16[2048,128]{1,0:T(8,128)(2,1)S(1)} %collective-permute-done.2.refs_3_, ...), custom_call_target="tpu_custom_call" | custom-call | flops 1073741824 | bytes 4718592 | tf_op jit(solution)/shard_map/project/pallas_call | solution.py:165
Async XLA Ops:
  0.0 1.6 copy-start
  1.6 0.8 copy-start.5
  2.4 0.8 copy-start.8
  3.2 0.8 copy-start.9
  3.9 0.7 copy-start.13
  13.3 74.1 %copy-start.6 = (f32[128,128]{1,0:T(8,128)S(1)}, f32[128,128]{1,0:T(8,128)}, u32[]{:S(2)}) copy-start(f32[128,128]{1,0:T(8,128)} %kernel_top.1) | copy-start | bytes 196612
  13.3 74.1 %copy-start.7 = (f32[128,128]{1,0:T(8,128)S(1)}, f32[128,128]{1,0:T(8,128)}, u32[]{:S(2)}) copy-start(f32[128,128]{1,0:T(8,128)} %untwist_top.1) | copy-start | bytes 196612
  13.3 74.1 %copy-start.10 = (bf16[128,128]{1,0:T(8,128)(2,1)S(1)}, bf16[128,128]{1,0:T(8,128)(2,1)}, u32[]{:S(2)}) copy-start(bf16[128,128]{1,0:T(8,128)(2,1)} %factor_top.1) | copy-start | bytes 98308
  13.3 74.1 %copy-start.11 = (bf16[128,128]{1,0:T(8,128)(2,1)S(1)}, bf16[128,128]{1,0:T(8,128)(2,1)}, u32[]{:S(2)}) copy-start(bf16[128,128]{1,0:T(8,128)(2,1)} %inverse_top.1) | copy-start | bytes 98308
  13.3 74.1 %copy-start.14 = (bf16[64,128]{1,0:T(8,128)(2,1)S(1)}, bf16[64,128]{1,0:T(8,128)(2,1)}, u32[]{:S(2)}) copy-start(bf16[64,128]{1,0:T(8,128)(2,1)} %kernel_low.1) | copy-start | bytes 49156
  93.2 1.3 copy-start.2
  94.5 9.2 %copy-start.15 = (f32[128,64]{0,1:T(8,128)S(1)}, f32[128,64]{0,1:T(8,128)}, u32[]{:S(2)}) copy-start(f32[128,64]{0,1:T(8,128)} %param.25) | copy-start | bytes 98308
  94.5 61.2 %copy-start.1 = (bf16[8192,128]{1,0:T(8,128)(2,1)S(1)}, bf16[8192,128]{1,0:T(8,128)(2,1)}, u32[]{:S(2)}) copy-start(bf16[8192,128]{1,0:T(8,128)(2,1)} %values.7) | copy-start | bytes 6291460
  94.5 61.2 %copy-start.3 = (bf16[64,64]{1,0:T(8,128)(2,1)S(1)}, bf16[64,64]{1,0:T(8,128)(2,1)}, u32[]{:S(2)}) copy-start(bf16[64,64]{1,0:T(8,128)(2,1)} %inverse_low.5) | copy-start | bytes 24580
  94.5 61.2 %copy-start.12 = (bf16[128,128]{1,0:T(8,128)(2,1)S(1)}, bf16[128,128]{1,0:T(8,128)(2,1)}, u32[]{:S(2)}) copy-start(bf16[128,128]{1,0:T(8,128)(2,1)} %inverse_mid.1) | copy-start | bytes 98308
  94.5 61.2 %all-to-all-start.1 = ((bf16[128,64,128]{2,1,0:T(8,128)(2,1)}), bf16[128,64,128]{2,1,0:T(8,128)(2,1)}, u32[]{:S(2)}, u32[]{:S(2)}) async-start(bf16[128,64,128]{2,1,0:T(8,128)(2,1)} %bitcast.5), calls=%async_computation.1 | async-start | bytes 4194304 | tf_op jit(solution)/shard_map/all_to_all | solution.py:218
  167.2 11.6 %copy-start.4 = (bf16[128,512]{1,0:T(8,128)(2,1)S(1)}, bf16[128,512]{1,0:T(8,128)(2,1)}, u32[]{:S(2)}) copy-start(bf16[128,512]{1,0:T(8,128)(2,1)} %refs_4_.1) | copy-start | bytes 393220
  168.8 37.2 %collective-permute-start = (bf16[2048,128]{1,0:T(8,128)(2,1)S(1)}, bf16[2048,128]{1,0:T(8,128)(2,1)S(1)}, u32[]{:S(2)}, u32[]{:S(2)}) collective-permute-start(bf16[2048,128]{1,0:T(8,128)(2,1)S(1)} %get-tuple-element.11), channel_id=1, source_target_pairs={{0,1},{1,0},{2,3},{3,2},{4,5},{5,4},{6,7},{7,6},{8,9},{9,8},{10,11... | collective-permute-start | bytes 1572872 | tf_op jit(solution)/shard_map/ppermute | solution.py:205
  173.6 32.3 %collective-permute-start.2 = (bf16[2048,128]{1,0:T(8,128)(2,1)S(1)}, bf16[2048,128]{1,0:T(8,128)(2,1)S(1)}, u32[]{:S(2)}, u32[]{:S(2)}) collective-permute-start(bf16[2048,128]{1,0:T(8,128)(2,1)S(1)} %gate.3), channel_id=1, source_target_pairs={{0,3},{1,2},{2,1},{3,0},{4,7},{5,6},{6,5},{7,4},{8,11},{9,10},{10,... | collective-permute-start | bytes 1572872 | tf_op jit(solution)/shard_map/ppermute | solution.py:205
  175.8 30.2 %collective-permute-start.1 = (bf16[2048,128]{1,0:T(8,128)(2,1)S(1)}, bf16[2048,128]{1,0:T(8,128)(2,1)S(1)}, u32[]{:S(2)}, u32[]{:S(2)}) collective-permute-start(bf16[2048,128]{1,0:T(8,128)(2,1)S(1)} %get-tuple-element.12), channel_id=1, source_target_pairs={{0,2},{1,3},{2,0},{3,1},{4,6},{5,7},{6,4},{7,5},{8,10},{9,11},{10,... | collective-permute-start | bytes 1572872 | tf_op jit(solution)/shard_map/ppermute | solution.py:205
  178.8 4.9 %collective-permute-start.3 = (bf16[128,512]{1,0:T(8,128)(2,1)S(1)}, bf16[128,512]{1,0:T(8,128)(2,1)S(1)}, u32[]{:S(2)}, u32[]{:S(2)}) collective-permute-start(bf16[128,512]{1,0:T(8,128)(2,1)S(1)} %copy-done.4), channel_id=1, source_target_pairs={{0,1},{1,0},{2,3},{3,2},{4,5},{5,4},{6,7},{7,6},{8,9},{9,8},{10,11... | collective-permute-start | bytes 393224 | tf_op jit(solution)/shard_map/ppermute | solution.py:205
  181.5 21.2 %collective-permute-start.4 = (bf16[128,512]{1,0:T(8,128)(2,1)S(1)}, bf16[128,512]{1,0:T(8,128)(2,1)S(1)}, u32[]{:S(2)}, u32[]{:S(2)}) collective-permute-start(bf16[128,512]{1,0:T(8,128)(2,1)S(1)} %copy-done.4), channel_id=1, source_target_pairs={{0,2},{1,3},{2,0},{3,1},{4,6},{5,7},{6,4},{7,5},{8,10},{9,11},{10,... | collective-permute-start | bytes 393224 | tf_op jit(solution)/shard_map/ppermute | solution.py:205
  183.8 22.1 %collective-permute-start.5 = (bf16[128,512]{1,0:T(8,128)(2,1)S(1)}, bf16[128,512]{1,0:T(8,128)(2,1)S(1)}, u32[]{:S(2)}, u32[]{:S(2)}) collective-permute-start(bf16[128,512]{1,0:T(8,128)(2,1)S(1)} %copy-done.4), channel_id=1, source_target_pairs={{0,3},{1,2},{2,1},{3,0},{4,7},{5,6},{6,5},{7,4},{8,11},{9,10},{10,... | collective-permute-start | bytes 393224 | tf_op jit(solution)/shard_map/ppermute | solution.py:205

commit v2 on v0

v2 whole, which is shorter than its diff:
```python
import functools

import jax
import jax.numpy as jnp
from jax import lax
from jax.experimental import pallas as pl
from jax.experimental.pallas import tpu as pltpu
from jax.sharding import PartitionSpec as P

F32 = jnp.float32
BF16 = jnp.bfloat16
LANES = 128
HALF = 64
PITCH = 72


def iota(shape, axis):
    return lax.broadcasted_iota(jnp.int32, shape, axis)


def dot(left, right):
    return jnp.dot(left, right, preferred_element_type=F32)


def repeat_lanes(matrix, times):
    n = matrix.shape[1]
    shape = (n, n * times)
    pick = (lax.rem(iota(shape, 1), n) == iota(shape, 0)).astype(F32).astype(BF16)
    return dot(matrix, pick)


def column_of_row(row):
    n = row.shape[1]
    square = jnp.broadcast_to(row, (n, n))
    return jnp.sum(jnp.where(iota((n, n), 0) == iota((n, n), 1), square, 0.0), axis=1, keepdims=True)


def trade_halves(one, two):
    low = iota(one.shape, 1) < HALF
    return jnp.where(low, one, pltpu.roll(two, HALF, 1)), jnp.where(low, pltpu.roll(one, HALF, 1), two)


def forward_kernel(low, values, factor_low, twist_low, factor_mid, twist_top, kernel_low, message, rows_f, diag):
    mid = factor_mid.shape[0]
    times = 256 // low
    place = lax.axis_index("seq")
    tiled = repeat_lanes(factor_low[...], times)
    for t in range(times):
        block = jnp.where(iota(tiled.shape, 1) // low == t, tiled, 0.0)
        diag[t * low:(t + 1) * low, :] = block.astype(BF16)

    def lows(n, _):
        at = pl.multiple_of(n * 512, 512)
        top = values[pl.ds(at, 256), :]
        bottom = values[pl.ds(at + 256, 256), :]
        both = dot(diag[...], jnp.concatenate([top, bottom], axis=1))
        for t in range(2 * times):
            to = pl.multiple_of((n * 2 * times + t) * PITCH, 8)
            side = t // times * LANES
            at = t % times * low
            rows_f[pl.ds(to, low), :] = both[at:at + low, side:side + LANES]
        return 0

    lax.fori_loop(0, mid * low // 512, lows, 0)
    scaled = column_of_row(twist_top[pl.ds(place, 1), :]) * factor_mid[...].astype(F32)
    profile = kernel_low[...].astype(F32)
    turned = pltpu.roll(profile, HALF, 1)
    for k in range(low):
        matrix = (scaled * twist_low[k:k + 1, :]).astype(BF16)
        second = dot(matrix, rows_f[pl.ds(k, mid, stride=PITCH), :].astype(BF16))
        halves = trade_halves(second[:HALF], second[HALF:])
        for h, (half, row) in enumerate(zip(halves, (profile, turned))):
            to = (2 * k + h) * PITCH
            message[to:to + HALF, :] = half.astype(BF16)
            message[to + HALF:to + PITCH, :] = jnp.broadcast_to(row[k:k + 1, :], (PITCH - HALF, LANES)).astype(BF16)


def middle_kernel(columns, factor_top, kernel_top, inverse_top, untwist_top, inverse_mid, untwist_low, third,
                  rows_f, rows_g, profile):
    top = factor_top.shape[0]

    def widen(n, _):
        at = pl.multiple_of(n * 8 * PITCH, 8 * PITCH)
        rows_f[pl.ds(at, 8 * PITCH), :] = columns[pl.ds(at, 8 * PITCH), :].astype(F32)
        return 0

    lax.fori_loop(0, top // 8, widen, 0)
    rows = rows_f[pl.ds(HALF, 2 * HALF, stride=PITCH), :]
    profile[...] = trade_halves(rows[:HALF], rows[HALF:])[0]
    for r in range(0, HALF, 2):
        one = rows_f[pl.ds(r, top, stride=PITCH), :].astype(BF16)
        two = rows_f[pl.ds(r + 1, top, stride=PITCH), :].astype(BF16)
        spectrum = dot(factor_top[...], jnp.concatenate([one, two], axis=1)).astype(BF16).astype(F32)
        first = spectrum[:, :LANES] * kernel_top[...] * profile[r:r + 1, :]
        other = spectrum[:, LANES:] * kernel_top[...] * profile[r + 1:r + 2, :]
        filtered = jnp.concatenate([first.astype(BF16), other.astype(BF16)], axis=1)
        back = dot(inverse_top[...], filtered)
        rows_g[pl.ds(r, top, stride=PITCH), :] = back[:, :LANES] * untwist_top[r * top:(r + 1) * top, :]
        rows_g[pl.ds(r + 1, top, stride=PITCH), :] = back[:, LANES:] * untwist_top[(r + 1) * top:(r + 2) * top, :]

    def inverse(n, _):
        sides = []
        for m in range(2):
            at = pl.multiple_of((n * 4 + m * 2) * PITCH, 8)
            upper, lower = trade_halves(rows_g[pl.ds(at, HALF), :], rows_g[pl.ds(at + PITCH, HALF), :])
            sides.append(jnp.concatenate([upper.astype(BF16), lower.astype(BF16)], axis=0))
        result = dot(inverse_mid[...], jnp.concatenate(sides, axis=1))
        for m in range(2):
            side = result[:, m * LANES:(m + 1) * LANES] * untwist_low[...]
            for q in range(4):
                pair = trade_halves(side[q * 32:q * 32 + 16], side[q * 32 + 16:q * 32 + 32])
                for p in range(2):
                    to = pl.multiple_of((n * 4 + m * 2 + p) * HALF + q * 16, 16)
                    third[pl.ds(to, 16), :] = pair[p].astype(BF16)
        return 0

    lax.fori_loop(0, top // 4, inverse, 0)


def prepare_kernel(kernel_top, untwist_top, untwist_low, *refs):
    sources, targets, (profile, scale_top, scale_low) = refs[:4], refs[4:8], refs[8:]
    place = lax.axis_index("seq")
    top = untwist_top.shape[0]
    shape = (top, LANES)
    lower = iota(shape, 1) < HALF
    whole = kernel_top[...]
    turned = pltpu.roll(whole, HALF, 1)
    first = lax.rem(place, 2) == 0
    profile[...] = jnp.where(first, jnp.where(lower, whole, turned), jnp.where(lower, turned, whole))
    scale_low[...] = jnp.broadcast_to(column_of_row(untwist_low[pl.ds(place // 2, 1), :]), scale_low.shape)
    for r in range(HALF):
        one = jnp.broadcast_to(untwist_top[:, r:r + 1], shape)
        two = jnp.broadcast_to(untwist_top[:, HALF + r:HALF + r + 1], shape)
        scale_top[r * top:(r + 1) * top, :] = jnp.where(lower, one, two)
    for source, target in zip(sources, targets):
        def body(n, _):
            at = pl.multiple_of(n * 256, 256)
            value = source[pl.ds(at, 256), :].astype(F32)
            target[pl.ds(at, 256), :] = (0.5 * value) * (1.0 + jnp.tanh(0.5 * value))
            return 0

        lax.fori_loop(0, source.shape[0] // 256, body, 0)


def last_kernel(low, third, inverse_low, *refs):
    silus, weights, out, rows_f, gated, result, sem = refs[:4], refs[4:8], refs[8], refs[9], refs[10], refs[11], refs[12]
    pitch = LANES + 8
    place = lax.axis_index("ch")

    def widen(k, _):
        for h in range(2):
            for t in range(4):
                source = pl.multiple_of(((k * 2 + h) * 4 + (place ^ t)) * 16, 16)
                to = pl.multiple_of(k * pitch + (h * 4 + t) * 16, 8)
                rows_f[pl.ds(to, 16), :] = third[pl.ds(source, 16), :].astype(F32)
        return 0

    lax.fori_loop(0, low, widen, 0)
    block = 4 * low
    copies = []
    for g in range(4):
        for b in range(4 * g, 4 * g + 4):
            for t in range(4):
                one = rows_f[pl.ds(t * 16 + b, low, stride=pitch), :]
                two = rows_f[pl.ds((4 + t) * 16 + b, low, stride=pitch), :]
                pair = trade_halves(one, two)
                mixed = dot(inverse_low[...], jnp.concatenate([p.astype(BF16) for p in pair], axis=1))
                for p in range(2):
                    at = (p * 16 + b) * low
                    gate = silus[t][at:at + low, :]
                    gated[at:at + low, t * LANES:(t + 1) * LANES] = (
                        mixed[:, p * LANES:(p + 1) * LANES] * gate
                    ).astype(BF16)
        for p in range(2):
            at = (p * 4 + g) * block
            total = dot(gated[at:at + block, :LANES], weights[0][...])
            for t in range(1, 4):
                total += dot(gated[at:at + block, t * LANES:(t + 1) * LANES], weights[t][...])
            result[at:at + block, :] = total.astype(BF16)
            slot = g * 2 + p
            copy = pltpu.make_async_copy(result.at[pl.ds(at, block)], out.at[pl.ds(at, block)], sem.at[slot])
            copy.start()
            copies.append(copy)
    for copy in copies:
        copy.wait()


def call(kernel, name, out_shape, scratch, flops, *args, limit=40 << 20, out_spec=None):
    vmem = pl.BlockSpec(memory_space=pltpu.VMEM)
    outs = jax.tree.leaves(out_shape)
    moved = sum(a.size * a.dtype.itemsize for a in args) + sum(o.size * o.dtype.itemsize for o in outs)
    return pl.pallas_call(
        kernel,
        name=name,
        out_shape=out_shape,
        in_specs=[vmem] * len(args),
        out_specs=jax.tree.map(lambda _: out_spec or vmem, out_shape),
        scratch_shapes=scratch,
        compiler_params=pltpu.CompilerParams(vmem_limit_bytes=limit),
        cost_estimate=pl.CostEstimate(flops=flops, bytes_accessed=moved, transcendentals=0),
    )(*args)


def local(
    values,
    factor_low,
    twist_low,
    factor_mid,
    twist_top,
    factor_top,
    kernel_top,
    kernel_low,
    inverse_top,
    untwist_top,
    inverse_mid,
    untwist_low,
    inverse_low,
    out_weight,
):
    low = factor_low.shape[0]
    mid = factor_mid.shape[0]
    top = factor_top.shape[0]
    rows, width = values.shape
    ch_place = lax.axis_index("ch")
    ch_count = lax.axis_size("ch")
    share = rows // ch_count
    columns_out = out_weight.shape[1]
    unit = 2 * rows * width
    padded = pltpu.VMEM((top * PITCH, width), F32)

    def swap(array, turn):
        if turn == 0:
            return array
        return lax.ppermute(array, "ch", [(c, c ^ turn) for c in range(ch_count)])

    message = call(
        functools.partial(forward_kernel, low), "forward", jax.ShapeDtypeStruct((2 * low * PITCH, width), BF16),
        [padded, pltpu.VMEM((256, 256), BF16)], unit * (low + mid),
        values, factor_low, twist_low.T, factor_mid, twist_top, kernel_low, limit=60 << 20,
    )
    columns = lax.all_to_all(message.reshape(2 * low, PITCH, width), "seq", 0, 0, tiled=True)

    turns = range(ch_count)
    shares = [
        swap(lax.dynamic_slice_in_dim(values, (ch_place ^ turn) * share, share, 0), turn) for turn in turns
    ]
    weights = [swap(out_weight, turn) for turn in turns]
    *silus, profile, scale_top, scale_low = call(
        prepare_kernel, "prepare",
        [jax.ShapeDtypeStruct((share, width), F32)] * ch_count
        + [jax.ShapeDtypeStruct((n, width), F32) for n in (top, HALF * top, mid)],
        [], unit, kernel_top, untwist_top, untwist_low.T, *shares,
    )
    columns, silus, weights, profile, scale_top, scale_low = lax.optimization_barrier(
        (columns, silus, weights, profile, scale_top, scale_low)
    )

    third = call(
        middle_kernel, "middle", jax.ShapeDtypeStruct((rows, width), BF16),
        [padded, padded, pltpu.VMEM((HALF, width), F32)], unit * (2 * top + mid),
        columns.reshape(top * PITCH, width), factor_top, profile, inverse_top, scale_top, inverse_mid, scale_low,
    )
    third = lax.all_to_all(third.reshape(top * ch_count, -1, width), ("seq", "ch"), 0, 0, tiled=True)
    return call(
        functools.partial(last_kernel, low), "last", jax.ShapeDtypeStruct((share, columns_out), BF16),
        [
            pltpu.VMEM((low * (width + 8), width), F32),
            pltpu.VMEM((share, columns_out), BF16),
            pltpu.VMEM((share, columns_out), BF16),
            pltpu.SemaphoreType.DMA((8,)),
        ],
        unit * low // 2 + 2 * share * columns_out ** 2,
        third.reshape(rows, width), inverse_low, *silus, *weights,
        out_spec=pl.BlockSpec(memory_space=pl.ANY),
    )


def solution(mesh):
    return jax.shard_map(
        local,
        mesh=mesh,
        in_specs=(
            P("seq", "ch"),
            P(),
            P(),
            P(),
            P(),
            P(),
            P(None, "ch"),
            P("seq", "ch"),
            P(),
            P(),
            P(),
            P(),
            P(),
            P("ch", None),
        ),
        out_specs=P(("seq", "ch"), None),
        check_vma=False,
    )
```

time: 216 us -> 186 us (0.86)
  Pallas kernels: 0 us -> 28.2 us
  matrix products: 22.4 us -> 0 us
  waiting for transfers between devices: 53 us -> 31.4 us
  blocking collectives: 90 us -> 72.2 us
  starting transfers between devices: 27.6 us -> 37.1 us
  local copies, waits for them, and re-layouts: 20.1 us -> 16.1 us
  other arithmetic: 2.59 us -> 0 us
    all_to_all x2 -> x1, waiting for transfers between devices: 53 us -> 0.01 us  [local(): lax.all_to_all(message.reshape(2 * low, PITCH, width), 'seq', 0, 0, tiled...]
    ppermute x0 -> x6, waiting for transfers between devices: none -> 31.4 us  [swap(): return lax.ppermute(array, 'ch', [(c, c ^ turn) for c in range(ch_count)])]
    all_gather x1 -> x0, blocking collectives: 29.2 us -> none  [local(): lax.all_gather(out_weight, 'ch', axis=0, tiled=True)]
    pallas_call x0 -> x4, Pallas kernels: none -> 28.2 us  [call(): pl.pallas_call(kernel, name=name, out_shape=out_shape, in_specs=[vmem] *...]
    dot_general x6 -> x0, matrix products: 22.4 us -> none  [the longest x1 8.72 us: local(): jnp.dot(inverse_top, filtered.reshape(top_all, -1), preferred_element_typ...]
    ppermute x0 -> x6, starting transfers between devices: none -> 16.3 us  [swap(): return lax.ppermute(array, 'ch', [(c, c ^ turn) for c in range(ch_count)])]
    unnamed x24 -> x52, local copies, waits for them, and re-layouts: 1.01 us -> 14.3 us
    all_to_all x1, blocking collectives: 60.8 us -> 72.2 us  [local(): lax.all_to_all(third.reshape(top * ch_count, -1, width), ('seq', 'ch'), 0...]
  transfers between devices with their start and end apart: 2 -> 7, of which waited for: 1 -> 2; matrix products, arithmetic and copies ran while one was open for 0% -> 1% of each run, Pallas kernels for 0% -> 2%
where the time goes in v2:
time: 186 us; the launch traced here: 185 us
  blocking collectives  72.2 us (39%)
  starting transfers between devices  37.1 us (20%)
  waiting for transfers between devices  31.4 us (17%)
  Pallas kernels  28.2 us (15%)
  local copies, waits for them, and re-layouts  16.1 us (9%)
    all_to_all x1, blocking collectives, local(): lax.all_to_all(third.reshape(top * ch_count, -1, width), ('seq', 'ch'), 0...  72.2 us
    ppermute x6, waiting for transfers between devices, swap(): return lax.ppermute(array, 'ch', [(c, c ^ turn) for c in range(ch_count)])  31.4 us
    pallas_call x4, Pallas kernels, call(): pl.pallas_call(kernel, name=name, out_shape=out_shape, in_specs=[vmem] *...  28.2 us
    all_to_all x1, starting transfers between devices, local(): lax.all_to_all(message.reshape(2 * low, PITCH, width), 'seq', 0, 0, tiled...  20.8 us
    ppermute x6, starting transfers between devices, swap(): return lax.ppermute(array, 'ch', [(c, c ^ turn) for c in range(ch_count)])  16.3 us
    unnamed x52, local copies, waits for them, and re-layouts  14.3 us
  transfers between devices with their start and end apart: 7, of which 2 were waited for; matrix products, arithmetic and copies ran while one was open for 1% of the time, Pallas kernels for 2%

profile of v2, /device:TPU:1, one launch (start us, length us, event | category | flops | bytes accessed | tf_op | source)
XLA Modules:
  0.0 185.5 jit_solution(8226254772823561745)
XLA Ops:
  0.0 7.6 %forward.1 = bf16[9216,128]{1,0:T(8,128)(2,1)} custom-call(bf16[8192,128]{1,0:T(8,128)(2,1)} %values.1, bf16[64,64]{1,0:T(8,128)(2,1)} %factor_low.1, f32[64,128]{1,0:T(8,128)} %bitcast.11, bf16[128,128]{1,0:T(8,128)(2,1)} %factor_mid.1, f32[128,128]{1,0:T(8,128)} %twist_top.1, bf16[64,128]{1,0:T(8,128)(2,1)} %kernel_low.1), custom_call_target="tpu_custom_call" | custom-call | flops 402653184 | bytes 4612096 | tf_op jit(solution)/shard_map/forward/pallas_call | solution.py:192
  7.7 20.8 %all-to-all-start = ((bf16[128,72,128]{2,1,0:T(8,128)(2,1)}), bf16[128,72,128]{2,1,0:T(8,128)(2,1)S(1)}, u32[]{:S(2)}, u32[]{:S(2)}) async-start(bf16[128,72,128]{2,1,0:T(8,128)(2,1)} %bitcast.10), calls=%async_computation | async-start | bytes 4718592 | tf_op jit(solution)/shard_map/all_to_all | solution.py:241
  28.5 0.0 copy-start.8
  28.5 0.0 copy-start.19
  28.5 0.0 copy-start.20
  28.5 0.0 copy-start.21
  28.5 1.7 constant_dynamic-slice_fusion
  30.3 3.1 %collective-permute-start.2 = (bf16[2048,128]{1,0:T(8,128)(2,1)S(1)}, bf16[2048,128]{1,0:T(8,128)(2,1)S(1)}, u32[]{:S(2)}, u32[]{:S(2)}) collective-permute-start(bf16[2048,128]{1,0:T(8,128)(2,1)S(1)} %get-tuple-element.43), channel_id=1, source_target_pairs={{0,3},{1,2},{2,1},{3,0},{4,7},{5,6},{6,5},{7,4},{8,11},{9,10},{10,... | collective-permute-start | bytes 1572872 | tf_op jit(solution)/shard_map/ppermute | solution.py:234
  33.4 1.9 %collective-permute-start = (bf16[2048,128]{1,0:T(8,128)(2,1)S(1)}, bf16[2048,128]{1,0:T(8,128)(2,1)S(1)}, u32[]{:S(2)}, u32[]{:S(2)}) collective-permute-start(bf16[2048,128]{1,0:T(8,128)(2,1)S(1)} %get-tuple-element.44), channel_id=1, source_target_pairs={{0,1},{1,0},{2,3},{3,2},{4,5},{5,4},{6,7},{7,6},{8,9},{9,8},{10,11... | collective-permute-start | bytes 1572872 | tf_op jit(solution)/shard_map/ppermute | solution.py:234
  35.3 3.1 %collective-permute-start.1 = (bf16[2048,128]{1,0:T(8,128)(2,1)S(1)}, bf16[2048,128]{1,0:T(8,128)(2,1)S(1)}, u32[]{:S(2)}, u32[]{:S(2)}) collective-permute-start(bf16[2048,128]{1,0:T(8,128)(2,1)S(1)} %get-tuple-element.46), channel_id=1, source_target_pairs={{0,2},{1,3},{2,0},{3,1},{4,6},{5,7},{6,4},{7,5},{8,10},{9,11},{10,... | collective-permute-start | bytes 1572872 | tf_op jit(solution)/shard_map/ppermute | solution.py:234
  38.4 0.0 copy-done.8
  38.4 2.2 %collective-permute-start.4 = (bf16[128,512]{1,0:T(8,128)(2,1)S(1)}, bf16[128,512]{1,0:T(8,128)(2,1)S(1)}, u32[]{:S(2)}, u32[]{:S(2)}) collective-permute-start(bf16[128,512]{1,0:T(8,128)(2,1)S(1)} %copy-done.8), channel_id=1, source_target_pairs={{0,2},{1,3},{2,0},{3,1},{4,6},{5,7},{6,4},{7,5},{8,10},{9,11},{10,... | collective-permute-start | bytes 393224 | tf_op jit(solution)/shard_map/ppermute | solution.py:234
  40.6 3.0 %collective-permute-start.3 = (bf16[128,512]{1,0:T(8,128)(2,1)S(1)}, bf16[128,512]{1,0:T(8,128)(2,1)S(1)}, u32[]{:S(2)}, u32[]{:S(2)}) collective-permute-start(bf16[128,512]{1,0:T(8,128)(2,1)S(1)} %copy-done.8), channel_id=1, source_target_pairs={{0,1},{1,0},{2,3},{3,2},{4,5},{5,4},{6,7},{7,6},{8,9},{9,8},{10,11... | collective-permute-start | bytes 393224 | tf_op jit(solution)/shard_map/ppermute | solution.py:234
  43.6 13.4 %collective-permute-done.2.refs_3_ = bf16[2048,128]{1,0:T(8,128)(2,1)S(1)} collective-permute-done((bf16[2048,128]{1,0:T(8,128)(2,1)S(1)}, bf16[2048,128]{1,0:T(8,128)(2,1)S(1)}, u32[]{:S(2)}, u32[]{:S(2)}) %collective-permute-start.2) | collective-permute-done | bytes 524320 | tf_op jit(solution)/shard_map/ppermute | solution.py:234
  57.0 3.1 %collective-permute-start.5 = (bf16[128,512]{1,0:T(8,128)(2,1)S(1)}, bf16[128,512]{1,0:T(8,128)(2,1)S(1)}, u32[]{:S(2)}, u32[]{:S(2)}) collective-permute-start(bf16[128,512]{1,0:T(8,128)(2,1)S(1)} %copy-done.8), channel_id=1, source_target_pairs={{0,3},{1,2},{2,1},{3,0},{4,7},{5,6},{6,5},{7,4},{8,11},{9,10},{10,... | collective-permute-start | bytes 393224 | tf_op jit(solution)/shard_map/ppermute | solution.py:234
  60.1 0.0 collective-permute-done.refs_1_
  60.1 18.0 %collective-permute-done.1.refs_2_ = bf16[2048,128]{1,0:T(8,128)(2,1)S(1)} collective-permute-done((bf16[2048,128]{1,0:T(8,128)(2,1)S(1)}, bf16[2048,128]{1,0:T(8,128)(2,1)S(1)}, u32[]{:S(2)}, u32[]{:S(2)}) %collective-permute-start.1) | collective-permute-done | bytes 524320 | tf_op jit(solution)/shard_map/ppermute | solution.py:234
  78.1 0.0 copy-done.19
  78.1 0.0 copy-done.20
  78.1 0.0 copy-done.21
  78.1 3.4 %prepare.1 = (f32[2048,128]{1,0:T(8,128)S(1)}, f32[2048,128]{1,0:T(8,128)S(1)}, f32[2048,128]{1,0:T(8,128)S(1)}, f32[2048,128]{1,0:T(8,128)S(1)}, f32[128,128]{1...) custom-call(f32[128,128]{1,0:T(8,128)S(1)} %copy-done.19, f32[128,128]{1,0:T(8,128)S(1)} %copy-done.20, ...), custom_call_target="tpu_custom_call" | custom-call | flops 2097152 | bytes 10780672 | tf_op jit(solution)/shard_map/prepare/pallas_call | solution.py:192
  81.6 0.0 copy-start
  81.6 2.0 %copy-done = f32[8192,128]{1,0:T(8,128)} copy-done((f32[8192,128]{1,0:T(8,128)}, f32[8192,128]{1,0:T(8,128)S(1)}, u32[]{:S(2)}) %copy-start) | copy-done | bytes 4194328
  83.5 0.0 copy-start.2
  83.5 1.0 copy-done.2
  84.5 0.0 copy-start.4
  84.5 1.0 copy-done.4
  85.5 0.0 copy-start.6
  85.5 1.0 copy-done.6
  86.5 0.0 copy-start.15
  86.5 0.6 copy-done.15
  87.1 0.0 copy-start.17
  87.1 0.6 copy-done.17
  87.7 0.0 collective-permute-done.4.refs_6_
  87.7 0.0 copy-start.9
  87.7 0.6 copy-done.9
  88.4 0.0 collective-permute-done.3.refs_5_
  88.4 0.7 copy-done.11
  89.0 0.0 collective-permute-done.5.refs_7_
  89.1 0.7 copy-done.13
  89.7 0.0 all-to-all-done
  89.7 2.2 %copy-done.1 = f32[8192,128]{1,0:T(8,128)S(1)} copy-done((f32[8192,128]{1,0:T(8,128)S(1)}, f32[8192,128]{1,0:T(8,128)}, u32[]{:S(2)}) %copy-start.1) | copy-done | bytes 4194328
  91.9 0.8 copy-done.16
  92.7 0.8 copy-done.18
  93.6 0.8 copy-done.22
  94.3 0.8 copy-done.23
  95.1 0.8 copy-done.24
  95.9 11.7 %middle.1 = bf16[8192,128]{1,0:T(8,128)(2,1)S(1)} custom-call(bf16[9216,128]{1,0:T(8,128)(2,1)S(1)} %bitcast.6, bf16[128,128]{1,0:T(8,128)(2,1)S(1)} %copy-done.22, f32[128,128]{1,0:T(8,128)S(1)} %copy-done.16, bf16[128,128]{1,0:T(8,128)(2,1)S(1)} %copy-done.23, f32[8192,128]{1,0:T(8,128)S(1)} %copy-done.1, bf16[128,128]{1,0:T(8,128)(2,1)S(1)} %copy-done.24, ...), custom_call_target="tpu_custom_call" | custom-call | flops 805306368 | bytes 8880128 | tf_op jit(solution)/shard_map/middle/pallas_call | solution.py:192
  107.5 0.0 copy-start.3
  107.6 0.0 copy-start.5
  107.6 0.0 copy-start.7
  107.6 0.0 copy-start.10
  107.6 0.0 copy-start.12
  107.6 0.0 copy-start.14
  107.6 0.0 copy-start.25
  107.6 72.2 %all_to_all.10 = bf16[512,16,128]{2,1,0:T(8,128)(2,1)S(1)} all-to-all(bf16[512,16,128]{2,1,0:T(8,128)(2,1)S(1)} %bitcast.8), channel_id=1, replica_groups=mesh['seq'=128,'ch'=4] {'seq','ch'}, dimensions={0} | all-to-all | bytes 4194304 | tf_op jit(solution)/shard_map/all_to_all | solution.py:263
  179.8 0.0 copy-done.3
  179.8 0.0 copy-done.5
  179.8 0.0 copy-done.7
  179.8 0.0 copy-done.10
  179.8 0.0 copy-done.12
  179.8 0.0 copy-done.14
  179.8 0.0 copy-done.25
  179.9 5.4 %last.1 = bf16[2048,512]{1,0:T(8,128)(2,1)} custom-call(bf16[8192,128]{1,0:T(8,128)(2,1)S(1)} %bitcast.7, bf16[64,64]{1,0:T(8,128)(2,1)S(1)} %copy-done.25, f32[2048,128]{1,0:T(8,128)S(1)} %get-tuple-element.35.refs_0_, f32[2048,128]{1,0:T(8,128)S(1)} %copy-done.3, f32[2048,128]{1,0:T(8,128)S(1)} %copy-done.5, f32[2048,128]{1,0:T(8,128)S(1)} %copy-done.7, ...), custom_call_target="tpu_custom_call" | custom-call | flops 1140850688 | bytes 8921088 | tf_op jit(solution)/shard_map/last/pallas_call | solution.py:192
  (8 shorter events, 0.0 us)
Async XLA Ops:
  7.7 82.1 %all-to-all-start = ((bf16[128,72,128]{2,1,0:T(8,128)(2,1)}), bf16[128,72,128]{2,1,0:T(8,128)(2,1)S(1)}, u32[]{:S(2)}, u32[]{:S(2)}) async-start(bf16[128,72,128]{2,1,0:T(8,128)(2,1)} %bitcast.10), calls=%async_computation | async-start | bytes 4718592 | tf_op jit(solution)/shard_map/all_to_all | solution.py:241
  28.5 9.9 %copy-start.8 = (bf16[128,512]{1,0:T(8,128)(2,1)S(1)}, bf16[128,512]{1,0:T(8,128)(2,1)}, u32[]{:S(2)}) copy-start(bf16[128,512]{1,0:T(8,128)(2,1)} %refs_4_) | copy-start | bytes 393220
  28.5 49.6 %copy-start.19 = (f32[128,128]{1,0:T(8,128)S(1)}, f32[128,128]{1,0:T(8,128)}, u32[]{:S(2)}) copy-start(f32[128,128]{1,0:T(8,128)} %kernel_top.1) | copy-start | bytes 196612
  28.5 49.6 %copy-start.20 = (f32[128,128]{1,0:T(8,128)S(1)}, f32[128,128]{1,0:T(8,128)}, u32[]{:S(2)}) copy-start(f32[128,128]{1,0:T(8,128)} %untwist_top.1) | copy-start | bytes 196612
  28.5 49.6 %copy-start.21 = (f32[128,64]{0,1:T(8,128)S(1)}, f32[128,64]{0,1:T(8,128)}, u32[]{:S(2)}) copy-start(f32[128,64]{0,1:T(8,128)} %param.25) | copy-start | bytes 98308
  30.3 26.7 %collective-permute-start.2 = (bf16[2048,128]{1,0:T(8,128)(2,1)S(1)}, bf16[2048,128]{1,0:T(8,128)(2,1)S(1)}, u32[]{:S(2)}, u32[]{:S(2)}) collective-permute-start(bf16[2048,128]{1,0:T(8,128)(2,1)S(1)} %get-tuple-element.43), channel_id=1, source_target_pairs={{0,3},{1,2},{2,1},{3,0},{4,7},{5,6},{6,5},{7,4},{8,11},{9,10},{10,... | collective-permute-start | bytes 1572872 | tf_op jit(solution)/shard_map/ppermute | solution.py:234
  33.4 26.7 %collective-permute-start = (bf16[2048,128]{1,0:T(8,128)(2,1)S(1)}, bf16[2048,128]{1,0:T(8,128)(2,1)S(1)}, u32[]{:S(2)}, u32[]{:S(2)}) collective-permute-start(bf16[2048,128]{1,0:T(8,128)(2,1)S(1)} %get-tuple-element.44), channel_id=1, source_target_pairs={{0,1},{1,0},{2,3},{3,2},{4,5},{5,4},{6,7},{7,6},{8,9},{9,8},{10,11... | collective-permute-start | bytes 1572872 | tf_op jit(solution)/shard_map/ppermute | solution.py:234
  35.3 42.8 %collective-permute-start.1 = (bf16[2048,128]{1,0:T(8,128)(2,1)S(1)}, bf16[2048,128]{1,0:T(8,128)(2,1)S(1)}, u32[]{:S(2)}, u32[]{:S(2)}) collective-permute-start(bf16[2048,128]{1,0:T(8,128)(2,1)S(1)} %get-tuple-element.46), channel_id=1, source_target_pairs={{0,2},{1,3},{2,0},{3,1},{4,6},{5,7},{6,4},{7,5},{8,10},{9,11},{10,... | collective-permute-start | bytes 1572872 | tf_op jit(solution)/shard_map/ppermute | solution.py:234
  38.4 49.4 %collective-permute-start.4 = (bf16[128,512]{1,0:T(8,128)(2,1)S(1)}, bf16[128,512]{1,0:T(8,128)(2,1)S(1)}, u32[]{:S(2)}, u32[]{:S(2)}) collective-permute-start(bf16[128,512]{1,0:T(8,128)(2,1)S(1)} %copy-done.8), channel_id=1, source_target_pairs={{0,2},{1,3},{2,0},{3,1},{4,6},{5,7},{6,4},{7,5},{8,10},{9,11},{10,... | collective-permute-start | bytes 393224 | tf_op jit(solution)/shard_map/ppermute | solution.py:234
  40.6 47.8 %collective-permute-start.3 = (bf16[128,512]{1,0:T(8,128)(2,1)S(1)}, bf16[128,512]{1,0:T(8,128)(2,1)S(1)}, u32[]{:S(2)}, u32[]{:S(2)}) collective-permute-start(bf16[128,512]{1,0:T(8,128)(2,1)S(1)} %copy-done.8), channel_id=1, source_target_pairs={{0,1},{1,0},{2,3},{3,2},{4,5},{5,4},{6,7},{7,6},{8,9},{9,8},{10,11... | collective-permute-start | bytes 393224 | tf_op jit(solution)/shard_map/ppermute | solution.py:234
  57.0 32.0 %collective-permute-start.5 = (bf16[128,512]{1,0:T(8,128)(2,1)S(1)}, bf16[128,512]{1,0:T(8,128)(2,1)S(1)}, u32[]{:S(2)}, u32[]{:S(2)}) collective-permute-start(bf16[128,512]{1,0:T(8,128)(2,1)S(1)} %copy-done.8), channel_id=1, source_target_pairs={{0,3},{1,2},{2,1},{3,0},{4,7},{5,6},{6,5},{7,4},{8,11},{9,10},{10,... | collective-permute-start | bytes 393224 | tf_op jit(solution)/shard_map/ppermute | solution.py:234
  81.6 2.0 %copy-start = (f32[8192,128]{1,0:T(8,128)}, f32[8192,128]{1,0:T(8,128)S(1)}, u32[]{:S(2)}) copy-start(f32[8192,128]{1,0:T(8,128)S(1)} %get-tuple-element.33.untwist_top) | copy-start | bytes 12582916
  83.5 1.0 copy-start.2
  84.5 1.0 copy-start.4
  85.5 1.0 copy-start.6
  86.5 0.6 copy-start.15
  87.1 0.6 copy-start.17
  87.7 0.6 copy-start.9
  88.4 0.7 copy-start.11
  89.1 0.7 copy-start.13
  89.7 2.2 %copy-start.1 = (f32[8192,128]{1,0:T(8,128)S(1)}, f32[8192,128]{1,0:T(8,128)}, u32[]{:S(2)}) copy-start(f32[8192,128]{1,0:T(8,128)} %copy-done) | copy-start | bytes 12582916
  91.9 0.8 copy-start.16
  92.7 0.8 copy-start.18
  93.6 0.8 copy-start.22
  94.3 0.8 copy-start.23
  95.1 0.8 copy-start.24
  107.5 72.3 %copy-start.3 = (f32[2048,128]{1,0:T(8,128)S(1)}, f32[2048,128]{1,0:T(8,128)}, u32[]{:S(2)}) copy-start(f32[2048,128]{1,0:T(8,128)} %copy-done.2) | copy-start | bytes 3145732
  107.6 72.3 %copy-start.5 = (f32[2048,128]{1,0:T(8,128)S(1)}, f32[2048,128]{1,0:T(8,128)}, u32[]{:S(2)}) copy-start(f32[2048,128]{1,0:T(8,128)} %copy-done.4) | copy-start | bytes 3145732
  107.6 72.2 %copy-start.7 = (f32[2048,128]{1,0:T(8,128)S(1)}, f32[2048,128]{1,0:T(8,128)}, u32[]{:S(2)}) copy-start(f32[2048,128]{1,0:T(8,128)} %copy-done.6) | copy-start | bytes 3145732
  107.6 72.2 %copy-start.10 = (bf16[128,512]{1,0:T(8,128)(2,1)S(1)}, bf16[128,512]{1,0:T(8,128)(2,1)}, u32[]{:S(2)}) copy-start(bf16[128,512]{1,0:T(8,128)(2,1)} %copy-done.9) | copy-start | bytes 393220
  107.6 72.2 %copy-start.12 = (bf16[128,512]{1,0:T(8,128)(2,1)S(1)}, bf16[128,512]{1,0:T(8,128)(2,1)}, u32[]{:S(2)}) copy-start(bf16[128,512]{1,0:T(8,128)(2,1)} %copy-done.11) | copy-start | bytes 393220
  107.6 72.2 %copy-start.14 = (bf16[128,512]{1,0:T(8,128)(2,1)S(1)}, bf16[128,512]{1,0:T(8,128)(2,1)}, u32[]{:S(2)}) copy-start(bf16[128,512]{1,0:T(8,128)(2,1)} %copy-done.13) | copy-start | bytes 393220
  107.6 72.2 %copy-start.25 = (bf16[64,64]{1,0:T(8,128)(2,1)S(1)}, bf16[64,64]{1,0:T(8,128)(2,1)}, u32[]{:S(2)}) copy-start(bf16[64,64]{1,0:T(8,128)(2,1)} %inverse_low.1) | copy-start | bytes 24580

commit v3 on v2

v3 whole, which is shorter than its diff:
```python
import functools

import jax
import jax.numpy as jnp
from jax import lax
from jax.experimental import pallas as pl
from jax.experimental.pallas import tpu as pltpu
from jax.sharding import PartitionSpec as P

F32 = jnp.float32
BF16 = jnp.bfloat16
LANES = 128
HALF = 64
PITCH = 72


def iota(shape, axis):
    return lax.broadcasted_iota(jnp.int32, shape, axis)


def dot(left, right):
    return jnp.dot(left, right, preferred_element_type=F32)


def repeat_lanes(matrix, times):
    n = matrix.shape[1]
    shape = (n, n * times)
    pick = (lax.rem(iota(shape, 1), n) == iota(shape, 0)).astype(F32).astype(BF16)
    return dot(matrix, pick)


def column_of_row(row):
    n = row.shape[1]
    square = jnp.broadcast_to(row, (n, n))
    return jnp.sum(jnp.where(iota((n, n), 0) == iota((n, n), 1), square, 0.0), axis=1, keepdims=True)


def trade_halves(one, two):
    low = iota(one.shape, 1) < HALF
    return jnp.where(low, one, pltpu.roll(two, HALF, 1)), jnp.where(low, pltpu.roll(one, HALF, 1), two)


def forward_kernel(low, values, factor_low, twist_low, factor_mid, twist_top, kernel_low, message,
                   held, small, wide, row, twist, rows_f, diag, out, sem_in, sem_out):
    mid = factor_mid.shape[0]
    times = 256 // low
    chunk = mid * low // 4
    place = lax.axis_index("seq")
    loads = [
        pltpu.make_async_copy(values.at[pl.ds(n * chunk, chunk)], held.at[pl.ds(n * chunk, chunk)], sem_in.at[n])
        for n in range(4)
    ]
    fetch_low = pltpu.make_async_copy(factor_low, small, sem_in.at[4])
    others = [
        pltpu.make_async_copy(factor_mid, wide, sem_in.at[5]),
        pltpu.make_async_copy(twist_top.at[pl.ds(place // 8 * 8, 8)], row, sem_in.at[6]),
        pltpu.make_async_copy(twist_low, twist, sem_in.at[7]),
    ]
    fetch_low.start()
    for copy in loads + others:
        copy.start()
    fetch_low.wait()
    tiled = repeat_lanes(small[...], times)
    for t in range(times):
        block = jnp.where(iota(tiled.shape, 1) // low == t, tiled, 0.0)
        diag[t * low:(t + 1) * low, :] = block.astype(BF16)
    for n in range(mid * low // 512):
        if n % 4 == 0:
            loads[n // 4].wait()
        at = n * 512
        both = dot(diag[...], jnp.concatenate([held[at:at + 256, :], held[at + 256:at + 512, :]], axis=1))
        for t in range(2 * times):
            to = (n * 2 * times + t) * PITCH
            side = t // times * LANES
            at = t % times * low
            rows_f[to:to + low, :] = both[at:at + low, side:side + LANES]
    for copy in others:
        copy.wait()
    scaled = column_of_row(row[pl.ds(lax.rem(place, 8), 1), :]) * wide[...].astype(F32)
    profile = kernel_low[...].astype(F32)
    turned = pltpu.roll(profile, HALF, 1)
    stores = []
    for k in range(low):
        matrix = (scaled * twist[k:k + 1, :]).astype(BF16)
        second = dot(matrix, rows_f[pl.ds(k, mid, stride=PITCH), :].astype(BF16))
        halves = trade_halves(second[:HALF], second[HALF:])
        for h, (half, line) in enumerate(zip(halves, (profile, turned))):
            to = (2 * k + h) * PITCH
            out[to:to + HALF, :] = half.astype(BF16)
            out[to + HALF:to + PITCH, :] = jnp.broadcast_to(line[k:k + 1, :], (PITCH - HALF, LANES)).astype(BF16)
        if k % 16 == 15:
            size = 32 * PITCH
            at = k // 16 * size
            store = pltpu.make_async_copy(
                out.at[pl.ds(at, size)], message.at[pl.ds(at, size)], sem_out.at[k // 16]
            )
            store.start()
            stores.append(store)
    for store in stores:
        store.wait()


def middle_kernel(columns, factor_top, kernel_top, inverse_top, scale_top, inverse_mid, untwist_low, third,
                  held, out, rows_f, rows_g, whole, lines, forth, reverse, scale, across, twist, sem, sem_in, sem_out):
    top = forth.shape[0]
    place = lax.axis_index("seq")
    pairs = ((factor_top, forth), (kernel_top, whole), (inverse_top, reverse), (inverse_mid, across),
             (untwist_low.at[pl.ds(place // 16 * 8, 8)], twist))
    copies = [pltpu.make_async_copy(a, b, sem.at[n]) for n, (a, b) in enumerate(pairs)]
    quarter = HALF * top // 4
    scales = [
        pltpu.make_async_copy(
            scale_top.at[pl.ds(n * quarter, quarter)], scale.at[pl.ds(n * quarter, quarter)], sem_in.at[4 + n]
        )
        for n in range(4)
    ]
    size = top // 4 * PITCH
    loads = [
        pltpu.make_async_copy(columns.at[pl.ds(n * size, size)], held.at[pl.ds(n * size, size)], sem_in.at[n])
        for n in range(4)
    ]
    for copy in loads + copies + scales:
        copy.start()
    for n in range(top // 8):
        if n % 4 == 0:
            loads[n // 4].wait()
        at = n * 8 * PITCH
        rows_f[at:at + 8 * PITCH, :] = held[at:at + 8 * PITCH, :].astype(F32)
    rows = rows_f[pl.ds(HALF, 2 * HALF, stride=PITCH), :]
    lines[...] = trade_halves(rows[:HALF], rows[HALF:])[0]
    for copy in copies:
        copy.wait()
    lower = iota((top, LANES), 1) < HALF
    all_top = whole[...]
    turned = pltpu.roll(all_top, HALF, 1)
    keep = lower == (lax.rem(place, 2) == 0)
    whole[...] = jnp.where(keep, all_top, turned)
    scale_low = jnp.broadcast_to(column_of_row(twist[pl.ds(lax.rem(place // 2, 8), 1), :]), (across.shape[0], LANES))

    for r in range(0, HALF, 2):
        if r % 16 == 0:
            scales[r // 16].wait()
        one = rows_f[pl.ds(r, top, stride=PITCH), :].astype(BF16)
        two = rows_f[pl.ds(r + 1, top, stride=PITCH), :].astype(BF16)
        spectrum = dot(forth[...], jnp.concatenate([one, two], axis=1)).astype(BF16).astype(F32)
        first = spectrum[:, :LANES] * whole[...] * lines[r:r + 1, :]
        other = spectrum[:, LANES:] * whole[...] * lines[r + 1:r + 2, :]
        filtered = jnp.concatenate([first.astype(BF16), other.astype(BF16)], axis=1)
        back = dot(reverse[...], filtered)
        rows_g[pl.ds(r, top, stride=PITCH), :] = back[:, :LANES] * scale[r * top:(r + 1) * top, :].astype(F32)
        rows_g[pl.ds(r + 1, top, stride=PITCH), :] = back[:, LANES:] * scale[(r + 1) * top:(r + 2) * top, :].astype(F32)

    part = 32 * HALF
    stores = []
    for n in range(top // 4):
        sides = []
        for m in range(2):
            at = (n * 4 + m * 2) * PITCH
            upper, under = trade_halves(rows_g[at:at + HALF, :], rows_g[at + PITCH:at + PITCH + HALF, :])
            sides.append(jnp.concatenate([upper.astype(BF16), under.astype(BF16)], axis=0))
        result = dot(across[...], jnp.concatenate(sides, axis=1))
        for m in range(2):
            side = result[:, m * LANES:(m + 1) * LANES] * scale_low
            for q in range(4):
                pair = trade_halves(side[q * 32:q * 32 + 16], side[q * 32 + 16:q * 32 + 32])
                for p in range(2):
                    to = (n * 4 + m * 2 + p) * HALF + q * 16
                    out[to:to + 16, :] = pair[p].astype(BF16)
        if n % 8 == 7:
            at = n // 8 * part
            store = pltpu.make_async_copy(out.at[pl.ds(at, part)], third.at[pl.ds(at, part)], sem_out.at[n // 8])
            store.start()
            stores.append(store)
    for store in stores:
        store.wait()


def spread_kernel(untwist_top, scale_top):
    top = untwist_top.shape[0]
    shape = (top, LANES)
    lower = iota(shape, 1) < HALF
    for r in range(HALF):
        one = jnp.broadcast_to(untwist_top[:, r:r + 1], shape)
        two = jnp.broadcast_to(untwist_top[:, HALF + r:HALF + r + 1], shape)
        scale_top[r * top:(r + 1) * top, :] = jnp.where(lower, one, two).astype(BF16)


def silu_kernel(*refs):
    sources, target = refs[:-1], refs[-1]
    for t, source in enumerate(sources):
        def body(n, _):
            at = pl.multiple_of(n * 256, 256)
            value = source[pl.ds(at, 256), :].astype(F32)
            target[t, pl.ds(at, 256), :] = ((0.5 * value) * (1.0 + jnp.tanh(0.5 * value))).astype(BF16)
            return 0

        lax.fori_loop(0, source.shape[0] // 256, body, 0)


def last_kernel(low, third, inverse_low, silu, *refs):
    weights, out = refs[:4], refs[4]
    held, small, gates, matrix, rows_f, gated, result, sem, sem_in, sem_gate, sem_out = refs[5:]
    pitch = LANES + 8
    block = 4 * low
    place = lax.axis_index("ch")
    part = low * LANES // 4
    loads = [
        pltpu.make_async_copy(third.at[pl.ds(n * part, part)], held.at[pl.ds(n * part, part)], sem_in.at[n])
        for n in range(4)
    ]
    fetch_low = pltpu.make_async_copy(inverse_low, small, sem.at[4])
    fetch_gates = [
        pltpu.make_async_copy(
            silu.at[:, pl.ds(at, block)], gates.at[:, pl.ds(at, block)], sem_gate.at[n]
        )
        for n, at in enumerate((p * 4 + g) * block for g in range(4) for p in range(2))
    ]
    fetch_weights = [pltpu.make_async_copy(w, matrix.at[pl.ds(t * LANES, LANES)], sem.at[t]) for t, w in enumerate(weights)]
    for copy in loads + [fetch_low] + fetch_gates[:2] + fetch_weights + fetch_gates[2:]:
        copy.start()
    for n in range(4):
        loads[n].wait()
        for k in range(n * low // 4, (n + 1) * low // 4):
            for h in range(2):
                for t in range(4):
                    source = pl.multiple_of(((k * 2 + h) * 4 + (place ^ t)) * 16, 16)
                    to = k * pitch + (h * 4 + t) * 16
                    rows_f[to:to + 16, :] = held[pl.ds(source, 16), :].astype(F32)
    fetch_low.wait()
    copies = []
    for g in range(4):
        for p in range(2):
            fetch_gates[2 * g + p].wait()
        for b in range(4 * g, 4 * g + 4):
            for t in range(4):
                one = rows_f[pl.ds(t * 16 + b, low, stride=pitch), :]
                two = rows_f[pl.ds((4 + t) * 16 + b, low, stride=pitch), :]
                pair = trade_halves(one, two)
                mixed = dot(small[...], jnp.concatenate([p.astype(BF16) for p in pair], axis=1))
                for p in range(2):
                    at = (p * 16 + b) * low
                    gated[at:at + low, t * LANES:(t + 1) * LANES] = (
                        mixed[:, p * LANES:(p + 1) * LANES] * gates[t, at:at + low, :].astype(F32)
                    ).astype(BF16)
        if g == 0:
            for copy in fetch_weights:
                copy.wait()
        for p in range(2):
            at = (p * 4 + g) * block
            result[at:at + block, :] = dot(gated[at:at + block, :], matrix[...]).astype(BF16)
            copy = pltpu.make_async_copy(
                result.at[pl.ds(at, block)], out.at[pl.ds(at, block)], sem_out.at[g * 2 + p]
            )
            copy.start()
            copies.append(copy)
    for copy in copies:
        copy.wait()


def call(kernel, name, out_shape, scratch, flops, *args, limit=40 << 20, far=(), out_spec=None):
    vmem, hbm = pl.BlockSpec(memory_space=pltpu.VMEM), pl.BlockSpec(memory_space=pl.ANY)
    outs = jax.tree.leaves(out_shape)
    moved = sum(a.size * a.dtype.itemsize for a in args) + sum(o.size * o.dtype.itemsize for o in outs)
    return pl.pallas_call(
        kernel,
        name=name,
        out_shape=out_shape,
        in_specs=[hbm if n in far else vmem for n in range(len(args))],
        out_specs=jax.tree.map(lambda _: out_spec or vmem, out_shape),
        scratch_shapes=scratch,
        compiler_params=pltpu.CompilerParams(vmem_limit_bytes=limit),
        cost_estimate=pl.CostEstimate(flops=flops, bytes_accessed=moved, transcendentals=0),
    )(*args)


def local(
    values,
    factor_low,
    twist_low,
    factor_mid,
    twist_top,
    factor_top,
    kernel_top,
    kernel_low,
    inverse_top,
    untwist_top,
    inverse_mid,
    untwist_low,
    inverse_low,
    out_weight,
):
    low = factor_low.shape[0]
    mid = factor_mid.shape[0]
    top = factor_top.shape[0]
    rows, width = values.shape
    ch_place = lax.axis_index("ch")
    ch_count = lax.axis_size("ch")
    share = rows // ch_count
    columns_out = out_weight.shape[1]
    unit = 2 * rows * width
    padded = pltpu.VMEM((top * PITCH, width), F32)

    def swap(array, turn):
        if turn == 0:
            return array
        return lax.ppermute(array, "ch", [(c, c ^ turn) for c in range(ch_count)])

    message = call(
        functools.partial(forward_kernel, low), "forward", jax.ShapeDtypeStruct((2 * low * PITCH, width), BF16),
        [
            pltpu.VMEM((rows, width), BF16),
            pltpu.VMEM((low, low), BF16),
            pltpu.VMEM((mid, mid), BF16),
            pltpu.VMEM((8, mid), F32),
            pltpu.VMEM((low, mid), F32),
            padded,
            pltpu.VMEM((256, 256), BF16),
            pltpu.VMEM((2 * low * PITCH, width), BF16),
            pltpu.SemaphoreType.DMA((8,)),
            pltpu.SemaphoreType.DMA((4,)),
        ], unit * (low + mid),
        values, factor_low, twist_low.T, factor_mid, twist_top, kernel_low,
        limit=60 << 20, far=range(5), out_spec=pl.BlockSpec(memory_space=pl.ANY),
    )
    columns = lax.all_to_all(message.reshape(2 * low, PITCH, width), "seq", 0, 0, tiled=True)

    turns = range(ch_count)
    shares = [
        swap(lax.dynamic_slice_in_dim(values, (ch_place ^ turn) * share, share, 0), turn) for turn in turns
    ]
    scale_top = call(
        spread_kernel, "spread", jax.ShapeDtypeStruct((HALF * top, width), BF16), [], unit, untwist_top,
        limit=60 << 20,
    )
    columns, shares, scale_top = lax.optimization_barrier((columns, shares, scale_top))
    third = call(
        middle_kernel, "middle", jax.ShapeDtypeStruct((rows, width), BF16),
        [
            pltpu.VMEM((top * PITCH, width), BF16),
            pltpu.VMEM((rows, width), BF16),
            padded,
            padded,
            pltpu.VMEM((top, width), F32),
            pltpu.VMEM((HALF, width), F32),
            pltpu.VMEM((top, top), BF16),
            pltpu.VMEM((top, top), BF16),
            pltpu.VMEM((HALF * top, width), BF16),
            pltpu.VMEM((mid, mid), BF16),
            pltpu.VMEM((8, mid), F32),
            pltpu.SemaphoreType.DMA((5,)),
            pltpu.SemaphoreType.DMA((8,)),
            pltpu.SemaphoreType.DMA((4,)),
        ], unit * (2 * top + mid),
        columns.reshape(top * PITCH, width), factor_top, kernel_top, inverse_top, scale_top, inverse_mid,
        untwist_low.T, limit=60 << 20, far=range(7), out_spec=pl.BlockSpec(memory_space=pl.ANY),
    )
    third, shares, out_weight = lax.optimization_barrier((third, shares, out_weight))
    weights = [swap(out_weight, turn) for turn in turns]
    silu = call(
        silu_kernel, "silu", jax.ShapeDtypeStruct((ch_count, share, width), BF16), [], unit, *shares, limit=60 << 20
    )
    third = lax.all_to_all(third.reshape(top * ch_count, -1, width), ("seq", "ch"), 0, 0, tiled=True)
    return call(
        functools.partial(last_kernel, low), "last", jax.ShapeDtypeStruct((share, columns_out), BF16),
        [
            pltpu.VMEM((rows, width), BF16),
            pltpu.VMEM((low, low), BF16),
            pltpu.VMEM((ch_count, share, width), BF16),
            pltpu.VMEM((ch_count * width, columns_out), BF16),
            pltpu.VMEM((low * (width + 8), width), F32),
            pltpu.VMEM((share, columns_out), BF16),
            pltpu.VMEM((share, columns_out), BF16),
            pltpu.SemaphoreType.DMA((5,)),
            pltpu.SemaphoreType.DMA((4,)),
            pltpu.SemaphoreType.DMA((8,)),
            pltpu.SemaphoreType.DMA((8,)),
        ],
        unit * low // 2 + 2 * share * columns_out ** 2,
        third.reshape(rows, width), inverse_low, silu, *weights,
        limit=60 << 20, far=range(3 + ch_count), out_spec=pl.BlockSpec(memory_space=pl.ANY),
    )


def solution(mesh):
    return jax.shard_map(
        local,
        mesh=mesh,
        in_specs=(
            P("seq", "ch"),
            P(),
            P(),
            P(),
            P(),
            P(),
            P(None, "ch"),
            P("seq", "ch"),
            P(),
            P(),
            P(),
            P(),
            P(),
            P("ch", None),
        ),
        out_specs=P(("seq", "ch"), None),
        check_vma=False,
    )
```

time: 186 us -> 168 us (0.903)
  blocking collectives: 72.2 us -> 0 us
  waiting for transfers between devices: 31.4 us -> 82.9 us
  starting transfers between devices: 37.1 us -> 52.3 us
  local copies, waits for them, and re-layouts: 16.1 us -> 5.49 us
  Pallas kernels: 28.2 us -> 26.3 us
    all_to_all x1 -> x0, blocking collectives: 72.2 us -> none  [local(): lax.all_to_all(third.reshape(top * ch_count, -1, width), ('seq', 'ch'), 0...]
    all_to_all x0 -> x1, waiting for transfers between devices: none -> 32.4 us  [local(): lax.all_to_all(third.reshape(top * ch_count, -1, width), ('seq', 'ch'), 0...]
    ppermute x6, waiting for transfers between devices: 31.4 us -> 44.8 us  [swap(): return lax.ppermute(array, 'ch', [(c, c ^ turn) for c in range(ch_count)])]
    unnamed x52 -> x14, local copies, waits for them, and re-layouts: 14.3 us -> 2.77 us
    all_to_all x0 -> x1, starting transfers between devices: none -> 11.4 us  [local(): lax.all_to_all(third.reshape(top * ch_count, -1, width), ('seq', 'ch'), 0...]
    all_to_all x1, waiting for transfers between devices: 0.01 us -> 5.69 us  [local(): lax.all_to_all(message.reshape(2 * low, PITCH, width), 'seq', 0, 0, tiled...]
    ppermute x6, starting transfers between devices: 16.3 us -> 20 us  [swap(): return lax.ppermute(array, 'ch', [(c, c ^ turn) for c in range(ch_count)])]
    pallas_call x4 -> x5, Pallas kernels: 28.2 us -> 26.3 us  [call(): pl.pallas_call(kernel, name=name, out_shape=out_shape, in_specs=[hbm if n...]
  transfers between devices with their start and end apart: 7 -> 8, of which waited for: 2 -> 5; matrix products, arithmetic and copies ran while one was open for 1% -> 2% of each run, Pallas kernels for 2% -> 4%
where the time goes in v3:
time: 168 us; the launch traced here: 167 us
  waiting for transfers between devices  82.9 us (49%)
  starting transfers between devices  52.3 us (31%)
  Pallas kernels  26.3 us (16%)
  local copies, waits for them, and re-layouts  5.49 us (3%)
    ppermute x6, waiting for transfers between devices, swap(): return lax.ppermute(array, 'ch', [(c, c ^ turn) for c in range(ch_count)])  44.8 us
    all_to_all x1, waiting for transfers between devices, local(): lax.all_to_all(third.reshape(top * ch_count, -1, width), ('seq', 'ch'), 0...  32.4 us
    pallas_call x5, Pallas kernels, call(): pl.pallas_call(kernel, name=name, out_shape=out_shape, in_specs=[hbm if n...  26.3 us
    all_to_all x1, starting transfers between devices, local(): lax.all_to_all(message.reshape(2 * low, PITCH, width), 'seq', 0, 0, tiled...  20.8 us
    ppermute x6, starting transfers between devices, swap(): return lax.ppermute(array, 'ch', [(c, c ^ turn) for c in range(ch_count)])  20 us
    all_to_all x1, starting transfers between devices, local(): lax.all_to_all(third.reshape(top * ch_count, -1, width), ('seq', 'ch'), 0...  11.4 us
    all_to_all x1, waiting for transfers between devices, local(): lax.all_to_all(message.reshape(2 * low, PITCH, width), 'seq', 0, 0, tiled...  5.69 us
  transfers between devices with their start and end apart: 8, of which 5 were waited for; matrix products, arithmetic and copies ran while one was open for 2% of the time, Pallas kernels for 4%

profile of v3, /device:TPU:1, one launch (start us, length us, event | category | flops | bytes accessed | tf_op | source)
XLA Modules:
  0.0 167.2 jit_solution(6262519830123354217)
XLA Ops:
  0.0 5.4 %forward.1 = bf16[9216,128]{1,0:T(8,128)(2,1)} custom-call(bf16[8192,128]{1,0:T(8,128)(2,1)} %values.1, bf16[64,64]{1,0:T(8,128)(2,1)} %factor_low.1, f32[64,128]{1,0:T(8,128)} %bitcast.10, bf16[128,128]{1,0:T(8,128)(2,1)} %factor_mid.1, f32[128,128]{1,0:T(8,128)} %twist_top.1, bf16[64,128]{1,0:T(8,128)(2,1)} %kernel_low.1), custom_call_target="tpu_custom_call" | custom-call | flops 402653184 | bytes 4612096 | tf_op jit(solution)/shard_map/forward/pallas_call | solution.py:264
  5.4 20.8 %all-to-all-start = ((bf16[128,72,128]{2,1,0:T(8,128)(2,1)}), bf16[128,72,128]{2,1,0:T(8,128)(2,1)S(1)}, u32[]{:S(2)}, u32[]{:S(2)}) async-start(bf16[128,72,128]{2,1,0:T(8,128)(2,1)} %bitcast.7), calls=%async_computation | async-start | bytes 4718592 | tf_op jit(solution)/shard_map/all_to_all | solution.py:325
  26.3 2.7 %constant_dynamic-slice_fusion = (bf16[2048,128]{1,0:T(8,128)(2,1)S(1)}, bf16[2048,128]{1,0:T(8,128)(2,1)}, bf16[2048,128]{1,0:T(8,128)(2,1)}, bf16[2048,128]{1,0:T(8,128)(2,1)}) fusion(bf16[8192,128]{1,0:T(8,128)(2,1)} %values.1, s32[]{:T(128)S(6)} %select_n.15, s32[]{:T(128)S(6)} %select_n.13, s32[]{:T(128)S(6)} %select_n.12, s32[]{:T(128)S(6)} %select_n.14), kind=kLoop, calls=%fused_computation | loop fusion | bytes 4194320 | tf_op jit(solution)/shard_map/dynamic_slice | solution.py:329
  29.0 2.9 %collective-permute-start = (bf16[2048,128]{1,0:T(8,128)(2,1)}, bf16[2048,128]{1,0:T(8,128)(2,1)S(1)}, u32[]{:S(2)}, u32[]{:S(2)}) collective-permute-start(bf16[2048,128]{1,0:T(8,128)(2,1)} %get-tuple-element.30), channel_id=1, source_target_pairs={{0,1},{1,0},{2,3},{3,2},{4,5},{5,4},{6,7},{7,6},{8,9},{9,8},{10,11... | collective-permute-start | bytes 1572872 | tf_op jit(solution)/shard_map/ppermute | solution.py:306
  31.9 2.2 %collective-permute-start.1 = (bf16[2048,128]{1,0:T(8,128)(2,1)}, bf16[2048,128]{1,0:T(8,128)(2,1)S(1)}, u32[]{:S(2)}, u32[]{:S(2)}) collective-permute-start(bf16[2048,128]{1,0:T(8,128)(2,1)} %get-tuple-element.32), channel_id=1, source_target_pairs={{0,2},{1,3},{2,0},{3,1},{4,6},{5,7},{6,4},{7,5},{8,10},{9,11},{10,... | collective-permute-start | bytes 1572872 | tf_op jit(solution)/shard_map/ppermute | solution.py:306
  34.1 3.2 %collective-permute-start.2 = (bf16[2048,128]{1,0:T(8,128)(2,1)S(1)}, bf16[2048,128]{1,0:T(8,128)(2,1)}, u32[]{:S(2)}, u32[]{:S(2)}) collective-permute-start(bf16[2048,128]{1,0:T(8,128)(2,1)S(1)} %get-tuple-element.29), channel_id=1, source_target_pairs={{0,3},{1,2},{2,1},{3,0},{4,7},{5,6},{6,5},{7,4},{8,11},{9,10},{10,... | collective-permute-start | bytes 1572872 | tf_op jit(solution)/shard_map/ppermute | solution.py:306
  37.3 3.5 %spread.1.scale_top = bf16[8192,128]{1,0:T(8,128)(2,1)} custom-call(f32[128,128]{1,0:T(8,128)} %untwist_top.1), custom_call_target="tpu_custom_call" | custom-call | flops 2097152 | bytes 2162688 | tf_op jit(solution)/shard_map/spread/pallas_call | solution.py:264
  40.8 0.0 collective-permute-done.refs_1_
  40.8 0.0 copy-start.2
  40.9 18.2 %collective-permute-done.1.refs_2_ = bf16[2048,128]{1,0:T(8,128)(2,1)S(1)} collective-permute-done((bf16[2048,128]{1,0:T(8,128)(2,1)}, bf16[2048,128]{1,0:T(8,128)(2,1)S(1)}, u32[]{:S(2)}, u32[]{:S(2)}) %collective-permute-start.1) | collective-permute-done | bytes 524320 | tf_op jit(solution)/shard_map/ppermute | solution.py:306
  59.0 0.0 copy-start.3
  59.0 20.4 %collective-permute-done.2.refs_3_ = bf16[2048,128]{1,0:T(8,128)(2,1)} collective-permute-done((bf16[2048,128]{1,0:T(8,128)(2,1)S(1)}, bf16[2048,128]{1,0:T(8,128)(2,1)}, u32[]{:S(2)}, u32[]{:S(2)}) %collective-permute-start.2) | collective-permute-done | bytes 524320 | tf_op jit(solution)/shard_map/ppermute | solution.py:306
  79.4 5.7 %all-to-all-done = bf16[128,72,128]{2,1,0:T(8,128)(2,1)S(1)} async-done(((bf16[128,72,128]{2,1,0:T(8,128)(2,1)}), bf16[128,72,128]{2,1,0:T(8,128)(2,1)S(1)}, u32[]{:S(2)}, u32[]{:S(2)}) %all-to-all-start) | async-done | bytes 2359328 | tf_op jit(solution)/shard_map/all_to_all | solution.py:325
  85.1 0.0 copy-start
  85.1 1.4 copy-done
  86.5 6.7 %middle.1 = bf16[8192,128]{1,0:T(8,128)(2,1)} custom-call(bf16[9216,128]{1,0:T(8,128)(2,1)} %bitcast.6, bf16[128,128]{1,0:T(8,128)(2,1)} %factor_top.1, f32[128,128]{1,0:T(8,128)} %kernel_top.1, bf16[128,128]{1,0:T(8,128)(2,1)} %inverse_top.1, bf16[8192,128]{1,0:T(8,128)(2,1)} %spread.1.scale_top, bf16[128,128]{1,0:T(8,128)(2,1)} %inverse_mid.1, ...), custom_call_target="tpu_custom_call" | custom-call | flops 805306368 | bytes 6750208 | tf_op jit(solution)/shard_map/middle/pallas_call | solution.py:264
  93.2 0.0 copy-start.4
  93.2 11.4 %all-to-all-start.1 = ((bf16[512,16,128]{2,1,0:T(8,128)(2,1)}), bf16[512,16,128]{2,1,0:T(8,128)(2,1)S(1)}, u32[]{:S(2)}, u32[]{:S(2)}) async-start(bf16[512,16,128]{2,1,0:T(8,128)(2,1)} %bitcast.8), calls=%async_computation.1 | async-start | bytes 4194304 | tf_op jit(solution)/shard_map/all_to_all | solution.py:362
  104.6 0.0 copy-done.4
  104.7 6.2 %collective-permute-start.3 = (bf16[128,512]{1,0:T(8,128)(2,1)S(1)}, bf16[128,512]{1,0:T(8,128)(2,1)S(1)}, u32[]{:S(2)}, u32[]{:S(2)}) collective-permute-start(bf16[128,512]{1,0:T(8,128)(2,1)S(1)} %copy-done.4), channel_id=1, source_target_pairs={{0,1},{1,0},{2,3},{3,2},{4,5},{5,4},{6,7},{7,6},{8,9},{9,8},{10,11... | collective-permute-start | bytes 393224 | tf_op jit(solution)/shard_map/ppermute | solution.py:306
  110.9 1.9 %collective-permute-start.4 = (bf16[128,512]{1,0:T(8,128)(2,1)S(1)}, bf16[128,512]{1,0:T(8,128)(2,1)S(1)}, u32[]{:S(2)}, u32[]{:S(2)}) collective-permute-start(bf16[128,512]{1,0:T(8,128)(2,1)S(1)} %copy-done.4), channel_id=1, source_target_pairs={{0,2},{1,3},{2,0},{3,1},{4,6},{5,7},{6,4},{7,5},{8,10},{9,11},{10,... | collective-permute-start | bytes 393224 | tf_op jit(solution)/shard_map/ppermute | solution.py:306
  112.8 3.5 %collective-permute-start.5 = (bf16[128,512]{1,0:T(8,128)(2,1)S(1)}, bf16[128,512]{1,0:T(8,128)(2,1)}, u32[]{:S(2)}, u32[]{:S(2)}) collective-permute-start(bf16[128,512]{1,0:T(8,128)(2,1)S(1)} %copy-done.4), channel_id=1, source_target_pairs={{0,3},{1,2},{2,1},{3,0},{4,7},{5,6},{6,5},{7,4},{8,11},{9,10},{10,... | collective-permute-start | bytes 393224 | tf_op jit(solution)/shard_map/ppermute | solution.py:306
  116.4 0.0 copy-done.2
  116.4 0.0 copy-done.3
  116.4 3.9 %silu.1 = bf16[4,2048,128]{2,1,0:T(8,128)(2,1)} custom-call(bf16[2048,128]{1,0:T(8,128)(2,1)} %get-tuple-element.24.refs_0_, bf16[2048,128]{1,0:T(8,128)(2,1)} %copy-done.2, bf16[2048,128]{1,0:T(8,128)(2,1)} %copy-done.3, bf16[2048,128]{1,0:T(8,128)(2,1)} %collective-permute-done.2.refs_3_), custom_call_target="tpu_custom_call" | custom-call | flops 2097152 | bytes 4194304 | tf_op jit(solution)/shard_map/silu/pallas_call | solution.py:264
  120.2 0.0 collective-permute-done.3.refs_1_
  120.2 0.0 copy-start.5
  120.2 0.0 collective-permute-done.4.refs_2_
  120.2 0.0 copy-start.6
  120.3 6.3 %collective-permute-done.5.refs_3_ = bf16[128,512]{1,0:T(8,128)(2,1)} collective-permute-done((bf16[128,512]{1,0:T(8,128)(2,1)S(1)}, bf16[128,512]{1,0:T(8,128)(2,1)}, u32[]{:S(2)}, u32[]{:S(2)}) %collective-permute-start.5) | collective-permute-done | bytes 131104 | tf_op jit(solution)/shard_map/ppermute | solution.py:306
  126.5 32.4 %all-to-all-done.1 = bf16[512,16,128]{2,1,0:T(8,128)(2,1)S(1)} async-done(((bf16[512,16,128]{2,1,0:T(8,128)(2,1)}), bf16[512,16,128]{2,1,0:T(8,128)(2,1)S(1)}, u32[]{:S(2)}, u32[]{:S(2)}) %all-to-all-start.1) | async-done | bytes 2097184 | tf_op jit(solution)/shard_map/all_to_all | solution.py:362
  158.9 0.0 copy-start.1
  158.9 0.0 copy-done.5
  158.9 0.0 copy-done.6
  158.9 1.3 copy-done.1
  160.2 6.8 %last.1 = bf16[2048,512]{1,0:T(8,128)(2,1)} custom-call(bf16[8192,128]{1,0:T(8,128)(2,1)} %bitcast.9, bf16[64,64]{1,0:T(8,128)(2,1)} %inverse_low.1, bf16[4,2048,128]{2,1,0:T(8,128)(2,1)} %silu.1, bf16[128,512]{1,0:T(8,128)(2,1)} %refs_0_, bf16[128,512]{1,0:T(8,128)(2,1)} %copy-done.5, bf16[128,512]{1,0:T(8,128)(2,1)} %copy-done.6, ...), custom_call_target="tpu_custom_call" | custom-call | flops 1140850688 | bytes 6823936 | tf_op jit(solution)/shard_map/last/pallas_call | solution.py:264
Async XLA Ops:
  5.4 79.6 %all-to-all-start = ((bf16[128,72,128]{2,1,0:T(8,128)(2,1)}), bf16[128,72,128]{2,1,0:T(8,128)(2,1)S(1)}, u32[]{:S(2)}, u32[]{:S(2)}) async-start(bf16[128,72,128]{2,1,0:T(8,128)(2,1)} %bitcast.7), calls=%async_computation | async-start | bytes 4718592 | tf_op jit(solution)/shard_map/all_to_all | solution.py:325
  29.0 11.8 %collective-permute-start = (bf16[2048,128]{1,0:T(8,128)(2,1)}, bf16[2048,128]{1,0:T(8,128)(2,1)S(1)}, u32[]{:S(2)}, u32[]{:S(2)}) collective-permute-start(bf16[2048,128]{1,0:T(8,128)(2,1)} %get-tuple-element.30), channel_id=1, source_target_pairs={{0,1},{1,0},{2,3},{3,2},{4,5},{5,4},{6,7},{7,6},{8,9},{9,8},{10,11... | collective-permute-start | bytes 1572872 | tf_op jit(solution)/shard_map/ppermute | solution.py:306
  31.9 27.2 %collective-permute-start.1 = (bf16[2048,128]{1,0:T(8,128)(2,1)}, bf16[2048,128]{1,0:T(8,128)(2,1)S(1)}, u32[]{:S(2)}, u32[]{:S(2)}) collective-permute-start(bf16[2048,128]{1,0:T(8,128)(2,1)} %get-tuple-element.32), channel_id=1, source_target_pairs={{0,2},{1,3},{2,0},{3,1},{4,6},{5,7},{6,4},{7,5},{8,10},{9,11},{10,... | collective-permute-start | bytes 1572872 | tf_op jit(solution)/shard_map/ppermute | solution.py:306
  34.1 45.3 %collective-permute-start.2 = (bf16[2048,128]{1,0:T(8,128)(2,1)S(1)}, bf16[2048,128]{1,0:T(8,128)(2,1)}, u32[]{:S(2)}, u32[]{:S(2)}) collective-permute-start(bf16[2048,128]{1,0:T(8,128)(2,1)S(1)} %get-tuple-element.29), channel_id=1, source_target_pairs={{0,3},{1,2},{2,1},{3,0},{4,7},{5,6},{6,5},{7,4},{8,11},{9,10},{10,... | collective-permute-start | bytes 1572872 | tf_op jit(solution)/shard_map/ppermute | solution.py:306
  40.8 75.5 %copy-start.2 = (bf16[2048,128]{1,0:T(8,128)(2,1)}, bf16[2048,128]{1,0:T(8,128)(2,1)S(1)}, u32[]{:S(2)}) copy-start(bf16[2048,128]{1,0:T(8,128)(2,1)S(1)} %collective-permute-done.refs_1_) | copy-start | bytes 1572868
  59.0 57.3 %copy-start.3 = (bf16[2048,128]{1,0:T(8,128)(2,1)}, bf16[2048,128]{1,0:T(8,128)(2,1)S(1)}, u32[]{:S(2)}) copy-start(bf16[2048,128]{1,0:T(8,128)(2,1)S(1)} %collective-permute-done.1.refs_2_) | copy-start | bytes 1572868
  85.1 1.4 copy-start
  93.2 11.5 %copy-start.4 = (bf16[128,512]{1,0:T(8,128)(2,1)S(1)}, bf16[128,512]{1,0:T(8,128)(2,1)}, u32[]{:S(2)}) copy-start(bf16[128,512]{1,0:T(8,128)(2,1)} %refs_0_) | copy-start | bytes 393220
  93.2 65.7 %all-to-all-start.1 = ((bf16[512,16,128]{2,1,0:T(8,128)(2,1)}), bf16[512,16,128]{2,1,0:T(8,128)(2,1)S(1)}, u32[]{:S(2)}, u32[]{:S(2)}) async-start(bf16[512,16,128]{2,1,0:T(8,128)(2,1)} %bitcast.8), calls=%async_computation.1 | async-start | bytes 4194304 | tf_op jit(solution)/shard_map/all_to_all | solution.py:362
  104.7 15.6 %collective-permute-start.3 = (bf16[128,512]{1,0:T(8,128)(2,1)S(1)}, bf16[128,512]{1,0:T(8,128)(2,1)S(1)}, u32[]{:S(2)}, u32[]{:S(2)}) collective-permute-start(bf16[128,512]{1,0:T(8,128)(2,1)S(1)} %copy-done.4), channel_id=1, source_target_pairs={{0,1},{1,0},{2,3},{3,2},{4,5},{5,4},{6,7},{7,6},{8,9},{9,8},{10,11... | collective-permute-start | bytes 393224 | tf_op jit(solution)/shard_map/ppermute | solution.py:306
  110.9 9.4 %collective-permute-start.4 = (bf16[128,512]{1,0:T(8,128)(2,1)S(1)}, bf16[128,512]{1,0:T(8,128)(2,1)S(1)}, u32[]{:S(2)}, u32[]{:S(2)}) collective-permute-start(bf16[128,512]{1,0:T(8,128)(2,1)S(1)} %copy-done.4), channel_id=1, source_target_pairs={{0,2},{1,3},{2,0},{3,1},{4,6},{5,7},{6,4},{7,5},{8,10},{9,11},{10,... | collective-permute-start | bytes 393224 | tf_op jit(solution)/shard_map/ppermute | solution.py:306
  112.8 13.7 %collective-permute-start.5 = (bf16[128,512]{1,0:T(8,128)(2,1)S(1)}, bf16[128,512]{1,0:T(8,128)(2,1)}, u32[]{:S(2)}, u32[]{:S(2)}) collective-permute-start(bf16[128,512]{1,0:T(8,128)(2,1)S(1)} %copy-done.4), channel_id=1, source_target_pairs={{0,3},{1,2},{2,1},{3,0},{4,7},{5,6},{6,5},{7,4},{8,11},{9,10},{10,... | collective-permute-start | bytes 393224 | tf_op jit(solution)/shard_map/ppermute | solution.py:306
  120.2 38.7 %copy-start.5 = (bf16[128,512]{1,0:T(8,128)(2,1)}, bf16[128,512]{1,0:T(8,128)(2,1)S(1)}, u32[]{:S(2)}) copy-start(bf16[128,512]{1,0:T(8,128)(2,1)S(1)} %collective-permute-done.3.refs_1_) | copy-start | bytes 393220
  120.2 38.7 %copy-start.6 = (bf16[128,512]{1,0:T(8,128)(2,1)}, bf16[128,512]{1,0:T(8,128)(2,1)S(1)}, u32[]{:S(2)}) copy-start(bf16[128,512]{1,0:T(8,128)(2,1)S(1)} %collective-permute-done.4.refs_2_) | copy-start | bytes 393220
  158.9 1.3 copy-start.1

commit v4 on v3

--- a/solution.py
+++ b/solution.py
@@ -100,55 +100,32 @@
         store.wait()
 
 
-def middle_kernel(columns, factor_top, kernel_top, inverse_top, scale_top, inverse_mid, untwist_low, third,
-                  held, out, rows_f, rows_g, whole, lines, forth, reverse, scale, across, twist, sem, sem_in, sem_out):
-    top = forth.shape[0]
+def middle_kernel(columns, kernel_top, packed, third,
+                  out, rows_f, rows_g, whole, lines, sem_out):
+    top = kernel_top.shape[0]
+    factor_top, inverse_top, inverse_mid = (packed.at[pl.ds((HALF + n) * top, top)] for n in range(3))
     place = lax.axis_index("seq")
-    pairs = ((factor_top, forth), (kernel_top, whole), (inverse_top, reverse), (inverse_mid, across),
-             (untwist_low.at[pl.ds(place // 16 * 8, 8)], twist))
-    copies = [pltpu.make_async_copy(a, b, sem.at[n]) for n, (a, b) in enumerate(pairs)]
-    quarter = HALF * top // 4
-    scales = [
-        pltpu.make_async_copy(
-            scale_top.at[pl.ds(n * quarter, quarter)], scale.at[pl.ds(n * quarter, quarter)], sem_in.at[4 + n]
-        )
-        for n in range(4)
-    ]
-    size = top // 4 * PITCH
-    loads = [
-        pltpu.make_async_copy(columns.at[pl.ds(n * size, size)], held.at[pl.ds(n * size, size)], sem_in.at[n])
-        for n in range(4)
-    ]
-    for copy in loads + copies + scales:
-        copy.start()
     for n in range(top // 8):
-        if n % 4 == 0:
-            loads[n // 4].wait()
         at = n * 8 * PITCH
-        rows_f[at:at + 8 * PITCH, :] = held[at:at + 8 * PITCH, :].astype(F32)
+        rows_f[at:at + 8 * PITCH, :] = columns[at:at + 8 * PITCH, :].astype(F32)
     rows = rows_f[pl.ds(HALF, 2 * HALF, stride=PITCH), :]
     lines[...] = trade_halves(rows[:HALF], rows[HALF:])[0]
-    for copy in copies:
-        copy.wait()
     lower = iota((top, LANES), 1) < HALF
-    all_top = whole[...]
+    all_top = kernel_top[...]
     turned = pltpu.roll(all_top, HALF, 1)
     keep = lower == (lax.rem(place, 2) == 0)
     whole[...] = jnp.where(keep, all_top, turned)
-    scale_low = jnp.broadcast_to(column_of_row(twist[pl.ds(lax.rem(place // 2, 8), 1), :]), (across.shape[0], LANES))
 
     for r in range(0, HALF, 2):
-        if r % 16 == 0:
-            scales[r // 16].wait()
         one = rows_f[pl.ds(r, top, stride=PITCH), :].astype(BF16)
         two = rows_f[pl.ds(r + 1, top, stride=PITCH), :].astype(BF16)
-        spectrum = dot(forth[...], jnp.concatenate([one, two], axis=1)).astype(BF16).astype(F32)
+        spectrum = dot(factor_top[...], jnp.concatenate([one, two], axis=1)).astype(BF16).astype(F32)
         first = spectrum[:, :LANES] * whole[...] * lines[r:r + 1, :]
         other = spectrum[:, LANES:] * whole[...] * lines[r + 1:r + 2, :]
         filtered = jnp.concatenate([first.astype(BF16), other.astype(BF16)], axis=1)
-        back = dot(reverse[...], filtered)
-        rows_g[pl.ds(r, top, stride=PITCH), :] = back[:, :LANES] * scale[r * top:(r + 1) * top, :].astype(F32)
-        rows_g[pl.ds(r + 1, top, stride=PITCH), :] = back[:, LANES:] * scale[(r + 1) * top:(r + 2) * top, :].astype(F32)
+        back = dot(inverse_top[...], filtered)
+        rows_g[pl.ds(r, top, stride=PITCH), :] = back[:, :LANES] * packed[r * top:(r + 1) * top, :].astype(F32)
+        rows_g[pl.ds(r + 1, top, stride=PITCH), :] = back[:, LANES:] * packed[(r + 1) * top:(r + 2) * top, :].astype(F32)
 
     part = 32 * HALF
     stores = []
@@ -158,9 +135,9 @@
             at = (n * 4 + m * 2) * PITCH
             upper, under = trade_halves(rows_g[at:at + HALF, :], rows_g[at + PITCH:at + PITCH + HALF, :])
             sides.append(jnp.concatenate([upper.astype(BF16), under.astype(BF16)], axis=0))
-        result = dot(across[...], jnp.concatenate(sides, axis=1))
+        result = dot(inverse_mid[...], jnp.concatenate(sides, axis=1))
         for m in range(2):
-            side = result[:, m * LANES:(m + 1) * LANES] * scale_low
+            side = result[:, m * LANES:(m + 1) * LANES]
             for q in range(4):
                 pair = trade_halves(side[q * 32:q * 32 + 16], side[q * 32 + 16:q * 32 + 32])
                 for p in range(2):
@@ -175,14 +152,20 @@
         store.wait()
 
 
-def spread_kernel(untwist_top, scale_top):
+def pack_kernel(untwist_top, factor_top, inverse_top, inverse_mid, untwist_low, packed):
     top = untwist_top.shape[0]
+    place = lax.axis_index("seq")
     shape = (top, LANES)
     lower = iota(shape, 1) < HALF
     for r in range(HALF):
         one = jnp.broadcast_to(untwist_top[:, r:r + 1], shape)
         two = jnp.broadcast_to(untwist_top[:, HALF + r:HALF + r + 1], shape)
-        scale_top[r * top:(r + 1) * top, :] = jnp.where(lower, one, two).astype(BF16)
+        packed[r * top:(r + 1) * top, :] = jnp.where(lower, one, two).astype(BF16)
+    at = HALF * top
+    packed[at:at + top, :] = factor_top[...]
+    packed[at + top:at + 2 * top, :] = inverse_top[...]
+    column = column_of_row(untwist_low[pl.ds(place // 2, 1), :])
+    packed[at + 2 * top:at + 3 * top, :] = (column * inverse_mid[...].astype(F32)).astype(BF16)
 
 
 def silu_kernel(*refs):
@@ -198,56 +181,35 @@
 
 
 def last_kernel(low, third, inverse_low, silu, *refs):
-    weights, out = refs[:4], refs[4]
-    held, small, gates, matrix, rows_f, gated, result, sem, sem_in, sem_gate, sem_out = refs[5:]
+    weights, out, rows_f, gated, result, sem_out = refs[:4], *refs[4:]
     pitch = LANES + 8
     block = 4 * low
     place = lax.axis_index("ch")
-    part = low * LANES // 4
-    loads = [
-        pltpu.make_async_copy(third.at[pl.ds(n * part, part)], held.at[pl.ds(n * part, part)], sem_in.at[n])
-        for n in range(4)
-    ]
-    fetch_low = pltpu.make_async_copy(inverse_low, small, sem.at[4])
-    fetch_gates = [
-        pltpu.make_async_copy(
-            silu.at[:, pl.ds(at, block)], gates.at[:, pl.ds(at, block)], sem_gate.at[n]
-        )
-        for n, at in enumerate((p * 4 + g) * block for g in range(4) for p in range(2))
-    ]
-    fetch_weights = [pltpu.make_async_copy(w, matrix.at[pl.ds(t * LANES, LANES)], sem.at[t]) for t, w in enumerate(weights)]
-    for copy in loads + [fetch_low] + fetch_gates[:2] + fetch_weights + fetch_gates[2:]:
-        copy.start()
-    for n in range(4):
-        loads[n].wait()
-        for k in range(n * low // 4, (n + 1) * low // 4):
-            for h in range(2):
-                for t in range(4):
-                    source = pl.multiple_of(((k * 2 + h) * 4 + (place ^ t)) * 16, 16)
-                    to = k * pitch + (h * 4 + t) * 16
-                    rows_f[to:to + 16, :] = held[pl.ds(source, 16), :].astype(F32)
-    fetch_low.wait()
+    for k in range(low):
+        for h in range(2):
+            for t in range(4):
+                source = pl.multiple_of(((k * 2 + h) * 4 + (place ^ t)) * 16, 16)
+                to = k * pitch + (h * 4 + t) * 16
+                rows_f[to:to + 16, :] = third[pl.ds(source, 16), :].astype(F32)
     copies = []
     for g in range(4):
-        for p in range(2):
-            fetch_gates[2 * g + p].wait()
         for b in range(4 * g, 4 * g + 4):
             for t in range(4):
                 one = rows_f[pl.ds(t * 16 + b, low, stride=pitch), :]
                 two = rows_f[pl.ds((4 + t) * 16 + b, low, stride=pitch), :]
                 pair = trade_halves(one, two)
-                mixed = dot(small[...], jnp.concatenate([p.astype(BF16) for p in pair], axis=1))
+                mixed = dot(inverse_low[...], jnp.concatenate([p.astype(BF16) for p in pair], axis=1))
                 for p in range(2):
                     at = (p * 16 + b) * low
                     gated[at:at + low, t * LANES:(t + 1) * LANES] = (
-                        mixed[:, p * LANES:(p + 1) * LANES] * gates[t, at:at + low, :].astype(F32)
+                        mixed[:, p * LANES:(p + 1) * LANES] * silu[t, at:at + low, :].astype(F32)
                     ).astype(BF16)
-        if g == 0:
-            for copy in fetch_weights:
-                copy.wait()
         for p in range(2):
             at = (p * 4 + g) * block
-            result[at:at + block, :] = dot(gated[at:at + block, :], matrix[...]).astype(BF16)
+            total = dot(gated[at:at + block, :LANES], weights[0][...])
+            for t in range(1, 4):
+                total += dot(gated[at:at + block, t * LANES:(t + 1) * LANES], weights[t][...])
+            result[at:at + block, :] = total.astype(BF16)
             copy = pltpu.make_async_copy(
                 result.at[pl.ds(at, block)], out.at[pl.ds(at, block)], sem_out.at[g * 2 + p]
             )
@@ -322,62 +284,47 @@
         values, factor_low, twist_low.T, factor_mid, twist_top, kernel_low,
         limit=60 << 20, far=range(5), out_spec=pl.BlockSpec(memory_space=pl.ANY),
     )
+    message, untwist_t = lax.optimization_barrier((message, untwist_top))
     columns = lax.all_to_all(message.reshape(2 * low, PITCH, width), "seq", 0, 0, tiled=True)
 
     turns = range(ch_count)
-    shares = [
-        swap(lax.dynamic_slice_in_dim(values, (ch_place ^ turn) * share, share, 0), turn) for turn in turns
-    ]
-    scale_top = call(
-        spread_kernel, "spread", jax.ShapeDtypeStruct((HALF * top, width), BF16), [], unit, untwist_top,
-        limit=60 << 20,
-    )
-    columns, shares, scale_top = lax.optimization_barrier((columns, shares, scale_top))
+    shares = [lax.dynamic_slice_in_dim(values, (ch_place ^ turn) * share, share, 0) for turn in turns]
+    shares = [swap(array, turn) if turn < 3 else array for turn, array in enumerate(shares)]
+    packed = call(
+        pack_kernel, "pack", jax.ShapeDtypeStruct(((HALF + 3) * top, width), BF16), [], unit,
+        untwist_t, factor_top, inverse_top, inverse_mid, untwist_low.T, limit=8 << 20,
+    )
+    columns, shares = lax.optimization_barrier((columns, shares))
     third = call(
         middle_kernel, "middle", jax.ShapeDtypeStruct((rows, width), BF16),
         [
-            pltpu.VMEM((top * PITCH, width), BF16),
             pltpu.VMEM((rows, width), BF16),
             padded,
             padded,
             pltpu.VMEM((top, width), F32),
             pltpu.VMEM((HALF, width), F32),
-            pltpu.VMEM((top, top), BF16),
-            pltpu.VMEM((top, top), BF16),
-            pltpu.VMEM((HALF * top, width), BF16),
-            pltpu.VMEM((mid, mid), BF16),
-            pltpu.VMEM((8, mid), F32),
-            pltpu.SemaphoreType.DMA((5,)),
-            pltpu.SemaphoreType.DMA((8,)),
             pltpu.SemaphoreType.DMA((4,)),
         ], unit * (2 * top + mid),
-        columns.reshape(top * PITCH, width), factor_top, kernel_top, inverse_top, scale_top, inverse_mid,
-        untwist_low.T, limit=60 << 20, far=range(7), out_spec=pl.BlockSpec(memory_space=pl.ANY),
+        columns.reshape(top * PITCH, width), kernel_top, packed, limit=24 << 20, out_spec=pl.BlockSpec(memory_space=pltpu.HBM),
     )
     third, shares, out_weight = lax.optimization_barrier((third, shares, out_weight))
+    shares = [swap(array, turn) if turn == 3 else array for turn, array in enumerate(shares)]
     weights = [swap(out_weight, turn) for turn in turns]
     silu = call(
-        silu_kernel, "silu", jax.ShapeDtypeStruct((ch_count, share, width), BF16), [], unit, *shares, limit=60 << 20
+        silu_kernel, "silu", jax.ShapeDtypeStruct((ch_count, share, width), BF16), [], unit, *shares, limit=12 << 20
     )
     third = lax.all_to_all(third.reshape(top * ch_count, -1, width), ("seq", "ch"), 0, 0, tiled=True)
     return call(
         functools.partial(last_kernel, low), "last", jax.ShapeDtypeStruct((share, columns_out), BF16),
         [
-            pltpu.VMEM((rows, width), BF16),
-            pltpu.VMEM((low, low), BF16),
-            pltpu.VMEM((ch_count, share, width), BF16),
-            pltpu.VMEM((ch_count * width, columns_out), BF16),
             pltpu.VMEM((low * (width + 8), width), F32),
             pltpu.VMEM((share, columns_out), BF16),
             pltpu.VMEM((share, columns_out), BF16),
-            pltpu.SemaphoreType.DMA((5,)),
-            pltpu.SemaphoreType.DMA((4,)),
-            pltpu.SemaphoreType.DMA((8,)),
             pltpu.SemaphoreType.DMA((8,)),
         ],
         unit * low // 2 + 2 * share * columns_out ** 2,
         third.reshape(rows, width), inverse_low, silu, *weights,
-        limit=60 << 20, far=range(3 + ch_count), out_spec=pl.BlockSpec(memory_space=pl.ANY),
+        limit=24 << 20, out_spec=pl.BlockSpec(memory_space=pltpu.HBM),
     )
 
 

time: 168 us -> 165 us (0.982)
  Pallas kernels: 26.3 us -> 16.5 us
  local copies, waits for them, and re-layouts: 5.49 us -> 13.2 us
    all_to_all x1, waiting for transfers between devices: 5.69 us -> 25.5 us  [local(): lax.all_to_all(message.reshape(2 * low, PITCH, width), 'seq', 0, 0, tiled...]
    all_to_all x1, waiting for transfers between devices: 32.4 us -> 16.1 us  [local(): lax.all_to_all(third.reshape(top * ch_count, -1, width), ('seq', 'ch'), 0...]
    pallas_call x5, Pallas kernels: 26.3 us -> 16.5 us  [call(): pl.pallas_call(kernel, name=name, out_shape=out_shape, in_specs=[hbm if n...]
    unnamed x14 -> x34, local copies, waits for them, and re-layouts: 2.77 us -> 10.7 us
    ppermute x6, waiting for transfers between devices: 44.8 us -> 42.3 us  [swap(): return lax.ppermute(array, 'ch', [(c, c ^ turn) for c in range(ch_count)])]
  transfers between devices with their start and end apart: 8 -> 8, of which waited for: 5 -> 6; matrix products, arithmetic and copies ran while one was open for 2% -> 2% of each run, Pallas kernels for 4% -> 1%
where the time goes in v4:
time: 165 us
  waiting for transfers between devices  83.9 us (51%)
  starting transfers between devices  50.9 us (31%)
  Pallas kernels  16.5 us (10%)
  local copies, waits for them, and re-layouts  13.2 us (8%)
    ppermute x6, waiting for transfers between devices, swap(): return lax.ppermute(array, 'ch', [(c, c ^ turn) for c in range(ch_count)])  42.3 us
    all_to_all x1, waiting for transfers between devices, local(): lax.all_to_all(message.reshape(2 * low, PITCH, width), 'seq', 0, 0, tiled...  25.5 us
    all_to_all x1, starting transfers between devices, local(): lax.all_to_all(message.reshape(2 * low, PITCH, width), 'seq', 0, 0, tiled...  20.8 us
    ppermute x6, starting transfers between devices, swap(): return lax.ppermute(array, 'ch', [(c, c ^ turn) for c in range(ch_count)])  19 us
    pallas_call x5, Pallas kernels, call(): pl.pallas_call(kernel, name=name, out_shape=out_shape, in_specs=[hbm if n...  16.5 us
    all_to_all x1, waiting for transfers between devices, local(): lax.all_to_all(third.reshape(top * ch_count, -1, width), ('seq', 'ch'), 0...  16.1 us
    all_to_all x1, starting transfers between devices, local(): lax.all_to_all(third.reshape(top * ch_count, -1, width), ('seq', 'ch'), 0...  11 us
    unnamed x34, local copies, waits for them, and re-layouts  10.7 us
  transfers between devices with their start and end apart: 8, of which 6 were waited for; matrix products, arithmetic and copies ran while one was open for 2% of the time, Pallas kernels for 1%

profile of v4, /device:TPU:1, one launch (start us, length us, event | category | flops | bytes accessed | tf_op | source)
XLA Modules:
  0.0 164.8 jit_solution(9176674916072990200)
XLA Ops:
  0.0 5.4 %forward.1 = bf16[9216,128]{1,0:T(8,128)(2,1)} custom-call(bf16[8192,128]{1,0:T(8,128)(2,1)} %values.1, bf16[64,64]{1,0:T(8,128)(2,1)} %factor_low.1, f32[64,128]{1,0:T(8,128)} %bitcast.11, bf16[128,128]{1,0:T(8,128)(2,1)} %factor_mid.1, f32[128,128]{1,0:T(8,128)} %twist_top.1, bf16[64,128]{1,0:T(8,128)(2,1)} %kernel_low.1), custom_call_target="tpu_custom_call" | custom-call | flops 402653184 | bytes 4612096 | tf_op jit(solution)/shard_map/forward/pallas_call | solution.py:226
  5.4 20.8 %all-to-all-start = ((bf16[128,72,128]{2,1,0:T(8,128)(2,1)}), bf16[128,72,128]{2,1,0:T(8,128)(2,1)S(1)}, u32[]{:S(2)}, u32[]{:S(2)}) async-start(bf16[128,72,128]{2,1,0:T(8,128)(2,1)} %bitcast.10), calls=%async_computation | async-start | bytes 4718592 | tf_op jit(solution)/shard_map/all_to_all | solution.py:288
  26.3 0.0 copy-start.11
  26.3 0.0 copy-start.12
  26.3 0.0 copy-start.13
  26.3 0.0 copy-start.14
  26.3 0.0 copy-start.15
  26.3 2.5 %constant_dynamic-slice_fusion = (bf16[2048,128]{1,0:T(8,128)(2,1)}, bf16[2048,128]{1,0:T(8,128)(2,1)S(1)}, bf16[2048,128]{1,0:T(8,128)(2,1)S(1)}, bf16[2048,128]{1,0:T(8,128)(2,1)S(1)}) fusion(bf16[8192,128]{1,0:T(8,128)(2,1)} %values.1, s32[]{:T(128)S(6)} %select_n.15, s32[]{:T(128)S(6)} %select_n.13, s32[]{:T(128)S(6)} %select_n.12, s32[]{:T(128)S(6)} %select_n.14), kind=kLoop, calls=%fused_computation | loop fusion | bytes 4194320 | tf_op jit(solution)/shard_map/dynamic_slice | solution.py:291
  28.8 0.0 copy-start.10
  28.8 3.0 %collective-permute-start = (bf16[2048,128]{1,0:T(8,128)(2,1)S(1)}, bf16[2048,128]{1,0:T(8,128)(2,1)S(1)}, u32[]{:S(2)}, u32[]{:S(2)}) collective-permute-start(bf16[2048,128]{1,0:T(8,128)(2,1)S(1)} %get-tuple-element.32), channel_id=1, source_target_pairs={{0,1},{1,0},{2,3},{3,2},{4,5},{5,4},{6,7},{7,6},{8,9},{9,8},{10,11... | collective-permute-start | bytes 1572872 | tf_op jit(solution)/shard_map/ppermute | solution.py:268
  31.8 2.2 %collective-permute-start.1 = (bf16[2048,128]{1,0:T(8,128)(2,1)S(1)}, bf16[2048,128]{1,0:T(8,128)(2,1)S(1)}, u32[]{:S(2)}, u32[]{:S(2)}) collective-permute-start(bf16[2048,128]{1,0:T(8,128)(2,1)S(1)} %get-tuple-element.34), channel_id=1, source_target_pairs={{0,2},{1,3},{2,0},{3,1},{4,6},{5,7},{6,4},{7,5},{8,10},{9,11},{10,... | collective-permute-start | bytes 1572872 | tf_op jit(solution)/shard_map/ppermute | solution.py:268
  34.1 0.0 copy-done.11
  34.1 0.0 copy-done.12
  34.1 0.0 copy-done.13
  34.1 0.0 copy-done.14
  34.1 0.0 copy-done.15
  34.1 1.4 pack.1.packed
  35.5 0.0 copy-start
  35.5 1.4 copy-done
  36.9 0.0 collective-permute-done.refs_1_
  36.9 21.9 %collective-permute-done.1.refs_2_ = bf16[2048,128]{1,0:T(8,128)(2,1)S(1)} collective-permute-done((bf16[2048,128]{1,0:T(8,128)(2,1)S(1)}, bf16[2048,128]{1,0:T(8,128)(2,1)S(1)}, u32[]{:S(2)}, u32[]{:S(2)}) %collective-permute-start.1) | collective-permute-done | bytes 524320 | tf_op jit(solution)/shard_map/ppermute | solution.py:268
  58.8 0.0 copy-start.5
  58.8 0.8 copy-done.5
  59.6 25.5 %all-to-all-done = bf16[128,72,128]{2,1,0:T(8,128)(2,1)S(1)} async-done(((bf16[128,72,128]{2,1,0:T(8,128)(2,1)}), bf16[128,72,128]{2,1,0:T(8,128)(2,1)S(1)}, u32[]{:S(2)}, u32[]{:S(2)}) %all-to-all-start) | async-done | bytes 2359328 | tf_op jit(solution)/shard_map/all_to_all | solution.py:288
  85.1 0.0 copy-done.10
  85.1 0.0 copy-start.1
  85.1 1.6 copy-done.1
  86.7 3.9 %middle.1 = bf16[8192,128]{1,0:T(8,128)(2,1)S(1)} custom-call(bf16[9216,128]{1,0:T(8,128)(2,1)S(1)} %bitcast.6, f32[128,128]{1,0:T(8,128)S(1)} %copy-done.10, bf16[8576,128]{1,0:T(8,128)(2,1)S(1)} %copy-done.1), custom_call_target="tpu_custom_call" | custom-call | flops 805306368 | bytes 6717440 | tf_op jit(solution)/shard_map/middle/pallas_call | solution.py:226
  90.6 0.0 copy-start.2
  90.6 1.3 copy-done.2
  92.0 0.0 copy-start.7
  92.0 0.0 copy-start.16
  92.0 11.0 %all-to-all-start.1 = ((bf16[512,16,128]{2,1,0:T(8,128)(2,1)}), bf16[512,16,128]{2,1,0:T(8,128)(2,1)S(1)}, u32[]{:S(2)}, u32[]{:S(2)}) async-start(bf16[512,16,128]{2,1,0:T(8,128)(2,1)} %bitcast.7), calls=%async_computation.1 | async-start | bytes 4194304 | tf_op jit(solution)/shard_map/all_to_all | solution.py:316
  103.0 3.5 %collective-permute-start.2 = (bf16[2048,128]{1,0:T(8,128)(2,1)}, bf16[2048,128]{1,0:T(8,128)(2,1)S(1)}, u32[]{:S(2)}, u32[]{:S(2)}) collective-permute-start(bf16[2048,128]{1,0:T(8,128)(2,1)} %get-tuple-element.29), channel_id=1, source_target_pairs={{0,3},{1,2},{2,1},{3,0},{4,7},{5,6},{6,5},{7,4},{8,11},{9,10},{10,... | collective-permute-start | bytes 1572872 | tf_op jit(solution)/shard_map/ppermute | solution.py:268
  106.5 0.0 copy-done.7
  106.5 2.0 %collective-permute-start.5 = (bf16[128,512]{1,0:T(8,128)(2,1)S(1)}, bf16[128,512]{1,0:T(8,128)(2,1)S(1)}, u32[]{:S(2)}, u32[]{:S(2)}) collective-permute-start(bf16[128,512]{1,0:T(8,128)(2,1)S(1)} %copy-done.7), channel_id=1, source_target_pairs={{0,3},{1,2},{2,1},{3,0},{4,7},{5,6},{6,5},{7,4},{8,11},{9,10},{10,... | collective-permute-start | bytes 393224 | tf_op jit(solution)/shard_map/ppermute | solution.py:268
  108.6 6.0 %collective-permute-start.4 = (bf16[128,512]{1,0:T(8,128)(2,1)S(1)}, bf16[128,512]{1,0:T(8,128)(2,1)S(1)}, u32[]{:S(2)}, u32[]{:S(2)}) collective-permute-start(bf16[128,512]{1,0:T(8,128)(2,1)S(1)} %copy-done.7), channel_id=1, source_target_pairs={{0,2},{1,3},{2,0},{3,1},{4,6},{5,7},{6,4},{7,5},{8,10},{9,11},{10,... | collective-permute-start | bytes 393224 | tf_op jit(solution)/shard_map/ppermute | solution.py:268
  114.5 2.3 %collective-permute-start.3 = (bf16[128,512]{1,0:T(8,128)(2,1)S(1)}, bf16[128,512]{1,0:T(8,128)(2,1)S(1)}, u32[]{:S(2)}, u32[]{:S(2)}) collective-permute-start(bf16[128,512]{1,0:T(8,128)(2,1)S(1)} %copy-done.7), channel_id=1, source_target_pairs={{0,1},{1,0},{2,3},{3,2},{4,5},{5,4},{6,7},{7,6},{8,9},{9,8},{10,11... | collective-permute-start | bytes 393224 | tf_op jit(solution)/shard_map/ppermute | solution.py:268
  116.8 9.2 %collective-permute-done.2.refs_3_ = bf16[2048,128]{1,0:T(8,128)(2,1)S(1)} collective-permute-done((bf16[2048,128]{1,0:T(8,128)(2,1)}, bf16[2048,128]{1,0:T(8,128)(2,1)S(1)}, u32[]{:S(2)}, u32[]{:S(2)}) %collective-permute-start.2) | collective-permute-done | bytes 524320 | tf_op jit(solution)/shard_map/ppermute | solution.py:268
  126.0 0.0 copy-start.6
  126.0 1.0 copy-done.6
  127.1 1.0 silu.1
  128.1 0.0 copy-start.3
  128.1 1.3 copy-done.3
  129.4 2.1 %collective-permute-done.5.refs_3_ = bf16[128,512]{1,0:T(8,128)(2,1)S(1)} collective-permute-done((bf16[128,512]{1,0:T(8,128)(2,1)S(1)}, bf16[128,512]{1,0:T(8,128)(2,1)S(1)}, u32[]{:S(2)}, u32[]{:S(2)}) %collective-permute-start.5) | collective-permute-done | bytes 131104 | tf_op jit(solution)/shard_map/ppermute | solution.py:268
  131.5 9.0 %collective-permute-done.4.refs_2_ = bf16[128,512]{1,0:T(8,128)(2,1)S(1)} collective-permute-done((bf16[128,512]{1,0:T(8,128)(2,1)S(1)}, bf16[128,512]{1,0:T(8,128)(2,1)S(1)}, u32[]{:S(2)}, u32[]{:S(2)}) %collective-permute-start.4) | collective-permute-done | bytes 131104 | tf_op jit(solution)/shard_map/ppermute | solution.py:268
  140.6 0.0 collective-permute-done.3.refs_1_
  140.6 0.0 copy-start.8
  140.6 0.6 copy-done.8
  141.2 16.1 %all-to-all-done.1 = bf16[512,16,128]{2,1,0:T(8,128)(2,1)S(1)} async-done(((bf16[512,16,128]{2,1,0:T(8,128)(2,1)}), bf16[512,16,128]{2,1,0:T(8,128)(2,1)S(1)}, u32[]{:S(2)}, u32[]{:S(2)}) %all-to-all-start.1) | async-done | bytes 2097184 | tf_op jit(solution)/shard_map/all_to_all | solution.py:316
  157.4 0.0 copy-done.16
  157.4 0.0 copy-start.4
  157.4 1.6 copy-done.4
  159.0 0.0 copy-start.9
  159.0 0.9 copy-done.9
  159.9 4.8 %last.1 = bf16[2048,512]{1,0:T(8,128)(2,1)} custom-call(bf16[8192,128]{1,0:T(8,128)(2,1)S(1)} %bitcast.8, bf16[64,64]{1,0:T(8,128)(2,1)S(1)} %copy-done.16, bf16[4,2048,128]{2,1,0:T(8,128)(2,1)S(1)} %copy-done.4, bf16[128,512]{1,0:T(8,128)(2,1)S(1)} %copy-done.7, bf16[128,512]{1,0:T(8,128)(2,1)S(1)} %copy-done.9, ...), custom_call_target="tpu_custom_call" | custom-call | flops 1140850688 | bytes 6823936 | tf_op jit(solution)/shard_map/last/pallas_call | solution.py:226
Async XLA Ops:
  5.4 79.6 %all-to-all-start = ((bf16[128,72,128]{2,1,0:T(8,128)(2,1)}), bf16[128,72,128]{2,1,0:T(8,128)(2,1)S(1)}, u32[]{:S(2)}, u32[]{:S(2)}) async-start(bf16[128,72,128]{2,1,0:T(8,128)(2,1)} %bitcast.10), calls=%async_computation | async-start | bytes 4718592 | tf_op jit(solution)/shard_map/all_to_all | solution.py:288
  26.3 7.8 %copy-start.11 = (f32[128,128]{1,0:T(8,128)S(1)}, f32[128,128]{1,0:T(8,128)}, u32[]{:S(2)}) copy-start(f32[128,128]{1,0:T(8,128)} %untwist_top) | copy-start | bytes 196612
  26.3 7.8 %copy-start.12 = (bf16[128,128]{1,0:T(8,128)(2,1)S(1)}, bf16[128,128]{1,0:T(8,128)(2,1)}, u32[]{:S(2)}) copy-start(bf16[128,128]{1,0:T(8,128)(2,1)} %factor_top.1) | copy-start | bytes 98308
  26.3 7.8 %copy-start.13 = (bf16[128,128]{1,0:T(8,128)(2,1)S(1)}, bf16[128,128]{1,0:T(8,128)(2,1)}, u32[]{:S(2)}) copy-start(bf16[128,128]{1,0:T(8,128)(2,1)} %inverse_top.1) | copy-start | bytes 98308
  26.3 7.8 %copy-start.14 = (bf16[128,128]{1,0:T(8,128)(2,1)S(1)}, bf16[128,128]{1,0:T(8,128)(2,1)}, u32[]{:S(2)}) copy-start(bf16[128,128]{1,0:T(8,128)(2,1)} %inverse_mid.1) | copy-start | bytes 98308
  26.3 7.8 %copy-start.15 = (f32[128,64]{0,1:T(8,128)S(1)}, f32[128,64]{0,1:T(8,128)}, u32[]{:S(2)}) copy-start(f32[128,64]{0,1:T(8,128)} %param.25) | copy-start | bytes 98308
  28.8 56.2 %copy-start.10 = (f32[128,128]{1,0:T(8,128)S(1)}, f32[128,128]{1,0:T(8,128)}, u32[]{:S(2)}) copy-start(f32[128,128]{1,0:T(8,128)} %kernel_top.1) | copy-start | bytes 196612
  28.8 8.0 %collective-permute-start = (bf16[2048,128]{1,0:T(8,128)(2,1)S(1)}, bf16[2048,128]{1,0:T(8,128)(2,1)S(1)}, u32[]{:S(2)}, u32[]{:S(2)}) collective-permute-start(bf16[2048,128]{1,0:T(8,128)(2,1)S(1)} %get-tuple-element.32), channel_id=1, source_target_pairs={{0,1},{1,0},{2,3},{3,2},{4,5},{5,4},{6,7},{7,6},{8,9},{9,8},{10,11... | collective-permute-start | bytes 1572872 | tf_op jit(solution)/shard_map/ppermute | solution.py:268
  31.8 26.9 %collective-permute-start.1 = (bf16[2048,128]{1,0:T(8,128)(2,1)S(1)}, bf16[2048,128]{1,0:T(8,128)(2,1)S(1)}, u32[]{:S(2)}, u32[]{:S(2)}) collective-permute-start(bf16[2048,128]{1,0:T(8,128)(2,1)S(1)} %get-tuple-element.34), channel_id=1, source_target_pairs={{0,2},{1,3},{2,0},{3,1},{4,6},{5,7},{6,4},{7,5},{8,10},{9,11},{10,... | collective-permute-start | bytes 1572872 | tf_op jit(solution)/shard_map/ppermute | solution.py:268
  35.5 1.4 copy-start
  58.8 0.8 copy-start.5
  85.1 1.6 copy-start.1
  90.6 1.3 copy-start.2
  92.0 14.6 %copy-start.7 = (bf16[128,512]{1,0:T(8,128)(2,1)S(1)}, bf16[128,512]{1,0:T(8,128)(2,1)}, u32[]{:S(2)}) copy-start(bf16[128,512]{1,0:T(8,128)(2,1)} %refs_0_) | copy-start | bytes 393220
  92.0 65.4 %copy-start.16 = (bf16[64,64]{1,0:T(8,128)(2,1)S(1)}, bf16[64,64]{1,0:T(8,128)(2,1)}, u32[]{:S(2)}) copy-start(bf16[64,64]{1,0:T(8,128)(2,1)} %inverse_low.1) | copy-start | bytes 24580
  92.0 65.4 %all-to-all-start.1 = ((bf16[512,16,128]{2,1,0:T(8,128)(2,1)}), bf16[512,16,128]{2,1,0:T(8,128)(2,1)S(1)}, u32[]{:S(2)}, u32[]{:S(2)}) async-start(bf16[512,16,128]{2,1,0:T(8,128)(2,1)} %bitcast.7), calls=%async_computation.1 | async-start | bytes 4194304 | tf_op jit(solution)/shard_map/all_to_all | solution.py:316
  103.0 23.1 %collective-permute-start.2 = (bf16[2048,128]{1,0:T(8,128)(2,1)}, bf16[2048,128]{1,0:T(8,128)(2,1)S(1)}, u32[]{:S(2)}, u32[]{:S(2)}) collective-permute-start(bf16[2048,128]{1,0:T(8,128)(2,1)} %get-tuple-element.29), channel_id=1, source_target_pairs={{0,3},{1,2},{2,1},{3,0},{4,7},{5,6},{6,5},{7,4},{8,11},{9,10},{10,... | collective-permute-start | bytes 1572872 | tf_op jit(solution)/shard_map/ppermute | solution.py:268
  106.5 25.0 %collective-permute-start.5 = (bf16[128,512]{1,0:T(8,128)(2,1)S(1)}, bf16[128,512]{1,0:T(8,128)(2,1)S(1)}, u32[]{:S(2)}, u32[]{:S(2)}) collective-permute-start(bf16[128,512]{1,0:T(8,128)(2,1)S(1)} %copy-done.7), channel_id=1, source_target_pairs={{0,3},{1,2},{2,1},{3,0},{4,7},{5,6},{6,5},{7,4},{8,11},{9,10},{10,... | collective-permute-start | bytes 393224 | tf_op jit(solution)/shard_map/ppermute | solution.py:268
  108.6 32.0 %collective-permute-start.4 = (bf16[128,512]{1,0:T(8,128)(2,1)S(1)}, bf16[128,512]{1,0:T(8,128)(2,1)S(1)}, u32[]{:S(2)}, u32[]{:S(2)}) collective-permute-start(bf16[128,512]{1,0:T(8,128)(2,1)S(1)} %copy-done.7), channel_id=1, source_target_pairs={{0,2},{1,3},{2,0},{3,1},{4,6},{5,7},{6,4},{7,5},{8,10},{9,11},{10,... | collective-permute-start | bytes 393224 | tf_op jit(solution)/shard_map/ppermute | solution.py:268
  114.5 26.1 %collective-permute-start.3 = (bf16[128,512]{1,0:T(8,128)(2,1)S(1)}, bf16[128,512]{1,0:T(8,128)(2,1)S(1)}, u32[]{:S(2)}, u32[]{:S(2)}) collective-permute-start(bf16[128,512]{1,0:T(8,128)(2,1)S(1)} %copy-done.7), channel_id=1, source_target_pairs={{0,1},{1,0},{2,3},{3,2},{4,5},{5,4},{6,7},{7,6},{8,9},{9,8},{10,11... | collective-permute-start | bytes 393224 | tf_op jit(solution)/shard_map/ppermute | solution.py:268
  126.0 1.0 copy-start.6
  128.1 1.3 copy-start.3
  140.6 0.6 copy-start.8
  157.4 1.6 copy-start.4
  159.0 0.9 copy-start.9

commit v5 on v4

--- a/solution.py
+++ b/solution.py
@@ -41,47 +41,28 @@
 
 
 def forward_kernel(low, values, factor_low, twist_low, factor_mid, twist_top, kernel_low, message,
-                   held, small, wide, row, twist, rows_f, diag, out, sem_in, sem_out):
+                   rows_f, diag, out, sem_out):
     mid = factor_mid.shape[0]
     times = 256 // low
-    chunk = mid * low // 4
     place = lax.axis_index("seq")
-    loads = [
-        pltpu.make_async_copy(values.at[pl.ds(n * chunk, chunk)], held.at[pl.ds(n * chunk, chunk)], sem_in.at[n])
-        for n in range(4)
-    ]
-    fetch_low = pltpu.make_async_copy(factor_low, small, sem_in.at[4])
-    others = [
-        pltpu.make_async_copy(factor_mid, wide, sem_in.at[5]),
-        pltpu.make_async_copy(twist_top.at[pl.ds(place // 8 * 8, 8)], row, sem_in.at[6]),
-        pltpu.make_async_copy(twist_low, twist, sem_in.at[7]),
-    ]
-    fetch_low.start()
-    for copy in loads + others:
-        copy.start()
-    fetch_low.wait()
-    tiled = repeat_lanes(small[...], times)
+    tiled = repeat_lanes(factor_low[...], times)
     for t in range(times):
         block = jnp.where(iota(tiled.shape, 1) // low == t, tiled, 0.0)
         diag[t * low:(t + 1) * low, :] = block.astype(BF16)
     for n in range(mid * low // 512):
-        if n % 4 == 0:
-            loads[n // 4].wait()
         at = n * 512
-        both = dot(diag[...], jnp.concatenate([held[at:at + 256, :], held[at + 256:at + 512, :]], axis=1))
+        both = dot(diag[...], jnp.concatenate([values[at:at + 256, :], values[at + 256:at + 512, :]], axis=1))
         for t in range(2 * times):
             to = (n * 2 * times + t) * PITCH
             side = t // times * LANES
             at = t % times * low
             rows_f[to:to + low, :] = both[at:at + low, side:side + LANES]
-    for copy in others:
-        copy.wait()
-    scaled = column_of_row(row[pl.ds(lax.rem(place, 8), 1), :]) * wide[...].astype(F32)
+    scaled = column_of_row(twist_top[pl.ds(place, 1), :]) * factor_mid[...].astype(F32)
     profile = kernel_low[...].astype(F32)
     turned = pltpu.roll(profile, HALF, 1)
     stores = []
     for k in range(low):
-        matrix = (scaled * twist[k:k + 1, :]).astype(BF16)
+        matrix = (scaled * twist_low[k:k + 1, :]).astype(BF16)
         second = dot(matrix, rows_f[pl.ds(k, mid, stride=PITCH), :].astype(BF16))
         halves = trade_halves(second[:HALF], second[HALF:])
         for h, (half, line) in enumerate(zip(halves, (profile, turned))):
@@ -168,23 +149,31 @@
     packed[at + 2 * top:at + 3 * top, :] = (column * inverse_mid[...].astype(F32)).astype(BF16)
 
 
-def silu_kernel(*refs):
-    sources, target = refs[:-1], refs[-1]
-    for t, source in enumerate(sources):
+def gate_kernel(*refs):
+    sources, weights, (target, matrix) = refs[:4], refs[4:8], refs[8:]
+    for t, (source, weight) in enumerate(zip(sources, weights)):
+        matrix[t * LANES:(t + 1) * LANES, :] = weight[...]
+
         def body(n, _):
             at = pl.multiple_of(n * 256, 256)
             value = source[pl.ds(at, 256), :].astype(F32)
-            target[t, pl.ds(at, 256), :] = ((0.5 * value) * (1.0 + jnp.tanh(0.5 * value))).astype(BF16)
+            gate = ((0.5 * value) * (1.0 + jnp.tanh(0.5 * value))).astype(BF16)
+            target[pl.ds(at, 256), t * LANES:(t + 1) * LANES] = gate
             return 0
 
         lax.fori_loop(0, source.shape[0] // 256, body, 0)
 
 
-def last_kernel(low, third, inverse_low, silu, *refs):
-    weights, out, rows_f, gated, result, sem_out = refs[:4], *refs[4:]
+def last_kernel(low, third, inverse_low, silu, matrix, out, gates, rows_f, gated, result, sem_in, sem_out):
     pitch = LANES + 8
     block = 4 * low
     place = lax.axis_index("ch")
+    fetches = [
+        pltpu.make_async_copy(silu.at[pl.ds(at, block)], gates.at[pl.ds(at, block)], sem_in.at[n])
+        for n, at in enumerate((p * 4 + g) * block for g in range(4) for p in range(2))
+    ]
+    for copy in fetches:
+        copy.start()
     for k in range(low):
         for h in range(2):
             for t in range(4):
@@ -192,6 +181,8 @@
                 to = k * pitch + (h * 4 + t) * 16
                 rows_f[to:to + 16, :] = third[pl.ds(source, 16), :].astype(F32)
     copies = []
+    for copy in fetches:
+        copy.wait()
     for g in range(4):
         for b in range(4 * g, 4 * g + 4):
             for t in range(4):
@@ -202,13 +193,11 @@
                 for p in range(2):
                     at = (p * 16 + b) * low
                     gated[at:at + low, t * LANES:(t + 1) * LANES] = (
-                        mixed[:, p * LANES:(p + 1) * LANES] * silu[t, at:at + low, :].astype(F32)
+                        mixed[:, p * LANES:(p + 1) * LANES] * gates[at:at + low, t * LANES:(t + 1) * LANES].astype(F32)
                     ).astype(BF16)
         for p in range(2):
             at = (p * 4 + g) * block
-            total = dot(gated[at:at + block, :LANES], weights[0][...])
-            for t in range(1, 4):
-                total += dot(gated[at:at + block, t * LANES:(t + 1) * LANES], weights[t][...])
+            total = dot(gated[at:at + block, :], matrix[...])
             result[at:at + block, :] = total.astype(BF16)
             copy = pltpu.make_async_copy(
                 result.at[pl.ds(at, block)], out.at[pl.ds(at, block)], sem_out.at[g * 2 + p]
@@ -219,7 +208,7 @@
         copy.wait()
 
 
-def call(kernel, name, out_shape, scratch, flops, *args, limit=40 << 20, far=(), out_spec=None):
+def call(kernel, name, out_shape, scratch, flops, *args, limit=40 << 20, far=(), out_spec=None, aliases=None):
     vmem, hbm = pl.BlockSpec(memory_space=pltpu.VMEM), pl.BlockSpec(memory_space=pl.ANY)
     outs = jax.tree.leaves(out_shape)
     moved = sum(a.size * a.dtype.itemsize for a in args) + sum(o.size * o.dtype.itemsize for o in outs)
@@ -230,6 +219,7 @@
         in_specs=[hbm if n in far else vmem for n in range(len(args))],
         out_specs=jax.tree.map(lambda _: out_spec or vmem, out_shape),
         scratch_shapes=scratch,
+        input_output_aliases=aliases or {},
         compiler_params=pltpu.CompilerParams(vmem_limit_bytes=limit),
         cost_estimate=pl.CostEstimate(flops=flops, bytes_accessed=moved, transcendentals=0),
     )(*args)
@@ -270,19 +260,13 @@
     message = call(
         functools.partial(forward_kernel, low), "forward", jax.ShapeDtypeStruct((2 * low * PITCH, width), BF16),
         [
-            pltpu.VMEM((rows, width), BF16),
-            pltpu.VMEM((low, low), BF16),
-            pltpu.VMEM((mid, mid), BF16),
-            pltpu.VMEM((8, mid), F32),
-            pltpu.VMEM((low, mid), F32),
             padded,
             pltpu.VMEM((256, 256), BF16),
             pltpu.VMEM((2 * low * PITCH, width), BF16),
-            pltpu.SemaphoreType.DMA((8,)),
             pltpu.SemaphoreType.DMA((4,)),
         ], unit * (low + mid),
         values, factor_low, twist_low.T, factor_mid, twist_top, kernel_low,
-        limit=60 << 20, far=range(5), out_spec=pl.BlockSpec(memory_space=pl.ANY),
+        limit=60 << 20, out_spec=pl.BlockSpec(memory_space=pl.ANY),
     )
     message, untwist_t = lax.optimization_barrier((message, untwist_top))
     columns = lax.all_to_all(message.reshape(2 * low, PITCH, width), "seq", 0, 0, tiled=True)
@@ -310,21 +294,25 @@
     third, shares, out_weight = lax.optimization_barrier((third, shares, out_weight))
     shares = [swap(array, turn) if turn == 3 else array for turn, array in enumerate(shares)]
     weights = [swap(out_weight, turn) for turn in turns]
-    silu = call(
-        silu_kernel, "silu", jax.ShapeDtypeStruct((ch_count, share, width), BF16), [], unit, *shares, limit=12 << 20
+    silu, matrix = call(
+        gate_kernel, "gate",
+        [jax.ShapeDtypeStruct((share, columns_out), BF16), jax.ShapeDtypeStruct((ch_count * width, columns_out), BF16)],
+        [], unit, *shares, *weights, limit=12 << 20,
     )
     third = lax.all_to_all(third.reshape(top * ch_count, -1, width), ("seq", "ch"), 0, 0, tiled=True)
     return call(
         functools.partial(last_kernel, low), "last", jax.ShapeDtypeStruct((share, columns_out), BF16),
         [
+            pltpu.VMEM((share, columns_out), BF16),
             pltpu.VMEM((low * (width + 8), width), F32),
             pltpu.VMEM((share, columns_out), BF16),
             pltpu.VMEM((share, columns_out), BF16),
             pltpu.SemaphoreType.DMA((8,)),
+            pltpu.SemaphoreType.DMA((8,)),
         ],
         unit * low // 2 + 2 * share * columns_out ** 2,
-        third.reshape(rows, width), inverse_low, silu, *weights,
-        limit=24 << 20, out_spec=pl.BlockSpec(memory_space=pltpu.HBM),
+        third.reshape(rows, width), inverse_low, silu, matrix,
+        limit=24 << 20, far=(2,), out_spec=pl.BlockSpec(memory_space=pl.ANY), aliases={2: 0},
     )
 
 

time: 165 us -> 164 us (level)
  local copies, waits for them, and re-layouts: 13.2 us -> 10.5 us
    all_to_all x1, waiting for transfers between devices: 16.1 us -> 12.5 us  [local(): lax.all_to_all(third.reshape(top * ch_count, -1, width), ('seq', 'ch'), 0...]
    ppermute x6, waiting for transfers between devices: 42.3 us -> 45.7 us  [swap(): return lax.ppermute(array, 'ch', [(c, c ^ turn) for c in range(ch_count)])]
    unnamed x34 -> x30, local copies, waits for them, and re-layouts: 10.7 us -> 8.03 us
  transfers between devices with their start and end apart: 8 -> 8, of which waited for: 6 -> 5; matrix products, arithmetic and copies ran while one was open for 2% -> 2% of each run, Pallas kernels for 1% -> 2%
where the time goes in v5:
time: 164 us; the launch traced here: 163 us
  waiting for transfers between devices  83.6 us (51%)
  starting transfers between devices  50.9 us (31%)
  Pallas kernels  17.6 us (11%)
  local copies, waits for them, and re-layouts  10.5 us (6%)
    ppermute x6, waiting for transfers between devices, swap(): return lax.ppermute(array, 'ch', [(c, c ^ turn) for c in range(ch_count)])  45.7 us
    all_to_all x1, waiting for transfers between devices, local(): lax.all_to_all(message.reshape(2 * low, PITCH, width), 'seq', 0, 0, tiled...  25.5 us
    all_to_all x1, starting transfers between devices, local(): lax.all_to_all(message.reshape(2 * low, PITCH, width), 'seq', 0, 0, tiled...  20.8 us
    ppermute x6, starting transfers between devices, swap(): return lax.ppermute(array, 'ch', [(c, c ^ turn) for c in range(ch_count)])  19 us
    pallas_call x5, Pallas kernels, call(): pl.pallas_call(kernel, name=name, out_shape=out_shape, in_specs=[hbm if n...  17.6 us
    all_to_all x1, waiting for transfers between devices, local(): lax.all_to_all(third.reshape(top * ch_count, -1, width), ('seq', 'ch'), 0...  12.5 us
    all_to_all x1, starting transfers between devices, local(): lax.all_to_all(third.reshape(top * ch_count, -1, width), ('seq', 'ch'), 0...  11 us
    unnamed x30, local copies, waits for them, and re-layouts  8.03 us
  transfers between devices with their start and end apart: 8, of which 5 were waited for; matrix products, arithmetic and copies ran while one was open for 2% of the time, Pallas kernels for 2%

profile of v5, /device:TPU:1, one launch (start us, length us, event | category | flops | bytes accessed | tf_op | source)
XLA Modules:
  0.0 162.9 jit_solution(14956530928803305000)
XLA Ops:
  0.0 4.7 %forward.1 = bf16[9216,128]{1,0:T(8,128)(2,1)} custom-call(bf16[8192,128]{1,0:T(8,128)(2,1)} %values.1, bf16[64,64]{1,0:T(8,128)(2,1)} %factor_low.1, f32[64,128]{1,0:T(8,128)} %bitcast.11, bf16[128,128]{1,0:T(8,128)(2,1)} %factor_mid.1, f32[128,128]{1,0:T(8,128)} %twist_top.1, bf16[64,128]{1,0:T(8,128)(2,1)} %kernel_low.1), custom_call_target="tpu_custom_call" | custom-call | flops 402653184 | bytes 4612096 | tf_op jit(solution)/shard_map/forward/pallas_call | solution.py:215
  4.7 20.8 %all-to-all-start = ((bf16[128,72,128]{2,1,0:T(8,128)(2,1)}), bf16[128,72,128]{2,1,0:T(8,128)(2,1)S(1)}, u32[]{:S(2)}, u32[]{:S(2)}) async-start(bf16[128,72,128]{2,1,0:T(8,128)(2,1)} %bitcast.10), calls=%async_computation | async-start | bytes 4718592 | tf_op jit(solution)/shard_map/all_to_all | solution.py:272
  25.6 0.0 copy-start.9
  25.6 0.0 copy-start.10
  25.6 0.0 copy-start.11
  25.6 0.0 copy-start.12
  25.6 0.0 copy-start.13
  25.6 2.5 %constant_dynamic-slice_fusion = (bf16[2048,128]{1,0:T(8,128)(2,1)}, bf16[2048,128]{1,0:T(8,128)(2,1)S(1)}, bf16[2048,128]{1,0:T(8,128)(2,1)S(1)}, bf16[2048,128]{1,0:T(8,128)(2,1)S(1)}) fusion(bf16[8192,128]{1,0:T(8,128)(2,1)} %values.1, s32[]{:T(128)S(6)} %select_n.15, s32[]{:T(128)S(6)} %select_n.13, s32[]{:T(128)S(6)} %select_n.12, s32[]{:T(128)S(6)} %select_n.14), kind=kLoop, calls=%fused_computation | loop fusion | bytes 4194320 | tf_op jit(solution)/shard_map/dynamic_slice | solution.py:275
  28.1 0.0 copy-start.8
  28.1 3.0 %collective-permute-start = (bf16[2048,128]{1,0:T(8,128)(2,1)S(1)}, bf16[2048,128]{1,0:T(8,128)(2,1)S(1)}, u32[]{:S(2)}, u32[]{:S(2)}) collective-permute-start(bf16[2048,128]{1,0:T(8,128)(2,1)S(1)} %get-tuple-element.36), channel_id=1, source_target_pairs={{0,1},{1,0},{2,3},{3,2},{4,5},{5,4},{6,7},{7,6},{8,9},{9,8},{10,11... | collective-permute-start | bytes 1572872 | tf_op jit(solution)/shard_map/ppermute | solution.py:258
  31.1 2.2 %collective-permute-start.1 = (bf16[2048,128]{1,0:T(8,128)(2,1)S(1)}, bf16[2048,128]{1,0:T(8,128)(2,1)S(1)}, u32[]{:S(2)}, u32[]{:S(2)}) collective-permute-start(bf16[2048,128]{1,0:T(8,128)(2,1)S(1)} %get-tuple-element.38), channel_id=1, source_target_pairs={{0,2},{1,3},{2,0},{3,1},{4,6},{5,7},{6,4},{7,5},{8,10},{9,11},{10,... | collective-permute-start | bytes 1572872 | tf_op jit(solution)/shard_map/ppermute | solution.py:258
  33.3 0.0 copy-done.9
  33.4 0.0 copy-done.10
  33.4 0.0 copy-done.11
  33.4 0.0 copy-done.12
  33.4 0.0 copy-done.13
  33.4 1.4 pack.1.packed
  34.8 0.0 copy-start
  34.8 1.4 copy-done
  36.2 0.0 collective-permute-done.refs_1_
  36.2 21.9 %collective-permute-done.1.refs_2_ = bf16[2048,128]{1,0:T(8,128)(2,1)S(1)} collective-permute-done((bf16[2048,128]{1,0:T(8,128)(2,1)S(1)}, bf16[2048,128]{1,0:T(8,128)(2,1)S(1)}, u32[]{:S(2)}, u32[]{:S(2)}) %collective-permute-start.1) | collective-permute-done | bytes 524320 | tf_op jit(solution)/shard_map/ppermute | solution.py:258
  58.1 0.0 copy-start.3
  58.1 0.8 copy-done.3
  58.9 25.5 %all-to-all-done = bf16[128,72,128]{2,1,0:T(8,128)(2,1)S(1)} async-done(((bf16[128,72,128]{2,1,0:T(8,128)(2,1)}), bf16[128,72,128]{2,1,0:T(8,128)(2,1)S(1)}, u32[]{:S(2)}, u32[]{:S(2)}) %all-to-all-start) | async-done | bytes 2359328 | tf_op jit(solution)/shard_map/all_to_all | solution.py:272
  84.4 0.0 copy-done.8
  84.4 0.0 copy-start.1
  84.4 1.6 copy-done.1
  86.0 3.9 %middle.1 = bf16[8192,128]{1,0:T(8,128)(2,1)S(1)} custom-call(bf16[9216,128]{1,0:T(8,128)(2,1)S(1)} %bitcast.6, f32[128,128]{1,0:T(8,128)S(1)} %copy-done.8, bf16[8576,128]{1,0:T(8,128)(2,1)S(1)} %copy-done.1), custom_call_target="tpu_custom_call" | custom-call | flops 805306368 | bytes 6717440 | tf_op jit(solution)/shard_map/middle/pallas_call | solution.py:215
  89.9 0.0 copy-start.2
  89.9 1.3 copy-done.2
  91.2 0.0 copy-start.7
  91.2 0.0 copy-start.14
  91.3 11.0 %all-to-all-start.1 = ((bf16[512,16,128]{2,1,0:T(8,128)(2,1)}), bf16[512,16,128]{2,1,0:T(8,128)(2,1)S(1)}, u32[]{:S(2)}, u32[]{:S(2)}) async-start(bf16[512,16,128]{2,1,0:T(8,128)(2,1)} %bitcast.7), calls=%async_computation.1 | async-start | bytes 4194304 | tf_op jit(solution)/shard_map/all_to_all | solution.py:302
  102.3 3.5 %collective-permute-start.2 = (bf16[2048,128]{1,0:T(8,128)(2,1)}, bf16[2048,128]{1,0:T(8,128)(2,1)S(1)}, u32[]{:S(2)}, u32[]{:S(2)}) collective-permute-start(bf16[2048,128]{1,0:T(8,128)(2,1)} %get-tuple-element.31), channel_id=1, source_target_pairs={{0,3},{1,2},{2,1},{3,0},{4,7},{5,6},{6,5},{7,4},{8,11},{9,10},{10,... | collective-permute-start | bytes 1572872 | tf_op jit(solution)/shard_map/ppermute | solution.py:258
  105.8 0.0 copy-done.7
  105.8 2.0 %collective-permute-start.5 = (bf16[128,512]{1,0:T(8,128)(2,1)S(1)}, bf16[128,512]{1,0:T(8,128)(2,1)S(1)}, u32[]{:S(2)}, u32[]{:S(2)}) collective-permute-start(bf16[128,512]{1,0:T(8,128)(2,1)S(1)} %copy-done.7), channel_id=1, source_target_pairs={{0,3},{1,2},{2,1},{3,0},{4,7},{5,6},{6,5},{7,4},{8,11},{9,10},{10,... | collective-permute-start | bytes 393224 | tf_op jit(solution)/shard_map/ppermute | solution.py:258
  107.9 6.0 %collective-permute-start.4 = (bf16[128,512]{1,0:T(8,128)(2,1)S(1)}, bf16[128,512]{1,0:T(8,128)(2,1)S(1)}, u32[]{:S(2)}, u32[]{:S(2)}) collective-permute-start(bf16[128,512]{1,0:T(8,128)(2,1)S(1)} %copy-done.7), channel_id=1, source_target_pairs={{0,2},{1,3},{2,0},{3,1},{4,6},{5,7},{6,4},{7,5},{8,10},{9,11},{10,... | collective-permute-start | bytes 393224 | tf_op jit(solution)/shard_map/ppermute | solution.py:258
  113.8 2.3 %collective-permute-start.3 = (bf16[128,512]{1,0:T(8,128)(2,1)S(1)}, bf16[128,512]{1,0:T(8,128)(2,1)S(1)}, u32[]{:S(2)}, u32[]{:S(2)}) collective-permute-start(bf16[128,512]{1,0:T(8,128)(2,1)S(1)} %copy-done.7), channel_id=1, source_target_pairs={{0,1},{1,0},{2,3},{3,2},{4,5},{5,4},{6,7},{7,6},{8,9},{9,8},{10,11... | collective-permute-start | bytes 393224 | tf_op jit(solution)/shard_map/ppermute | solution.py:258
  116.1 14.7 %collective-permute-done.5.refs_7_ = bf16[128,512]{1,0:T(8,128)(2,1)S(1)} collective-permute-done((bf16[128,512]{1,0:T(8,128)(2,1)S(1)}, bf16[128,512]{1,0:T(8,128)(2,1)S(1)}, u32[]{:S(2)}, u32[]{:S(2)}) %collective-permute-start.5) | collective-permute-done | bytes 131104 | tf_op jit(solution)/shard_map/ppermute | solution.py:258
  130.9 9.0 %collective-permute-done.4.refs_6_ = bf16[128,512]{1,0:T(8,128)(2,1)S(1)} collective-permute-done((bf16[128,512]{1,0:T(8,128)(2,1)S(1)}, bf16[128,512]{1,0:T(8,128)(2,1)S(1)}, u32[]{:S(2)}, u32[]{:S(2)}) %collective-permute-start.4) | collective-permute-done | bytes 131104 | tf_op jit(solution)/shard_map/ppermute | solution.py:258
  139.9 0.0 collective-permute-done.3.refs_5_
  139.9 0.0 collective-permute-done.2.refs_3_
  139.9 0.0 copy-start.4
  139.9 1.0 copy-done.4
  140.9 2.5 %gate.1 = (bf16[2048,512]{1,0:T(8,128)(2,1)}, bf16[512,512]{1,0:T(8,128)(2,1)S(1)}) custom-call(bf16[2048,128]{1,0:T(8,128)(2,1)S(1)} %get-tuple-element.28.refs_0_, bf16[2048,128]{1,0:T(8,128)(2,1)S(1)} %collective-permute-done.refs_1_, bf16[2048,128]{1,0:T(8,128)(2,1)S(1)} %copy-done.4, bf16[2048,128]{1,0:T(8,128)(2,1)S(1)} %collective-permute-done.2.refs_3_, ...), custom_call_target="tpu_custom_call" | custom-call | flops 2097152 | bytes 5242880 | tf_op jit(solution)/shard_map/gate/pallas_call | solution.py:215
  143.4 0.0 copy-start.5
  143.4 0.8 copy-done.5
  144.2 12.5 %all-to-all-done.1 = bf16[512,16,128]{2,1,0:T(8,128)(2,1)S(1)} async-done(((bf16[512,16,128]{2,1,0:T(8,128)(2,1)}), bf16[512,16,128]{2,1,0:T(8,128)(2,1)S(1)}, u32[]{:S(2)}, u32[]{:S(2)}) %all-to-all-start.1) | async-done | bytes 2097184 | tf_op jit(solution)/shard_map/all_to_all | solution.py:302
  156.7 0.0 copy-done.14
  156.7 0.0 copy-start.6
  156.7 1.0 copy-done.6
  157.7 5.1 %last.1 = bf16[2048,512]{1,0:T(8,128)(2,1)} custom-call(bf16[8192,128]{1,0:T(8,128)(2,1)S(1)} %bitcast.8, bf16[64,64]{1,0:T(8,128)(2,1)S(1)} %copy-done.14, bf16[2048,512]{1,0:T(8,128)(2,1)} %get-tuple-element.33.silu, bf16[512,512]{1,0:T(8,128)(2,1)S(1)} %copy-done.6), custom_call_target="tpu_custom_call", output_to_operand_aliasing={{}: (2, {})} | custom-call | flops 1140850688 | bytes 6823936 | tf_op jit(solution)/shard_map/last/pallas_call | solution.py:215
Async XLA Ops:
  4.7 79.6 %all-to-all-start = ((bf16[128,72,128]{2,1,0:T(8,128)(2,1)}), bf16[128,72,128]{2,1,0:T(8,128)(2,1)S(1)}, u32[]{:S(2)}, u32[]{:S(2)}) async-start(bf16[128,72,128]{2,1,0:T(8,128)(2,1)} %bitcast.10), calls=%async_computation | async-start | bytes 4718592 | tf_op jit(solution)/shard_map/all_to_all | solution.py:272
  25.6 7.8 %copy-start.9 = (f32[128,128]{1,0:T(8,128)S(1)}, f32[128,128]{1,0:T(8,128)}, u32[]{:S(2)}) copy-start(f32[128,128]{1,0:T(8,128)} %untwist_top) | copy-start | bytes 196612
  25.6 7.8 %copy-start.10 = (bf16[128,128]{1,0:T(8,128)(2,1)S(1)}, bf16[128,128]{1,0:T(8,128)(2,1)}, u32[]{:S(2)}) copy-start(bf16[128,128]{1,0:T(8,128)(2,1)} %factor_top.1) | copy-start | bytes 98308
  25.6 7.8 %copy-start.11 = (bf16[128,128]{1,0:T(8,128)(2,1)S(1)}, bf16[128,128]{1,0:T(8,128)(2,1)}, u32[]{:S(2)}) copy-start(bf16[128,128]{1,0:T(8,128)(2,1)} %inverse_top.1) | copy-start | bytes 98308
  25.6 7.8 %copy-start.12 = (bf16[128,128]{1,0:T(8,128)(2,1)S(1)}, bf16[128,128]{1,0:T(8,128)(2,1)}, u32[]{:S(2)}) copy-start(bf16[128,128]{1,0:T(8,128)(2,1)} %inverse_mid.1) | copy-start | bytes 98308
  25.6 7.8 %copy-start.13 = (f32[128,64]{0,1:T(8,128)S(1)}, f32[128,64]{0,1:T(8,128)}, u32[]{:S(2)}) copy-start(f32[128,64]{0,1:T(8,128)} %param.25) | copy-start | bytes 98308
  28.1 56.2 %copy-start.8 = (f32[128,128]{1,0:T(8,128)S(1)}, f32[128,128]{1,0:T(8,128)}, u32[]{:S(2)}) copy-start(f32[128,128]{1,0:T(8,128)} %kernel_top.1) | copy-start | bytes 196612
  28.1 8.0 %collective-permute-start = (bf16[2048,128]{1,0:T(8,128)(2,1)S(1)}, bf16[2048,128]{1,0:T(8,128)(2,1)S(1)}, u32[]{:S(2)}, u32[]{:S(2)}) collective-permute-start(bf16[2048,128]{1,0:T(8,128)(2,1)S(1)} %get-tuple-element.36), channel_id=1, source_target_pairs={{0,1},{1,0},{2,3},{3,2},{4,5},{5,4},{6,7},{7,6},{8,9},{9,8},{10,11... | collective-permute-start | bytes 1572872 | tf_op jit(solution)/shard_map/ppermute | solution.py:258
  31.1 27.0 %collective-permute-start.1 = (bf16[2048,128]{1,0:T(8,128)(2,1)S(1)}, bf16[2048,128]{1,0:T(8,128)(2,1)S(1)}, u32[]{:S(2)}, u32[]{:S(2)}) collective-permute-start(bf16[2048,128]{1,0:T(8,128)(2,1)S(1)} %get-tuple-element.38), channel_id=1, source_target_pairs={{0,2},{1,3},{2,0},{3,1},{4,6},{5,7},{6,4},{7,5},{8,10},{9,11},{10,... | collective-permute-start | bytes 1572872 | tf_op jit(solution)/shard_map/ppermute | solution.py:258
  34.8 1.4 copy-start
  58.1 0.8 copy-start.3
  84.4 1.6 copy-start.1
  89.9 1.3 copy-start.2
  91.2 14.6 %copy-start.7 = (bf16[128,512]{1,0:T(8,128)(2,1)S(1)}, bf16[128,512]{1,0:T(8,128)(2,1)}, u32[]{:S(2)}) copy-start(bf16[128,512]{1,0:T(8,128)(2,1)} %refs_4_) | copy-start | bytes 393220
  91.2 65.4 %copy-start.14 = (bf16[64,64]{1,0:T(8,128)(2,1)S(1)}, bf16[64,64]{1,0:T(8,128)(2,1)}, u32[]{:S(2)}) copy-start(bf16[64,64]{1,0:T(8,128)(2,1)} %inverse_low.1) | copy-start | bytes 24580
  91.3 65.4 %all-to-all-start.1 = ((bf16[512,16,128]{2,1,0:T(8,128)(2,1)}), bf16[512,16,128]{2,1,0:T(8,128)(2,1)S(1)}, u32[]{:S(2)}, u32[]{:S(2)}) async-start(bf16[512,16,128]{2,1,0:T(8,128)(2,1)} %bitcast.7), calls=%async_computation.1 | async-start | bytes 4194304 | tf_op jit(solution)/shard_map/all_to_all | solution.py:302
  102.3 37.6 %collective-permute-start.2 = (bf16[2048,128]{1,0:T(8,128)(2,1)}, bf16[2048,128]{1,0:T(8,128)(2,1)S(1)}, u32[]{:S(2)}, u32[]{:S(2)}) collective-permute-start(bf16[2048,128]{1,0:T(8,128)(2,1)} %get-tuple-element.31), channel_id=1, source_target_pairs={{0,3},{1,2},{2,1},{3,0},{4,7},{5,6},{6,5},{7,4},{8,11},{9,10},{10,... | collective-permute-start | bytes 1572872 | tf_op jit(solution)/shard_map/ppermute | solution.py:258
  105.8 25.0 %collective-permute-start.5 = (bf16[128,512]{1,0:T(8,128)(2,1)S(1)}, bf16[128,512]{1,0:T(8,128)(2,1)S(1)}, u32[]{:S(2)}, u32[]{:S(2)}) collective-permute-start(bf16[128,512]{1,0:T(8,128)(2,1)S(1)} %copy-done.7), channel_id=1, source_target_pairs={{0,3},{1,2},{2,1},{3,0},{4,7},{5,6},{6,5},{7,4},{8,11},{9,10},{10,... | collective-permute-start | bytes 393224 | tf_op jit(solution)/shard_map/ppermute | solution.py:258
  107.9 32.0 %collective-permute-start.4 = (bf16[128,512]{1,0:T(8,128)(2,1)S(1)}, bf16[128,512]{1,0:T(8,128)(2,1)S(1)}, u32[]{:S(2)}, u32[]{:S(2)}) collective-permute-start(bf16[128,512]{1,0:T(8,128)(2,1)S(1)} %copy-done.7), channel_id=1, source_target_pairs={{0,2},{1,3},{2,0},{3,1},{4,6},{5,7},{6,4},{7,5},{8,10},{9,11},{10,... | collective-permute-start | bytes 393224 | tf_op jit(solution)/shard_map/ppermute | solution.py:258
  113.8 26.1 %collective-permute-start.3 = (bf16[128,512]{1,0:T(8,128)(2,1)S(1)}, bf16[128,512]{1,0:T(8,128)(2,1)S(1)}, u32[]{:S(2)}, u32[]{:S(2)}) collective-permute-start(bf16[128,512]{1,0:T(8,128)(2,1)S(1)} %copy-done.7), channel_id=1, source_target_pairs={{0,1},{1,0},{2,3},{3,2},{4,5},{5,4},{6,7},{7,6},{8,9},{9,8},{10,11... | collective-permute-start | bytes 393224 | tf_op jit(solution)/shard_map/ppermute | solution.py:258
  139.9 1.0 copy-start.4
  143.4 0.8 copy-start.5
  156.7 1.0 copy-start.6

commit v6 on v5

--- a/solution.py
+++ b/solution.py
@@ -273,12 +273,18 @@
 
     turns = range(ch_count)
     shares = [lax.dynamic_slice_in_dim(values, (ch_place ^ turn) * share, share, 0) for turn in turns]
-    shares = [swap(array, turn) if turn < 3 else array for turn, array in enumerate(shares)]
+    shares = [swap(array, turn) for turn, array in enumerate(shares)]
+    weights = [swap(out_weight, turn) for turn in turns]
+    silu, matrix = call(
+        gate_kernel, "gate",
+        [jax.ShapeDtypeStruct((share, columns_out), BF16), jax.ShapeDtypeStruct((ch_count * width, columns_out), BF16)],
+        [], unit, *shares, *weights, limit=12 << 20,
+    )
     packed = call(
         pack_kernel, "pack", jax.ShapeDtypeStruct(((HALF + 3) * top, width), BF16), [], unit,
         untwist_t, factor_top, inverse_top, inverse_mid, untwist_low.T, limit=8 << 20,
     )
-    columns, shares = lax.optimization_barrier((columns, shares))
+    columns, silu, matrix = lax.optimization_barrier((columns, silu, matrix))
     third = call(
         middle_kernel, "middle", jax.ShapeDtypeStruct((rows, width), BF16),
         [
@@ -290,14 +296,6 @@
             pltpu.SemaphoreType.DMA((4,)),
         ], unit * (2 * top + mid),
         columns.reshape(top * PITCH, width), kernel_top, packed, limit=24 << 20, out_spec=pl.BlockSpec(memory_space=pltpu.HBM),
-    )
-    third, shares, out_weight = lax.optimization_barrier((third, shares, out_weight))
-    shares = [swap(array, turn) if turn == 3 else array for turn, array in enumerate(shares)]
-    weights = [swap(out_weight, turn) for turn in turns]
-    silu, matrix = call(
-        gate_kernel, "gate",
-        [jax.ShapeDtypeStruct((share, columns_out), BF16), jax.ShapeDtypeStruct((ch_count * width, columns_out), BF16)],
-        [], unit, *shares, *weights, limit=12 << 20,
     )
     third = lax.all_to_all(third.reshape(top * ch_count, -1, width), ("seq", "ch"), 0, 0, tiled=True)
     return call(

time: 164 us -> 172 us (1.049)
  blocking collectives: 0 us -> 71.3 us
  waiting for transfers between devices: 83.6 us -> 40.4 us
  starting transfers between devices: 50.9 us -> 36.9 us
  local copies, waits for them, and re-layouts: 10.5 us -> 4.77 us
    all_to_all x0 -> x1, blocking collectives: none -> 71.3 us  [local(): lax.all_to_all(third.reshape(top * ch_count, -1, width), ('seq', 'ch'), 0...]
    all_to_all x1, waiting for transfers between devices: 25.5 us -> 0.01 us  [local(): lax.all_to_all(message.reshape(2 * low, PITCH, width), 'seq', 0, 0, tiled...]
    all_to_all x1 -> x0, waiting for transfers between devices: 12.5 us -> none  [local(): lax.all_to_all(third.reshape(top * ch_count, -1, width), ('seq', 'ch'), 0...]
    all_to_all x1 -> x0, starting transfers between devices: 11 us -> none  [local(): lax.all_to_all(third.reshape(top * ch_count, -1, width), ('seq', 'ch'), 0...]
    ppermute x6, waiting for transfers between devices: 45.7 us -> 40.4 us  [swap(): return lax.ppermute(array, 'ch', [(c, c ^ turn) for c in range(ch_count)])]
    unnamed x30 -> x20, local copies, waits for them, and re-layouts: 8.03 us -> 3.03 us
    ppermute x6, starting transfers between devices: 19 us -> 16.1 us  [swap(): return lax.ppermute(array, 'ch', [(c, c ^ turn) for c in range(ch_count)])]
  transfers between devices with their start and end apart: 8 -> 7, of which waited for: 5 -> 2; matrix products, arithmetic and copies ran while one was open for 2% -> 1% of each run, Pallas kernels for 2% -> 2%
where the time goes in v6:
time: 172 us; the launch traced here: 171 us
  blocking collectives  71.3 us (41%)
  waiting for transfers between devices  40.4 us (23%)
  starting transfers between devices  36.9 us (21%)
  Pallas kernels  17.6 us (10%)
  local copies, waits for them, and re-layouts  4.77 us (3%)
    all_to_all x1, blocking collectives, local(): lax.all_to_all(third.reshape(top * ch_count, -1, width), ('seq', 'ch'), 0...  71.3 us
    ppermute x6, waiting for transfers between devices, swap(): return lax.ppermute(array, 'ch', [(c, c ^ turn) for c in range(ch_count)])  40.4 us
    all_to_all x1, starting transfers between devices, local(): lax.all_to_all(message.reshape(2 * low, PITCH, width), 'seq', 0, 0, tiled...  20.8 us
    pallas_call x5, Pallas kernels, call(): pl.pallas_call(kernel, name=name, out_shape=out_shape, in_specs=[hbm if n...  17.6 us
    ppermute x6, starting transfers between devices, swap(): return lax.ppermute(array, 'ch', [(c, c ^ turn) for c in range(ch_count)])  16.1 us
  transfers between devices with their start and end apart: 7, of which 2 were waited for; matrix products, arithmetic and copies ran while one was open for 1% of the time, Pallas kernels for 2%

profile of v6, /device:TPU:1, one launch (start us, length us, event | category | flops | bytes accessed | tf_op | source)
XLA Modules:
  0.0 171.3 jit_solution(1017258275814384673)
XLA Ops:
  0.0 4.7 %forward.1 = bf16[9216,128]{1,0:T(8,128)(2,1)} custom-call(bf16[8192,128]{1,0:T(8,128)(2,1)} %values.1, bf16[64,64]{1,0:T(8,128)(2,1)} %factor_low.1, f32[64,128]{1,0:T(8,128)} %bitcast.11, bf16[128,128]{1,0:T(8,128)(2,1)} %factor_mid.1, f32[128,128]{1,0:T(8,128)} %twist_top.1, bf16[64,128]{1,0:T(8,128)(2,1)} %kernel_low.1), custom_call_target="tpu_custom_call" | custom-call | flops 402653184 | bytes 4612096 | tf_op jit(solution)/shard_map/forward/pallas_call | solution.py:215
  4.7 20.8 %all-to-all-start = ((bf16[128,72,128]{2,1,0:T(8,128)(2,1)}), bf16[128,72,128]{2,1,0:T(8,128)(2,1)S(1)}, u32[]{:S(2)}, u32[]{:S(2)}) async-start(bf16[128,72,128]{2,1,0:T(8,128)(2,1)} %bitcast.10), calls=%async_computation | async-start | bytes 4718592 | tf_op jit(solution)/shard_map/all_to_all | solution.py:272
  25.6 0.0 copy-start.2
  25.6 0.0 copy-start.4
  25.6 0.0 copy-start.5
  25.6 0.0 copy-start.6
  25.6 0.0 copy-start.7
  25.6 0.0 copy-start.8
  25.6 1.7 %constant_dynamic-slice_fusion = (bf16[2048,128]{1,0:T(8,128)(2,1)S(1)}, bf16[2048,128]{1,0:T(8,128)(2,1)S(1)}, bf16[2048,128]{1,0:T(8,128)(2,1)S(1)}, bf16[2048,128]{1,0:T(8,128)(2,1)S(1)}) fusion(bf16[8192,128]{1,0:T(8,128)(2,1)} %values.1, s32[]{:T(128)S(6)} %select_n.15, s32[]{:T(128)S(6)} %select_n.13, s32[]{:T(128)S(6)} %select_n.12, s32[]{:T(128)S(6)} %select_n.14), kind=kLoop, calls=%fused_computation | loop fusion | bytes 4194320 | tf_op jit(solution)/shard_map/dynamic_slice | solution.py:275
  27.4 3.1 %collective-permute-start.2 = (bf16[2048,128]{1,0:T(8,128)(2,1)S(1)}, bf16[2048,128]{1,0:T(8,128)(2,1)S(1)}, u32[]{:S(2)}, u32[]{:S(2)}) collective-permute-start(bf16[2048,128]{1,0:T(8,128)(2,1)S(1)} %get-tuple-element.19), channel_id=1, source_target_pairs={{0,3},{1,2},{2,1},{3,0},{4,7},{5,6},{6,5},{7,4},{8,11},{9,10},{10,... | collective-permute-start | bytes 1572872 | tf_op jit(solution)/shard_map/ppermute | solution.py:258
  30.5 1.9 %collective-permute-start = (bf16[2048,128]{1,0:T(8,128)(2,1)S(1)}, bf16[2048,128]{1,0:T(8,128)(2,1)S(1)}, u32[]{:S(2)}, u32[]{:S(2)}) collective-permute-start(bf16[2048,128]{1,0:T(8,128)(2,1)S(1)} %get-tuple-element.20), channel_id=1, source_target_pairs={{0,1},{1,0},{2,3},{3,2},{4,5},{5,4},{6,7},{7,6},{8,9},{9,8},{10,11... | collective-permute-start | bytes 1572872 | tf_op jit(solution)/shard_map/ppermute | solution.py:258
  32.4 3.1 %collective-permute-start.1 = (bf16[2048,128]{1,0:T(8,128)(2,1)S(1)}, bf16[2048,128]{1,0:T(8,128)(2,1)S(1)}, u32[]{:S(2)}, u32[]{:S(2)}) collective-permute-start(bf16[2048,128]{1,0:T(8,128)(2,1)S(1)} %get-tuple-element.22), channel_id=1, source_target_pairs={{0,2},{1,3},{2,0},{3,1},{4,6},{5,7},{6,4},{7,5},{8,10},{9,11},{10,... | collective-permute-start | bytes 1572872 | tf_op jit(solution)/shard_map/ppermute | solution.py:258
  35.5 0.0 copy-done.2
  35.5 2.2 %collective-permute-start.4 = (bf16[128,512]{1,0:T(8,128)(2,1)S(1)}, bf16[128,512]{1,0:T(8,128)(2,1)S(1)}, u32[]{:S(2)}, u32[]{:S(2)}) collective-permute-start(bf16[128,512]{1,0:T(8,128)(2,1)S(1)} %copy-done.2), channel_id=1, source_target_pairs={{0,2},{1,3},{2,0},{3,1},{4,6},{5,7},{6,4},{7,5},{8,10},{9,11},{10,... | collective-permute-start | bytes 393224 | tf_op jit(solution)/shard_map/ppermute | solution.py:258
  37.7 3.0 %collective-permute-start.3 = (bf16[128,512]{1,0:T(8,128)(2,1)S(1)}, bf16[128,512]{1,0:T(8,128)(2,1)S(1)}, u32[]{:S(2)}, u32[]{:S(2)}) collective-permute-start(bf16[128,512]{1,0:T(8,128)(2,1)S(1)} %copy-done.2), channel_id=1, source_target_pairs={{0,1},{1,0},{2,3},{3,2},{4,5},{5,4},{6,7},{7,6},{8,9},{9,8},{10,11... | collective-permute-start | bytes 393224 | tf_op jit(solution)/shard_map/ppermute | solution.py:258
  40.7 38.8 %collective-permute-done.4.refs_6_ = bf16[128,512]{1,0:T(8,128)(2,1)S(1)} collective-permute-done((bf16[128,512]{1,0:T(8,128)(2,1)S(1)}, bf16[128,512]{1,0:T(8,128)(2,1)S(1)}, u32[]{:S(2)}, u32[]{:S(2)}) %collective-permute-start.4) | collective-permute-done | bytes 131104 | tf_op jit(solution)/shard_map/ppermute | solution.py:258
  79.5 2.9 %collective-permute-start.5 = (bf16[128,512]{1,0:T(8,128)(2,1)S(1)}, bf16[128,512]{1,0:T(8,128)(2,1)S(1)}, u32[]{:S(2)}, u32[]{:S(2)}) collective-permute-start(bf16[128,512]{1,0:T(8,128)(2,1)S(1)} %copy-done.2), channel_id=1, source_target_pairs={{0,3},{1,2},{2,1},{3,0},{4,7},{5,6},{6,5},{7,4},{8,11},{9,10},{10,... | collective-permute-start | bytes 393224 | tf_op jit(solution)/shard_map/ppermute | solution.py:258
  82.4 0.0 copy-done.4
  82.4 0.0 copy-done.5
  82.4 0.0 copy-done.6
  82.4 0.0 copy-done.7
  82.4 0.0 copy-done.8
  82.4 0.0 copy-start.3
  82.5 1.4 pack.1.packed
  83.8 0.0 copy-start
  83.9 1.4 copy-done
  85.2 0.0 collective-permute-done.3.refs_5_
  85.2 1.5 collective-permute-done.5.refs_7_
  86.7 0.0 collective-permute-done.2.refs_3_
  86.7 0.0 collective-permute-done.refs_1_
  86.7 0.0 collective-permute-done.1.refs_2_
  86.7 2.5 %gate.1 = (bf16[2048,512]{1,0:T(8,128)(2,1)}, bf16[512,512]{1,0:T(8,128)(2,1)S(1)}) custom-call(bf16[2048,128]{1,0:T(8,128)(2,1)S(1)} %get-tuple-element.21.refs_0_, bf16[2048,128]{1,0:T(8,128)(2,1)S(1)} %collective-permute-done.refs_1_, bf16[2048,128]{1,0:T(8,128)(2,1)S(1)} %collective-permute-done.1.refs_2_, ...), custom_call_target="tpu_custom_call" | custom-call | flops 2097152 | bytes 5242880 | tf_op jit(solution)/shard_map/gate/pallas_call | solution.py:215
  89.2 0.0 all-to-all-done
  89.2 0.0 copy-done.3
  89.2 0.0 copy-start.1
  89.2 1.6 copy-done.1
  90.8 3.9 %middle.1 = bf16[8192,128]{1,0:T(8,128)(2,1)S(1)} custom-call(bf16[9216,128]{1,0:T(8,128)(2,1)S(1)} %bitcast.6, f32[128,128]{1,0:T(8,128)S(1)} %copy-done.3, bf16[8576,128]{1,0:T(8,128)(2,1)S(1)} %copy-done.1), custom_call_target="tpu_custom_call" | custom-call | flops 805306368 | bytes 6717440 | tf_op jit(solution)/shard_map/middle/pallas_call | solution.py:215
  94.8 0.0 copy-start.9
  94.8 71.3 %all_to_all.10 = bf16[512,16,128]{2,1,0:T(8,128)(2,1)S(1)} all-to-all(bf16[512,16,128]{2,1,0:T(8,128)(2,1)S(1)} %bitcast.7), channel_id=1, replica_groups=mesh['seq'=128,'ch'=4] {'seq','ch'}, dimensions={0} | all-to-all | bytes 4194304 | tf_op jit(solution)/shard_map/all_to_all | solution.py:300
  166.1 0.0 copy-done.9
  166.1 5.1 %last.1 = bf16[2048,512]{1,0:T(8,128)(2,1)} custom-call(bf16[8192,128]{1,0:T(8,128)(2,1)S(1)} %bitcast.8, bf16[64,64]{1,0:T(8,128)(2,1)S(1)} %copy-done.9, bf16[2048,512]{1,0:T(8,128)(2,1)} %get-tuple-element.17.silu, bf16[512,512]{1,0:T(8,128)(2,1)S(1)} %get-tuple-element.18.matrix), custom_call_target="tpu_custom_call", output_to_operand_aliasing={{}: (2, {})} | custom-call | flops 1140850688 | bytes 6823936 | tf_op jit(solution)/shard_map/last/pallas_call | solution.py:215
Async XLA Ops:
  4.7 84.5 %all-to-all-start = ((bf16[128,72,128]{2,1,0:T(8,128)(2,1)}), bf16[128,72,128]{2,1,0:T(8,128)(2,1)S(1)}, u32[]{:S(2)}, u32[]{:S(2)}) async-start(bf16[128,72,128]{2,1,0:T(8,128)(2,1)} %bitcast.10), calls=%async_computation | async-start | bytes 4718592 | tf_op jit(solution)/shard_map/all_to_all | solution.py:272
  25.6 9.9 %copy-start.2 = (bf16[128,512]{1,0:T(8,128)(2,1)S(1)}, bf16[128,512]{1,0:T(8,128)(2,1)}, u32[]{:S(2)}) copy-start(bf16[128,512]{1,0:T(8,128)(2,1)} %refs_4_.1) | copy-start | bytes 393220
  25.6 56.8 %copy-start.4 = (f32[128,128]{1,0:T(8,128)S(1)}, f32[128,128]{1,0:T(8,128)}, u32[]{:S(2)}) copy-start(f32[128,128]{1,0:T(8,128)} %untwist_top) | copy-start | bytes 196612
  25.6 56.8 %copy-start.5 = (bf16[128,128]{1,0:T(8,128)(2,1)S(1)}, bf16[128,128]{1,0:T(8,128)(2,1)}, u32[]{:S(2)}) copy-start(bf16[128,128]{1,0:T(8,128)(2,1)} %factor_top.1) | copy-start | bytes 98308
  25.6 56.8 %copy-start.6 = (bf16[128,128]{1,0:T(8,128)(2,1)S(1)}, bf16[128,128]{1,0:T(8,128)(2,1)}, u32[]{:S(2)}) copy-start(bf16[128,128]{1,0:T(8,128)(2,1)} %inverse_top.1) | copy-start | bytes 98308
  25.6 56.8 %copy-start.7 = (bf16[128,128]{1,0:T(8,128)(2,1)S(1)}, bf16[128,128]{1,0:T(8,128)(2,1)}, u32[]{:S(2)}) copy-start(bf16[128,128]{1,0:T(8,128)(2,1)} %inverse_mid.1) | copy-start | bytes 98308
  25.6 56.8 %copy-start.8 = (f32[128,64]{0,1:T(8,128)S(1)}, f32[128,64]{0,1:T(8,128)}, u32[]{:S(2)}) copy-start(f32[128,64]{0,1:T(8,128)} %param.25) | copy-start | bytes 98308
  27.4 59.3 %collective-permute-start.2 = (bf16[2048,128]{1,0:T(8,128)(2,1)S(1)}, bf16[2048,128]{1,0:T(8,128)(2,1)S(1)}, u32[]{:S(2)}, u32[]{:S(2)}) collective-permute-start(bf16[2048,128]{1,0:T(8,128)(2,1)S(1)} %get-tuple-element.19), channel_id=1, source_target_pairs={{0,3},{1,2},{2,1},{3,0},{4,7},{5,6},{6,5},{7,4},{8,11},{9,10},{10,... | collective-permute-start | bytes 1572872 | tf_op jit(solution)/shard_map/ppermute | solution.py:258
  30.5 56.3 %collective-permute-start = (bf16[2048,128]{1,0:T(8,128)(2,1)S(1)}, bf16[2048,128]{1,0:T(8,128)(2,1)S(1)}, u32[]{:S(2)}, u32[]{:S(2)}) collective-permute-start(bf16[2048,128]{1,0:T(8,128)(2,1)S(1)} %get-tuple-element.20), channel_id=1, source_target_pairs={{0,1},{1,0},{2,3},{3,2},{4,5},{5,4},{6,7},{7,6},{8,9},{9,8},{10,11... | collective-permute-start | bytes 1572872 | tf_op jit(solution)/shard_map/ppermute | solution.py:258
  32.4 54.4 %collective-permute-start.1 = (bf16[2048,128]{1,0:T(8,128)(2,1)S(1)}, bf16[2048,128]{1,0:T(8,128)(2,1)S(1)}, u32[]{:S(2)}, u32[]{:S(2)}) collective-permute-start(bf16[2048,128]{1,0:T(8,128)(2,1)S(1)} %get-tuple-element.22), channel_id=1, source_target_pairs={{0,2},{1,3},{2,0},{3,1},{4,6},{5,7},{6,4},{7,5},{8,10},{9,11},{10,... | collective-permute-start | bytes 1572872 | tf_op jit(solution)/shard_map/ppermute | solution.py:258
  35.5 44.0 %collective-permute-start.4 = (bf16[128,512]{1,0:T(8,128)(2,1)S(1)}, bf16[128,512]{1,0:T(8,128)(2,1)S(1)}, u32[]{:S(2)}, u32[]{:S(2)}) collective-permute-start(bf16[128,512]{1,0:T(8,128)(2,1)S(1)} %copy-done.2), channel_id=1, source_target_pairs={{0,2},{1,3},{2,0},{3,1},{4,6},{5,7},{6,4},{7,5},{8,10},{9,11},{10,... | collective-permute-start | bytes 393224 | tf_op jit(solution)/shard_map/ppermute | solution.py:258
  37.7 47.5 %collective-permute-start.3 = (bf16[128,512]{1,0:T(8,128)(2,1)S(1)}, bf16[128,512]{1,0:T(8,128)(2,1)S(1)}, u32[]{:S(2)}, u32[]{:S(2)}) collective-permute-start(bf16[128,512]{1,0:T(8,128)(2,1)S(1)} %copy-done.2), channel_id=1, source_target_pairs={{0,1},{1,0},{2,3},{3,2},{4,5},{5,4},{6,7},{7,6},{8,9},{9,8},{10,11... | collective-permute-start | bytes 393224 | tf_op jit(solution)/shard_map/ppermute | solution.py:258
  79.5 7.2 %collective-permute-start.5 = (bf16[128,512]{1,0:T(8,128)(2,1)S(1)}, bf16[128,512]{1,0:T(8,128)(2,1)S(1)}, u32[]{:S(2)}, u32[]{:S(2)}) collective-permute-start(bf16[128,512]{1,0:T(8,128)(2,1)S(1)} %copy-done.2), channel_id=1, source_target_pairs={{0,3},{1,2},{2,1},{3,0},{4,7},{5,6},{6,5},{7,4},{8,11},{9,10},{10,... | collective-permute-start | bytes 393224 | tf_op jit(solution)/shard_map/ppermute | solution.py:258
  82.4 6.8 %copy-start.3 = (f32[128,128]{1,0:T(8,128)S(1)}, f32[128,128]{1,0:T(8,128)}, u32[]{:S(2)}) copy-start(f32[128,128]{1,0:T(8,128)} %kernel_top.1) | copy-start | bytes 196612
  83.8 1.4 copy-start
  89.2 1.6 copy-start.1
  94.8 71.3 %copy-start.9 = (bf16[64,64]{1,0:T(8,128)(2,1)S(1)}, bf16[64,64]{1,0:T(8,128)(2,1)}, u32[]{:S(2)}) copy-start(bf16[64,64]{1,0:T(8,128)(2,1)} %inverse_low.1) | copy-start | bytes 24580

commit v7 on v5

--- a/solution.py
+++ b/solution.py
@@ -81,23 +81,30 @@
         store.wait()
 
 
-def middle_kernel(columns, kernel_top, packed, third,
-                  out, rows_f, rows_g, whole, lines, sem_out):
-    top = kernel_top.shape[0]
-    factor_top, inverse_top, inverse_mid = (packed.at[pl.ds((HALF + n) * top, top)] for n in range(3))
-    place = lax.axis_index("seq")
+def middle_kernel(columns, packed, spread, third, spread_out,
+                  scale, out, rows_f, rows_g, whole, lines, sem_in, sem_out):
+    top = packed.shape[1]
+    factor_top, inverse_top, inverse_mid = (packed.at[pl.ds(n * top, top)] for n in range(3))
+    chunk = HALF // 8 * top
+    loads = [
+        pltpu.make_async_copy(spread.at[pl.ds(n * chunk, chunk)], scale.at[pl.ds(n * chunk, chunk)], sem_in.at[n])
+        for n in range(2)
+    ]
+    for copy in loads:
+        copy.start()
     for n in range(top // 8):
         at = n * 8 * PITCH
         rows_f[at:at + 8 * PITCH, :] = columns[at:at + 8 * PITCH, :].astype(F32)
     rows = rows_f[pl.ds(HALF, 2 * HALF, stride=PITCH), :]
     lines[...] = trade_halves(rows[:HALF], rows[HALF:])[0]
-    lower = iota((top, LANES), 1) < HALF
-    all_top = kernel_top[...]
-    turned = pltpu.roll(all_top, HALF, 1)
-    keep = lower == (lax.rem(place, 2) == 0)
-    whole[...] = jnp.where(keep, all_top, turned)
+    whole[...] = packed[3 * top:, :].astype(F32)
+
+    def scale_of(r):
+        return scale[r // 4 * top:(r // 4 + 1) * top, r % 4 * LANES:(r % 4 + 1) * LANES].astype(F32)
 
     for r in range(0, HALF, 2):
+        if r % 32 == 0:
+            loads[r // 32].wait()
         one = rows_f[pl.ds(r, top, stride=PITCH), :].astype(BF16)
         two = rows_f[pl.ds(r + 1, top, stride=PITCH), :].astype(BF16)
         spectrum = dot(factor_top[...], jnp.concatenate([one, two], axis=1)).astype(BF16).astype(F32)
@@ -105,8 +112,8 @@
         other = spectrum[:, LANES:] * whole[...] * lines[r + 1:r + 2, :]
         filtered = jnp.concatenate([first.astype(BF16), other.astype(BF16)], axis=1)
         back = dot(inverse_top[...], filtered)
-        rows_g[pl.ds(r, top, stride=PITCH), :] = back[:, :LANES] * packed[r * top:(r + 1) * top, :].astype(F32)
-        rows_g[pl.ds(r + 1, top, stride=PITCH), :] = back[:, LANES:] * packed[(r + 1) * top:(r + 2) * top, :].astype(F32)
+        rows_g[pl.ds(r, top, stride=PITCH), :] = back[:, :LANES] * scale_of(r)
+        rows_g[pl.ds(r + 1, top, stride=PITCH), :] = back[:, LANES:] * scale_of(r + 1)
 
     part = 32 * HALF
     stores = []
@@ -133,7 +140,7 @@
         store.wait()
 
 
-def pack_kernel(untwist_top, factor_top, inverse_top, inverse_mid, untwist_low, packed):
+def pack_kernel(untwist_top, factor_top, inverse_top, inverse_mid, untwist_low, kernel_top, packed, spread):
     top = untwist_top.shape[0]
     place = lax.axis_index("seq")
     shape = (top, LANES)
@@ -141,16 +148,18 @@
     for r in range(HALF):
         one = jnp.broadcast_to(untwist_top[:, r:r + 1], shape)
         two = jnp.broadcast_to(untwist_top[:, HALF + r:HALF + r + 1], shape)
-        packed[r * top:(r + 1) * top, :] = jnp.where(lower, one, two).astype(BF16)
-    at = HALF * top
-    packed[at:at + top, :] = factor_top[...]
-    packed[at + top:at + 2 * top, :] = inverse_top[...]
+        at, side = r // 4 * top, r % 4 * LANES
+        spread[at:at + top, side:side + LANES] = jnp.where(lower, one, two).astype(BF16)
+    packed[:top, :] = factor_top[...]
+    packed[top:2 * top, :] = inverse_top[...]
     column = column_of_row(untwist_low[pl.ds(place // 2, 1), :])
-    packed[at + 2 * top:at + 3 * top, :] = (column * inverse_mid[...].astype(F32)).astype(BF16)
+    packed[2 * top:3 * top, :] = (column * inverse_mid[...].astype(F32)).astype(BF16)
+    keep = lower == (lax.rem(place, 2) == 0)
+    packed[3 * top:, :] = jnp.where(keep, kernel_top[...], pltpu.roll(kernel_top[...], HALF, 1)).astype(BF16)
 
 
 def gate_kernel(*refs):
-    sources, weights, (target, matrix) = refs[:4], refs[4:8], refs[8:]
+    sources, weights, (target, matrix) = refs[:4], refs[4:8], refs[9:]
     for t, (source, weight) in enumerate(zip(sources, weights)):
         matrix[t * LANES:(t + 1) * LANES, :] = weight[...]
 
@@ -274,22 +283,26 @@
     turns = range(ch_count)
     shares = [lax.dynamic_slice_in_dim(values, (ch_place ^ turn) * share, share, 0) for turn in turns]
     shares = [swap(array, turn) if turn < 3 else array for turn, array in enumerate(shares)]
-    packed = call(
-        pack_kernel, "pack", jax.ShapeDtypeStruct(((HALF + 3) * top, width), BF16), [], unit,
-        untwist_t, factor_top, inverse_top, inverse_mid, untwist_low.T, limit=8 << 20,
+    result = jax.ShapeDtypeStruct((share, columns_out), BF16)
+    packed, spread = call(
+        pack_kernel, "pack", [jax.ShapeDtypeStruct((4 * top, width), BF16), result], [], unit,
+        untwist_t, factor_top, inverse_top, inverse_mid, untwist_low.T, kernel_top, limit=8 << 20,
     )
     columns, shares = lax.optimization_barrier((columns, shares))
-    third = call(
-        middle_kernel, "middle", jax.ShapeDtypeStruct((rows, width), BF16),
+    third, spread = call(
+        middle_kernel, "middle", [jax.ShapeDtypeStruct((rows, width), BF16), result],
         [
+            pltpu.VMEM((share, columns_out), BF16),
             pltpu.VMEM((rows, width), BF16),
             padded,
             padded,
             pltpu.VMEM((top, width), F32),
             pltpu.VMEM((HALF, width), F32),
+            pltpu.SemaphoreType.DMA((2,)),
             pltpu.SemaphoreType.DMA((4,)),
         ], unit * (2 * top + mid),
-        columns.reshape(top * PITCH, width), kernel_top, packed, limit=24 << 20, out_spec=pl.BlockSpec(memory_space=pltpu.HBM),
+        columns.reshape(top * PITCH, width), packed, spread,
+        limit=24 << 20, far=(2,), aliases={2: 1}, out_spec=pl.BlockSpec(memory_space=pltpu.HBM),
     )
     third, shares, out_weight = lax.optimization_barrier((third, shares, out_weight))
     shares = [swap(array, turn) if turn == 3 else array for turn, array in enumerate(shares)]
@@ -297,7 +310,7 @@
     silu, matrix = call(
         gate_kernel, "gate",
         [jax.ShapeDtypeStruct((share, columns_out), BF16), jax.ShapeDtypeStruct((ch_count * width, columns_out), BF16)],
-        [], unit, *shares, *weights, limit=12 << 20,
+        [], unit, *shares, *weights, spread, limit=12 << 20, far=(8,), aliases={8: 0},
     )
     third = lax.all_to_all(third.reshape(top * ch_count, -1, width), ("seq", "ch"), 0, 0, tiled=True)
     return call(

time: 164 us -> 163 us (level)
  local copies, waits for them, and re-layouts: 10.5 us -> 7.57 us
  Pallas kernels: 17.6 us -> 20 us
    unnamed x30 -> x26, local copies, waits for them, and re-layouts: 8.03 us -> 5.06 us
    pallas_call x5, Pallas kernels: 17.6 us -> 20 us  [call(): pl.pallas_call(kernel, name=name, out_shape=out_shape, in_specs=[hbm if n...]
  transfers between devices with their start and end apart: 8 -> 8, of which waited for: 5 -> 5; matrix products, arithmetic and copies ran while one was open for 2% -> 2% of each run, Pallas kernels for 2% -> 3%
where the time goes in v7:
time: 163 us; the launch traced here: 162 us
  waiting for transfers between devices  83.8 us (51%)
  starting transfers between devices  50.7 us (31%)
  Pallas kernels  20 us (12%)
  local copies, waits for them, and re-layouts  7.57 us (5%)
    ppermute x6, waiting for transfers between devices, swap(): return lax.ppermute(array, 'ch', [(c, c ^ turn) for c in range(ch_count)])  45.6 us
    all_to_all x1, waiting for transfers between devices, local(): lax.all_to_all(message.reshape(2 * low, PITCH, width), 'seq', 0, 0, tiled...  25.7 us
    all_to_all x1, starting transfers between devices, local(): lax.all_to_all(message.reshape(2 * low, PITCH, width), 'seq', 0, 0, tiled...  20.8 us
    pallas_call x5, Pallas kernels, call(): pl.pallas_call(kernel, name=name, out_shape=out_shape, in_specs=[hbm if n...  20 us
    ppermute x6, starting transfers between devices, swap(): return lax.ppermute(array, 'ch', [(c, c ^ turn) for c in range(ch_count)])  18.9 us
    all_to_all x1, waiting for transfers between devices, local(): lax.all_to_all(third.reshape(top * ch_count, -1, width), ('seq', 'ch'), 0...  12.5 us
    all_to_all x1, starting transfers between devices, local(): lax.all_to_all(third.reshape(top * ch_count, -1, width), ('seq', 'ch'), 0...  11 us
    unnamed x26, local copies, waits for them, and re-layouts  5.06 us
  transfers between devices with their start and end apart: 8, of which 5 were waited for; matrix products, arithmetic and copies ran while one was open for 2% of the time, Pallas kernels for 3%

profile of v7, /device:TPU:1, one launch (start us, length us, event | category | flops | bytes accessed | tf_op | source)
XLA Modules:
  0.0 162.4 jit_solution(5541533954013438695)
XLA Ops:
  0.0 4.7 %forward.1 = bf16[9216,128]{1,0:T(8,128)(2,1)} custom-call(bf16[8192,128]{1,0:T(8,128)(2,1)} %values.1, bf16[64,64]{1,0:T(8,128)(2,1)} %factor_low.1, f32[64,128]{1,0:T(8,128)} %bitcast.11, bf16[128,128]{1,0:T(8,128)(2,1)} %factor_mid.1, f32[128,128]{1,0:T(8,128)} %twist_top.1, bf16[64,128]{1,0:T(8,128)(2,1)} %kernel_low.1), custom_call_target="tpu_custom_call" | custom-call | flops 402653184 | bytes 4612096 | tf_op jit(solution)/shard_map/forward/pallas_call | solution.py:224
  4.7 20.8 %all-to-all-start = ((bf16[128,72,128]{2,1,0:T(8,128)(2,1)}), bf16[128,72,128]{2,1,0:T(8,128)(2,1)S(1)}, u32[]{:S(2)}, u32[]{:S(2)}) async-start(bf16[128,72,128]{2,1,0:T(8,128)(2,1)} %bitcast.10), calls=%async_computation | async-start | bytes 4718592 | tf_op jit(solution)/shard_map/all_to_all | solution.py:281
  25.6 0.0 copy-start.6
  25.6 0.0 copy-start.7
  25.6 0.0 copy-start.8
  25.6 0.0 copy-start.9
  25.6 0.0 copy-start.10
  25.6 0.0 copy-start.11
  25.7 2.5 %constant_dynamic-slice_fusion = (bf16[2048,128]{1,0:T(8,128)(2,1)}, bf16[2048,128]{1,0:T(8,128)(2,1)S(1)}, bf16[2048,128]{1,0:T(8,128)(2,1)S(1)}, bf16[2048,128]{1,0:T(8,128)(2,1)S(1)}) fusion(bf16[8192,128]{1,0:T(8,128)(2,1)} %values.1, s32[]{:T(128)S(6)} %select_n.15, s32[]{:T(128)S(6)} %select_n.13, s32[]{:T(128)S(6)} %select_n.12, s32[]{:T(128)S(6)} %select_n.14), kind=kLoop, calls=%fused_computation | loop fusion | bytes 4194320 | tf_op jit(solution)/shard_map/dynamic_slice | solution.py:284
  28.2 2.9 %collective-permute-start = (bf16[2048,128]{1,0:T(8,128)(2,1)S(1)}, bf16[2048,128]{1,0:T(8,128)(2,1)S(1)}, u32[]{:S(2)}, u32[]{:S(2)}) collective-permute-start(bf16[2048,128]{1,0:T(8,128)(2,1)S(1)} %get-tuple-element.44), channel_id=1, source_target_pairs={{0,1},{1,0},{2,3},{3,2},{4,5},{5,4},{6,7},{7,6},{8,9},{9,8},{10,11... | collective-permute-start | bytes 1572872 | tf_op jit(solution)/shard_map/ppermute | solution.py:267
  31.0 2.2 %collective-permute-start.1 = (bf16[2048,128]{1,0:T(8,128)(2,1)S(1)}, bf16[2048,128]{1,0:T(8,128)(2,1)S(1)}, u32[]{:S(2)}, u32[]{:S(2)}) collective-permute-start(bf16[2048,128]{1,0:T(8,128)(2,1)S(1)} %get-tuple-element.46), channel_id=1, source_target_pairs={{0,2},{1,3},{2,0},{3,1},{4,6},{5,7},{6,4},{7,5},{8,10},{9,11},{10,... | collective-permute-start | bytes 1572872 | tf_op jit(solution)/shard_map/ppermute | solution.py:267
  33.2 0.0 copy-done.6
  33.3 0.0 copy-done.7
  33.3 0.0 copy-done.8
  33.3 0.0 copy-done.9
  33.3 0.0 copy-done.10
  33.3 0.0 copy-done.11
  33.3 2.7 %pack.1 = (bf16[512,128]{1,0:T(8,128)(2,1)S(1)}, bf16[2048,512]{1,0:T(8,128)(2,1)}) custom-call(f32[128,128]{1,0:T(8,128)S(1)} %copy-done.6, bf16[128,128]{1,0:T(8,128)(2,1)S(1)} %copy-done.8, bf16[128,128]{1,0:T(8,128)(2,1)S(1)} %copy-done.9, bf16[128,128]{1,0:T(8,128)(2,1)S(1)} %copy-done.10, f32[64,128]{1,0:T(8,128)S(1)} %bitcast.9, f32[128,128]{1,0:T(8,128)S(1)} %copy-done.7), custom_call_target="tpu_custom_call" | custom-call | flops 2097152 | bytes 2490368 | tf_op jit(solution)/shard_map/pack/pallas_call | solution.py:224
  36.0 0.0 collective-permute-done.refs_1_
  36.0 21.9 %collective-permute-done.1.refs_2_ = bf16[2048,128]{1,0:T(8,128)(2,1)S(1)} collective-permute-done((bf16[2048,128]{1,0:T(8,128)(2,1)S(1)}, bf16[2048,128]{1,0:T(8,128)(2,1)S(1)}, u32[]{:S(2)}, u32[]{:S(2)}) %collective-permute-start.1) | collective-permute-done | bytes 524320 | tf_op jit(solution)/shard_map/ppermute | solution.py:267
  57.9 0.0 copy-start.1
  57.9 0.8 copy-done.1
  58.7 25.7 %all-to-all-done = bf16[128,72,128]{2,1,0:T(8,128)(2,1)S(1)} async-done(((bf16[128,72,128]{2,1,0:T(8,128)(2,1)}), bf16[128,72,128]{2,1,0:T(8,128)(2,1)S(1)}, u32[]{:S(2)}, u32[]{:S(2)}) %all-to-all-start) | async-done | bytes 2359328 | tf_op jit(solution)/shard_map/all_to_all | solution.py:281
  84.4 5.0 %middle.1 = (bf16[8192,128]{1,0:T(8,128)(2,1)S(1)}, bf16[2048,512]{1,0:T(8,128)(2,1)}) custom-call(bf16[9216,128]{1,0:T(8,128)(2,1)S(1)} %bitcast.6, bf16[512,128]{1,0:T(8,128)(2,1)S(1)} %get-tuple-element.27.packed, bf16[2048,512]{1,0:T(8,128)(2,1)} %get-tuple-element.28.spread), custom_call_target="tpu_custom_call", output_to_operand_aliasing={{1}: (2, {})} | custom-call | flops 805306368 | bytes 8781824 | tf_op jit(solution)/shard_map/middle/pallas_call | solution.py:224
  89.4 0.0 copy-start
  89.4 1.3 copy-done
  90.7 0.0 copy-start.5
  90.7 11.0 %all-to-all-start.1 = ((bf16[512,16,128]{2,1,0:T(8,128)(2,1)}), bf16[512,16,128]{2,1,0:T(8,128)(2,1)S(1)}, u32[]{:S(2)}, u32[]{:S(2)}) async-start(bf16[512,16,128]{2,1,0:T(8,128)(2,1)} %bitcast.8), calls=%async_computation.1 | async-start | bytes 4194304 | tf_op jit(solution)/shard_map/all_to_all | solution.py:315
  101.8 3.5 %collective-permute-start.2 = (bf16[2048,128]{1,0:T(8,128)(2,1)}, bf16[2048,128]{1,0:T(8,128)(2,1)S(1)}, u32[]{:S(2)}, u32[]{:S(2)}) collective-permute-start(bf16[2048,128]{1,0:T(8,128)(2,1)} %get-tuple-element.38), channel_id=1, source_target_pairs={{0,3},{1,2},{2,1},{3,0},{4,7},{5,6},{6,5},{7,4},{8,11},{9,10},{10,... | collective-permute-start | bytes 1572872 | tf_op jit(solution)/shard_map/ppermute | solution.py:267
  105.3 0.0 copy-done.5
  105.3 2.0 %collective-permute-start.5 = (bf16[128,512]{1,0:T(8,128)(2,1)S(1)}, bf16[128,512]{1,0:T(8,128)(2,1)S(1)}, u32[]{:S(2)}, u32[]{:S(2)}) collective-permute-start(bf16[128,512]{1,0:T(8,128)(2,1)S(1)} %copy-done.5), channel_id=1, source_target_pairs={{0,3},{1,2},{2,1},{3,0},{4,7},{5,6},{6,5},{7,4},{8,11},{9,10},{10,... | collective-permute-start | bytes 393224 | tf_op jit(solution)/shard_map/ppermute | solution.py:267
  107.3 6.0 %collective-permute-start.4 = (bf16[128,512]{1,0:T(8,128)(2,1)S(1)}, bf16[128,512]{1,0:T(8,128)(2,1)S(1)}, u32[]{:S(2)}, u32[]{:S(2)}) collective-permute-start(bf16[128,512]{1,0:T(8,128)(2,1)S(1)} %copy-done.5), channel_id=1, source_target_pairs={{0,2},{1,3},{2,0},{3,1},{4,6},{5,7},{6,4},{7,5},{8,10},{9,11},{10,... | collective-permute-start | bytes 393224 | tf_op jit(solution)/shard_map/ppermute | solution.py:267
  113.3 2.3 %collective-permute-start.3 = (bf16[128,512]{1,0:T(8,128)(2,1)S(1)}, bf16[128,512]{1,0:T(8,128)(2,1)S(1)}, u32[]{:S(2)}, u32[]{:S(2)}) collective-permute-start(bf16[128,512]{1,0:T(8,128)(2,1)S(1)} %copy-done.5), channel_id=1, source_target_pairs={{0,1},{1,0},{2,3},{3,2},{4,5},{5,4},{6,7},{7,6},{8,9},{9,8},{10,11... | collective-permute-start | bytes 393224 | tf_op jit(solution)/shard_map/ppermute | solution.py:267
  115.6 14.7 %collective-permute-done.5.refs_7_ = bf16[128,512]{1,0:T(8,128)(2,1)S(1)} collective-permute-done((bf16[128,512]{1,0:T(8,128)(2,1)S(1)}, bf16[128,512]{1,0:T(8,128)(2,1)S(1)}, u32[]{:S(2)}, u32[]{:S(2)}) %collective-permute-start.5) | collective-permute-done | bytes 131104 | tf_op jit(solution)/shard_map/ppermute | solution.py:267
  130.3 9.0 %collective-permute-done.4.refs_6_ = bf16[128,512]{1,0:T(8,128)(2,1)S(1)} collective-permute-done((bf16[128,512]{1,0:T(8,128)(2,1)S(1)}, bf16[128,512]{1,0:T(8,128)(2,1)S(1)}, u32[]{:S(2)}, u32[]{:S(2)}) %collective-permute-start.4) | collective-permute-done | bytes 131104 | tf_op jit(solution)/shard_map/ppermute | solution.py:267
  139.4 0.0 collective-permute-done.3.refs_5_
  139.4 0.0 collective-permute-done.2.refs_3_
  139.4 0.0 copy-start.2
  139.4 1.0 copy-done.2
  140.4 0.0 copy-start.12
  140.4 2.5 %gate.1 = (bf16[2048,512]{1,0:T(8,128)(2,1)}, bf16[512,512]{1,0:T(8,128)(2,1)S(1)}) custom-call(bf16[2048,128]{1,0:T(8,128)(2,1)S(1)} %get-tuple-element.35.refs_0_, bf16[2048,128]{1,0:T(8,128)(2,1)S(1)} %collective-permute-done.refs_1_, bf16[2048,128]{1,0:T(8,128)(2,1)S(1)} %copy-done.2, ...), custom_call_target="tpu_custom_call", output_to_operand_aliasing={{0}: (8, {})} | custom-call | flops 2097152 | bytes 7340032 | tf_op jit(solution)/shard_map/gate/pallas_call | solution.py:224
  142.9 0.0 copy-start.3
  142.9 0.8 copy-done.3
  143.7 12.5 %all-to-all-done.1 = bf16[512,16,128]{2,1,0:T(8,128)(2,1)S(1)} async-done(((bf16[512,16,128]{2,1,0:T(8,128)(2,1)}), bf16[512,16,128]{2,1,0:T(8,128)(2,1)S(1)}, u32[]{:S(2)}, u32[]{:S(2)}) %all-to-all-start.1) | async-done | bytes 2097184 | tf_op jit(solution)/shard_map/all_to_all | solution.py:315
  156.2 0.0 copy-done.12
  156.2 0.0 copy-start.4
  156.2 1.0 copy-done.4
  157.2 5.1 %last.1 = bf16[2048,512]{1,0:T(8,128)(2,1)} custom-call(bf16[8192,128]{1,0:T(8,128)(2,1)S(1)} %bitcast.7, bf16[64,64]{1,0:T(8,128)(2,1)S(1)} %copy-done.12, bf16[2048,512]{1,0:T(8,128)(2,1)} %get-tuple-element.41.silu, bf16[512,512]{1,0:T(8,128)(2,1)S(1)} %copy-done.4), custom_call_target="tpu_custom_call", output_to_operand_aliasing={{}: (2, {})} | custom-call | flops 1140850688 | bytes 6823936 | tf_op jit(solution)/shard_map/last/pallas_call | solution.py:224
Async XLA Ops:
  4.7 79.6 %all-to-all-start = ((bf16[128,72,128]{2,1,0:T(8,128)(2,1)}), bf16[128,72,128]{2,1,0:T(8,128)(2,1)S(1)}, u32[]{:S(2)}, u32[]{:S(2)}) async-start(bf16[128,72,128]{2,1,0:T(8,128)(2,1)} %bitcast.10), calls=%async_computation | async-start | bytes 4718592 | tf_op jit(solution)/shard_map/all_to_all | solution.py:281
  25.6 7.7 %copy-start.6 = (f32[128,128]{1,0:T(8,128)S(1)}, f32[128,128]{1,0:T(8,128)}, u32[]{:S(2)}) copy-start(f32[128,128]{1,0:T(8,128)} %untwist_top) | copy-start | bytes 196612
  25.6 7.7 %copy-start.7 = (f32[128,128]{1,0:T(8,128)S(1)}, f32[128,128]{1,0:T(8,128)}, u32[]{:S(2)}) copy-start(f32[128,128]{1,0:T(8,128)} %kernel_top.1) | copy-start | bytes 196612
  25.6 7.7 %copy-start.8 = (bf16[128,128]{1,0:T(8,128)(2,1)S(1)}, bf16[128,128]{1,0:T(8,128)(2,1)}, u32[]{:S(2)}) copy-start(bf16[128,128]{1,0:T(8,128)(2,1)} %factor_top.1) | copy-start | bytes 98308
  25.6 7.7 %copy-start.9 = (bf16[128,128]{1,0:T(8,128)(2,1)S(1)}, bf16[128,128]{1,0:T(8,128)(2,1)}, u32[]{:S(2)}) copy-start(bf16[128,128]{1,0:T(8,128)(2,1)} %inverse_top.1) | copy-start | bytes 98308
  25.6 7.7 %copy-start.10 = (bf16[128,128]{1,0:T(8,128)(2,1)S(1)}, bf16[128,128]{1,0:T(8,128)(2,1)}, u32[]{:S(2)}) copy-start(bf16[128,128]{1,0:T(8,128)(2,1)} %inverse_mid.1) | copy-start | bytes 98308
  25.6 7.7 %copy-start.11 = (f32[128,64]{0,1:T(8,128)S(1)}, f32[128,64]{0,1:T(8,128)}, u32[]{:S(2)}) copy-start(f32[128,64]{0,1:T(8,128)} %param.25) | copy-start | bytes 98308
  28.2 7.8 %collective-permute-start = (bf16[2048,128]{1,0:T(8,128)(2,1)S(1)}, bf16[2048,128]{1,0:T(8,128)(2,1)S(1)}, u32[]{:S(2)}, u32[]{:S(2)}) collective-permute-start(bf16[2048,128]{1,0:T(8,128)(2,1)S(1)} %get-tuple-element.44), channel_id=1, source_target_pairs={{0,1},{1,0},{2,3},{3,2},{4,5},{5,4},{6,7},{7,6},{8,9},{9,8},{10,11... | collective-permute-start | bytes 1572872 | tf_op jit(solution)/shard_map/ppermute | solution.py:267
  31.0 26.8 %collective-permute-start.1 = (bf16[2048,128]{1,0:T(8,128)(2,1)S(1)}, bf16[2048,128]{1,0:T(8,128)(2,1)S(1)}, u32[]{:S(2)}, u32[]{:S(2)}) collective-permute-start(bf16[2048,128]{1,0:T(8,128)(2,1)S(1)} %get-tuple-element.46), channel_id=1, source_target_pairs={{0,2},{1,3},{2,0},{3,1},{4,6},{5,7},{6,4},{7,5},{8,10},{9,11},{10,... | collective-permute-start | bytes 1572872 | tf_op jit(solution)/shard_map/ppermute | solution.py:267
  57.9 0.8 copy-start.1
  89.4 1.3 copy-start
  90.7 14.6 %copy-start.5 = (bf16[128,512]{1,0:T(8,128)(2,1)S(1)}, bf16[128,512]{1,0:T(8,128)(2,1)}, u32[]{:S(2)}) copy-start(bf16[128,512]{1,0:T(8,128)(2,1)} %refs_4_) | copy-start | bytes 393220
  90.7 65.4 %all-to-all-start.1 = ((bf16[512,16,128]{2,1,0:T(8,128)(2,1)}), bf16[512,16,128]{2,1,0:T(8,128)(2,1)S(1)}, u32[]{:S(2)}, u32[]{:S(2)}) async-start(bf16[512,16,128]{2,1,0:T(8,128)(2,1)} %bitcast.8), calls=%async_computation.1 | async-start | bytes 4194304 | tf_op jit(solution)/shard_map/all_to_all | solution.py:315
  101.8 37.6 %collective-permute-start.2 = (bf16[2048,128]{1,0:T(8,128)(2,1)}, bf16[2048,128]{1,0:T(8,128)(2,1)S(1)}, u32[]{:S(2)}, u32[]{:S(2)}) collective-permute-start(bf16[2048,128]{1,0:T(8,128)(2,1)} %get-tuple-element.38), channel_id=1, source_target_pairs={{0,3},{1,2},{2,1},{3,0},{4,7},{5,6},{6,5},{7,4},{8,11},{9,10},{10,... | collective-permute-start | bytes 1572872 | tf_op jit(solution)/shard_map/ppermute | solution.py:267
  105.3 25.0 %collective-permute-start.5 = (bf16[128,512]{1,0:T(8,128)(2,1)S(1)}, bf16[128,512]{1,0:T(8,128)(2,1)S(1)}, u32[]{:S(2)}, u32[]{:S(2)}) collective-permute-start(bf16[128,512]{1,0:T(8,128)(2,1)S(1)} %copy-done.5), channel_id=1, source_target_pairs={{0,3},{1,2},{2,1},{3,0},{4,7},{5,6},{6,5},{7,4},{8,11},{9,10},{10,... | collective-permute-start | bytes 393224 | tf_op jit(solution)/shard_map/ppermute | solution.py:267
  107.3 32.0 %collective-permute-start.4 = (bf16[128,512]{1,0:T(8,128)(2,1)S(1)}, bf16[128,512]{1,0:T(8,128)(2,1)S(1)}, u32[]{:S(2)}, u32[]{:S(2)}) collective-permute-start(bf16[128,512]{1,0:T(8,128)(2,1)S(1)} %copy-done.5), channel_id=1, source_target_pairs={{0,2},{1,3},{2,0},{3,1},{4,6},{5,7},{6,4},{7,5},{8,10},{9,11},{10,... | collective-permute-start | bytes 393224 | tf_op jit(solution)/shard_map/ppermute | solution.py:267
  113.3 26.1 %collective-permute-start.3 = (bf16[128,512]{1,0:T(8,128)(2,1)S(1)}, bf16[128,512]{1,0:T(8,128)(2,1)S(1)}, u32[]{:S(2)}, u32[]{:S(2)}) collective-permute-start(bf16[128,512]{1,0:T(8,128)(2,1)S(1)} %copy-done.5), channel_id=1, source_target_pairs={{0,1},{1,0},{2,3},{3,2},{4,5},{5,4},{6,7},{7,6},{8,9},{9,8},{10,11... | collective-permute-start | bytes 393224 | tf_op jit(solution)/shard_map/ppermute | solution.py:267
  139.4 1.0 copy-start.2
  140.4 15.7 %copy-start.12 = (bf16[64,64]{1,0:T(8,128)(2,1)S(1)}, bf16[64,64]{1,0:T(8,128)(2,1)}, u32[]{:S(2)}) copy-start(bf16[64,64]{1,0:T(8,128)(2,1)} %inverse_low.1) | copy-start | bytes 24580
  142.9 0.8 copy-start.3
  156.2 1.0 copy-start.4
